TPU v7x, 32 devices: a whole 2x2x4 slice. The times are simulated.
32 devices in a mesh: expert: 8 (over z, y), narrow: 4 (over x, core).
Axes of the slice: x: 2, y: 2, z: 4, core: 2. Of those that a mesh axis runs over, the one named last changes fastest.
Arguments:
- tokens: bfloat16 [32768, 768], P(('expert', 'narrow')), may hold values from -6 to 6
- segments: int32 [32, 1024], P(('expert', 'narrow')), may hold values from 0 to 3, never falling along the last dimension, each value on 1 to 512 neighbouring positions
- routes: int32 [32768, 1], P(('expert', 'narrow')), may hold values from 0 to 7; in each aligned block of 1024 rows (0 to 1023, 1024 to 2047, ...) at most 256 rows name the same one
- gate_logit: float32 [32768], P(('expert', 'narrow')), may hold values from -3 to 3
- w_qkv: bfloat16 [768, 2304], P(('expert', 'narrow')), may hold values from -0.21875 to 0.21875
- w_out: bfloat16 [768, 768], P(('expert', 'narrow')), may hold values from -1.5 to 1.5
- norm_gains: bfloat16 [2, 768], P(None, ('expert', 'narrow')), may hold values from 0.5 to 1.5
- w_in: bfloat16 [8, 768, 3072], P('expert', None, 'narrow'), may hold values from -0.21875 to 0.21875
- w_hid: bfloat16 [8, 3072, 768], P('expert', 'narrow'), may hold values from -0.3125 to 0.3125
- cotangent: bfloat16 [32768, 768], P(('expert', 'narrow')), may hold values from -6 to 6
Outputs:
- block_out: bfloat16 [32768, 768], P(('expert', 'narrow'))
- grad_tokens: float32 [32768, 768], P(('expert', 'narrow'))
- grad_qkv: float32 [768, 2304], P(('expert', 'narrow'))
- grad_out: float32 [768, 768], P(('expert', 'narrow'))
- grad_gains: float32 [2, 768], P(None, ('expert', 'narrow'))
- grad_w_in: float32 [8, 768, 3072], P('expert', None, 'narrow')
- grad_w_hid: float32 [8, 3072, 768], P('expert', 'narrow')
Inputs may be any that keep to these rules, and one draw needn't show every extreme that they name: `routes`: within the 1024 tokens of one device at most 256 go to one expert. `segments`: within a packed row ids never fall; a document holds at most 512 tokens.
All inputs are finite; a program needn't handle non-finite values.
Results may differ from a plain program's by a relative error of at most 0.013.
Values may be sent and summed in bfloat16 or wider, within the bound.
A program may use at most 448 MiB of HBM per device.

v0:
```python
from functools import partial

import jax
import jax.numpy as jnp
from jax import lax
from jax.sharding import PartitionSpec as P

HEAD_DIM = 64
SEQ = 1024


epsilon = 1e-05
big_negative = -1e30


def normalize(values):
    centre = jnp.mean(values, axis=-1, keepdims=True)
    shifted = values - centre
    factor = lax.rsqrt(jnp.mean(shifted * shifted, axis=-1, keepdims=True) + epsilon)
    return (shifted * factor, factor)


def norm_back(grad_normed, normed, factor):
    return factor * (
        grad_normed
        - jnp.mean(grad_normed, axis=-1, keepdims=True)
        - normed * jnp.mean(grad_normed * normed, axis=-1, keepdims=True)
    )


def scores_of(queries, key_rows, seg_row):
    positions = jnp.arange(seg_row.shape[0], dtype=jnp.int32)
    allowed = (positions[:, None] >= positions[None, :]) & (seg_row[:, None] == seg_row[None, :])
    scores = jnp.einsum(
        "qhd,khd->hqk", queries, key_rows, preferred_element_type=jnp.float32
    ) * queries.shape[-1] ** (-0.5)
    return jnp.where(allowed[None], scores, big_negative)


def attend_forward(pieces):
    queries, key_rows, value_rows, seg_row = pieces
    scores = scores_of(queries, key_rows, seg_row)
    largest = jnp.max(scores, axis=-1, keepdims=True)
    raised = jnp.exp(scores - largest)
    totals = jnp.sum(raised, axis=-1, keepdims=True)
    weights = (raised / totals).astype(jnp.bfloat16)
    context = jnp.einsum("hqk,khd->qhd", weights, value_rows, preferred_element_type=jnp.float32)
    return (context, (largest + jnp.log(totals))[..., 0])


def attend_backward(pieces):
    queries, key_rows, value_rows, seg_row, logsum, grad_context = pieces
    weights = jnp.exp(scores_of(queries, key_rows, seg_row) - logsum[..., None])
    grad_value = jnp.einsum(
        "hqk,qhd->khd",
        weights.astype(jnp.bfloat16),
        grad_context,
        preferred_element_type=jnp.float32,
    )
    grad_weights = jnp.einsum(
        "qhd,khd->hqk", grad_context, value_rows, preferred_element_type=jnp.float32
    )
    grad_scores = (
        weights * (grad_weights - jnp.sum(weights * grad_weights, axis=-1, keepdims=True))
    ).astype(jnp.bfloat16)
    factor = queries.shape[-1] ** (-0.5)
    grad_query = (
        jnp.einsum("hqk,khd->qhd", grad_scores, key_rows, preferred_element_type=jnp.float32)
        * factor
    )
    grad_key = (
        jnp.einsum("hqk,qhd->khd", grad_scores, queries, preferred_element_type=jnp.float32)
        * factor
    )
    return (
        grad_query.astype(jnp.bfloat16),
        grad_key.astype(jnp.bfloat16),
        grad_value.astype(jnp.bfloat16),
    )


def over_rows(left, right):
    return lax.dot_general(
        left, right, (((0,), (0,)), ((), ())), preferred_element_type=jnp.float32
    )


def over_columns(left, right):
    return lax.dot_general(
        left, right, (((1,), (1,)), ((), ())), preferred_element_type=jnp.float32
    )


def local(tokens, segments, routes, gate_logit, w_qkv, w_out, norm_gains, w_in, w_hid, cotangent):
    tok_count, model_width = tokens.shape
    head_count = model_width // HEAD_DIM
    rows_here = tok_count // SEQ
    n_expert = lax.axis_size("expert")
    capacity = 2 * tok_count // n_expert
    slot_rows = n_expert * capacity
    qkv_full, out_full, gains_full = (
        lax.all_gather(w_qkv, ("expert", "narrow"), axis=0, tiled=True),
        lax.all_gather(w_out, ("expert", "narrow"), axis=0, tiled=True),
        lax.all_gather(norm_gains, ("expert", "narrow"), axis=1, tiled=True),
    )
    gain_one = gains_full[0].astype(jnp.float32)
    gain_two = gains_full[1].astype(jnp.float32)
    resid_in = tokens.astype(jnp.float32)
    normed_one, factor_one = normalize(resid_in)
    act_one = (normed_one * gain_one).astype(jnp.bfloat16)
    packed = jnp.dot(act_one, qkv_full, preferred_element_type=jnp.float32).astype(jnp.bfloat16)
    packed = packed.reshape(rows_here, SEQ, 3, head_count, HEAD_DIM)
    queries = packed[:, :, 0]
    key_rows = packed[:, :, 1]
    value_rows = packed[:, :, 2]
    context, logsum = lax.map(attend_forward, (queries, key_rows, value_rows, segments))
    context_low = context.reshape(tok_count, model_width).astype(jnp.bfloat16)
    hidden_state = resid_in + jnp.dot(context_low, out_full, preferred_element_type=jnp.float32)
    normed_two, factor_two = normalize(hidden_state)
    act_two = (normed_two * gain_two).astype(jnp.bfloat16)
    chosen = routes[:, 0]
    onehot = (chosen[:, None] == jnp.arange(n_expert, dtype=jnp.int32)[None, :]).astype(jnp.int32)
    rank_index = jnp.sum((jnp.cumsum(onehot, axis=0) - 1) * onehot, axis=1)
    slot_index = chosen * capacity + rank_index

    def to_slots(values):
        return (
            jnp.zeros((slot_rows, model_width), jnp.bfloat16)
            .at[slot_index]
            .set(values)
            .reshape(n_expert, capacity, model_width)
        )

    received = lax.all_to_all(
        to_slots(act_two), "expert", split_axis=0, concat_axis=0, tiled=True
    ).reshape(slot_rows, model_width)
    all_rows = lax.all_gather(received, "narrow", axis=0, tiled=True)
    pre_act = jnp.dot(all_rows, w_in[0], preferred_element_type=jnp.float32)
    activated = jax.nn.gelu(pre_act, approximate=False).astype(jnp.bfloat16)
    returned = lax.psum_scatter(
        jnp.dot(activated, w_hid[0], preferred_element_type=jnp.float32).astype(jnp.bfloat16),
        "narrow",
        scatter_dimension=0,
        tiled=True,
    )
    returned_rows = lax.all_to_all(
        returned.reshape(n_expert, capacity, model_width),
        "expert",
        split_axis=0,
        concat_axis=0,
        tiled=True,
    )
    expert_out = returned_rows.reshape(slot_rows, model_width)[slot_index].astype(jnp.float32)
    gating = jax.nn.sigmoid(gate_logit)[:, None]
    block_out = (hidden_state + gating * expert_out).astype(jnp.bfloat16)
    grad_final = cotangent.astype(jnp.float32)
    grad_recv = lax.all_to_all(
        to_slots((gating * grad_final).astype(jnp.bfloat16)),
        "expert",
        split_axis=0,
        concat_axis=0,
        tiled=True,
    ).reshape(slot_rows, model_width)
    unused, gelu_back = jax.vjp(partial(jax.nn.gelu, approximate=False), pre_act)
    grad_rows = lax.all_gather(grad_recv, "narrow", axis=0, tiled=True)
    grad_act = over_columns(grad_rows, w_hid[0])
    grad_pre = gelu_back(grad_act)[0].astype(jnp.bfloat16)
    grad_in_w = over_rows(all_rows, grad_pre)[None]
    grad_hid_w = over_rows(activated, grad_rows)[None]
    grad_act_two = lax.psum_scatter(
        over_columns(grad_pre, w_in[0]).astype(jnp.bfloat16),
        "narrow",
        scatter_dimension=0,
        tiled=True,
    )
    grad_returned = lax.all_to_all(
        grad_act_two.reshape(n_expert, capacity, model_width),
        "expert",
        split_axis=0,
        concat_axis=0,
        tiled=True,
    )
    grad_norm_two = grad_returned.reshape(slot_rows, model_width)[slot_index].astype(jnp.float32)
    grad_gain_two = jnp.sum(grad_norm_two * normed_two, axis=0)
    grad_hidden = grad_final + norm_back(grad_norm_two * gain_two, normed_two, factor_two)
    grad_branch = grad_hidden.astype(jnp.bfloat16)
    grad_out_w = over_rows(context_low, grad_branch)
    grad_context = (
        over_columns(grad_branch, out_full)
        .astype(jnp.bfloat16)
        .reshape(rows_here, SEQ, head_count, HEAD_DIM)
    )
    grad_query, grad_key, grad_value = lax.map(
        attend_backward, (queries, key_rows, value_rows, segments, logsum, grad_context)
    )
    grad_packed = jnp.stack((grad_query, grad_key, grad_value), axis=2).reshape(
        tok_count, 3 * model_width
    )
    grad_qkv_w = over_rows(act_one, grad_packed)
    grad_norm_one = over_columns(grad_packed, qkv_full)
    grad_gain_one = jnp.sum(grad_norm_one * normed_one, axis=0)
    grad_tokens = grad_hidden + norm_back(grad_norm_one * gain_one, normed_one, factor_one)
    grad_qkv_part, grad_out_part, grad_gain_part = (
        lax.psum_scatter(grad_qkv_w, ("expert", "narrow"), scatter_dimension=0, tiled=True),
        lax.psum_scatter(grad_out_w, ("expert", "narrow"), scatter_dimension=0, tiled=True),
        lax.psum_scatter(
            jnp.stack((grad_gain_one, grad_gain_two)),
            ("expert", "narrow"),
            scatter_dimension=1,
            tiled=True,
        ),
    )
    return (
        block_out,
        grad_tokens,
        grad_qkv_part,
        grad_out_part,
        grad_gain_part,
        grad_in_w,
        grad_hid_w,
    )


def solution(mesh):
    placed = (
        P(("expert", "narrow"), None),
        P(("expert", "narrow"), None),
        P(("expert", "narrow"), None),
        P(("expert", "narrow")),
        P(("expert", "narrow"), None),
        P(("expert", "narrow"), None),
        P(None, ("expert", "narrow")),
        P("expert", None, "narrow"),
        P("expert", "narrow", None),
        P(("expert", "narrow"), None),
    )
    return jax.shard_map(
        local,
        mesh=mesh,
        in_specs=placed,
        out_specs=(
            P(("expert", "narrow"), None),
            P(("expert", "narrow"), None),
            P(("expert", "narrow"), None),
            P(("expert", "narrow"), None),
            P(None, ("expert", "narrow")),
            P("expert", None, "narrow"),
            P("expert", "narrow", None),
        ),
        check_vma=False,
    )
```

profile of v0, /device:TPU:0, one launch (start us, length us, event | category | flops | bytes accessed | tf_op | source)
XLA Modules:
  0.0 1056.5 jit_solution(5343795546009866682)
XLA Ops:
  8.7 43.3 %all-gather = bf16[32,24,2]{1,2,0:T(2,128)(2,1)S(1)} all-gather(bf16[1,24,2]{1,2,0:T(2,128)(2,1)} %bitcast.136), channel_id=1, replica_groups=mesh['expert'=8,'narrow'=4] {'expert','narrow'}, dimensions={0}, use_global_device_ids=true | all-gather | bytes 3168 | tf_op jit(solution)/shard_map/all_gather | solution.py:104
  64.9 8.9 all-gather.6.cloned.1.call-done
  73.9 8.6 convolution_convert_fusion.2
  82.6 6.7 copy.46
  89.3 21.5 %fusion.12 = (f32[12,1024]{1,0:T(8,128)S(1)}, f32[12,1024,1024]{1,2,0:T(8,128)}) fusion(pred[1024,1024]{0,1:T(8,128)(4,1)S(1)} %fusion.13, bf16[1,1024,3,12,64]{1,4,3,2,0:T(8,128)(2,1)} %bitcast.112), kind=kOutput, calls=%fused_computation.32 | convolution fusion | flops 1648349184 | bytes 54575104 | tf_op jit(solution)/shard_map/while/body/eval_jaxpr/qhd,khd->hqk/dot_general | solution.py:34
  110.8 21.1 %fusion = f32[12,1024]{1,0:T(8,128)S(1)} fusion(f32[12,1024]{1,0:T(8,128)S(1)} %get-tuple-element.91, f32[12,1024,1024]{1,2,0:T(8,128)} %get-tuple-element.92, pred[1024,1024]{0,1:T(8,128)(4,1)S(1)} %fusion.13), kind=kLoop, calls=%fused_computation.10 | loop fusion | flops 50319360 | bytes 51478528 | tf_op jit(solution)/shard_map/while/body/eval_jaxpr/reduce_sum | solution.py:45
  132.5 21.2 %fusion.38 = bf16[12,64,1024]{2,1,0:T(8,128)(2,1)} fusion(f32[12,1024]{1,0:T(8,128)S(1)} %fusion, f32[12,1024]{1,0:T(8,128)S(1)} %get-tuple-element.91, f32[12,1024,1024]{1,2,0:T(8,128)} %get-tuple-element.92, pred[1024,1024]{0,1:T(8,128)(4,1)S(1)} %fusion.13, bf16[1,1024,3,12,64]{1,4,3,2,0:T(8,128)(2,1)} %bitcast.113), kind=kOutput, calls=%fused_computation.78 | convolution fusion | flops 1674313728 | bytes 54624256 | tf_op jit(solution)/shard_map/while/body/eval_jaxpr/hqk,khd->qhd/dot_general | solution.py:47
  161.1 7.9 scatter_custom_fusion
  169.0 75.8 %all_to_all.20 = bf16[8,256,768]{2,1,0:T(8,128)(2,1)} all-to-all(bf16[8,256,768]{2,1,0:T(8,128)(2,1)} %bitcast.120), channel_id=1, replica_groups=mesh['expert'=8,'narrow'=4] {'expert'}, dimensions={0} | all-to-all | bytes 6291456 | tf_op jit(solution)/shard_map/all_to_all | solution.py:134
  251.7 8.0 scatter_custom_fusion.1
  259.7 75.0 %all_to_all.21 = bf16[8,256,768]{2,1,0:T(8,128)(2,1)} all-to-all(bf16[8,256,768]{2,1,0:T(8,128)(2,1)} %bitcast.119), channel_id=1, replica_groups=mesh['expert'=8,'narrow'=4] {'expert'}, dimensions={0} | all-to-all | bytes 6291456 | tf_op jit(solution)/shard_map/all_to_all | solution.py:157
  334.8 64.8 %multiply_convert_fusion.1 = (bf16[8192,768]{1,0:T(8,128)(2,1)}, f32[8192,768]{1,0:T(8,128)}, f32[8192,768]{1,0:T(8,128)}) fusion(bf16[8192,768]{1,0:T(8,128)(2,1)} %all-gather.10.cloned.1.call-done, bf16[1,768,768]{2,1,0:T(8,128)(2,1)S(1)} %copy-done), kind=kOutput, calls=%fused_computation.17 | convolution fusion | flops 10072621056 | bytes 76677120 | tf_op jit(solution)/shard_map/dot_general | solution.py:138
  399.6 16.2 %all-gather.12.cloned.1.call-done = bf16[8192,768]{1,0:T(8,128)(2,1)} async-done(((bf16[2048,768]{1,0:T(8,128)(2,1)}), bf16[8192,768]{1,0:T(8,128)(2,1)}) %all-gather.12.cloned.1.call-update) | async-done | bytes 12582928 | tf_op jit(solution)/shard_map/all_gather | solution.py:165
  415.8 31.0 %add_convert_fusion = bf16[8192,768]{1,0:T(8,128)(2,1)} fusion(f32[8192,768]{1,0:T(8,128)} %get-tuple-element.88, f32[8192,768]{1,0:T(8,128)} %get-tuple-element.95, bf16[8192,768]{1,0:T(8,128)(2,1)} %all-gather.12.cloned.1.call-done, bf16[1,768,768]{2,1,0:T(8,128)(2,1)S(1)} %copy-done.37), kind=kOutput, calls=%fused_computation.16 | convolution fusion | flops 9751756800 | bytes 76677120 | tf_op jit(solution)/shard_map/dot_general | solution.py:89
  446.8 17.1 %convolution_convert_fusion = bf16[8192,768]{1,0:T(8,128)(2,1)} fusion(bf16[8192,768]{1,0:T(8,128)(2,1)} %add_convert_fusion, bf16[1,768,768]{2,1,0:T(8,128)(2,1)S(1)} %copy-done), kind=kOutput, calls=%fused_computation.33 | convolution fusion | flops 9669967872 | bytes 26345472 | tf_op jit(solution)/shard_map/dot_general | solution.py:89
  464.0 17.9 %convolution_convert_fusion.1 = bf16[8192,768]{1,0:T(8,128)(2,1)} fusion(bf16[8192,768]{1,0:T(8,128)(2,1)} %get-tuple-element.87, bf16[1,768,768]{2,1,0:T(8,128)(2,1)S(1)} %copy-done.37), kind=kOutput, calls=%fused_computation.34 | convolution fusion | flops 9669967872 | bytes 26345472 | tf_op jit(solution)/shard_map/dot_general | solution.py:141
  481.9 81.2 %reduce-scatter.8.cloned.1.call-done = bf16[2048,768]{1,0:T(8,128)(2,1)} async-done(((bf16[8192,768]{1,0:T(8,128)(2,1)}), bf16[2048,768]{1,0:T(8,128)(2,1)}) %reduce-scatter.8.cloned.1.call-update) | async-done | bytes 3145744 | tf_op jit(solution)/shard_map/reduce_scatter | solution.py:170
  568.7 96.0 %reduce-scatter.6.cloned.1.call-done = bf16[2048,768]{1,0:T(8,128)(2,1)} async-done(((bf16[8192,768]{1,0:T(8,128)(2,1)}), bf16[2048,768]{1,0:T(8,128)(2,1)}) %reduce-scatter.6.cloned.1.call-update) | async-done | bytes 3145744 | tf_op jit(solution)/shard_map/reduce_scatter | solution.py:140
  670.3 6.8 gather_fusion.1
  678.7 62.3 %all-to-all-done.1 = bf16[8,256,768]{2,1,0:T(8,128)(2,1)} async-done(((bf16[8,256,768]{2,1,0:T(8,128)(2,1)}), bf16[8,256,768]{2,1,0:T(8,128)(2,1)}, u32[]{:S(2)}, u32[]{:S(2)}) %all-to-all-start.1) | async-done | bytes 3145760 | tf_op jit(solution)/shard_map/all_to_all | solution.py:146
  741.0 7.9 gather_fusion
  769.8 20.8 %fusion.45 = bf16[1,1024,1,12,64]{1,4,3,2,0:T(8,128)(2,1)} fusion(bf16[1024,12,64]{0,2,1:T(8,128)(2,1)S(1)} %bitcast.125, f32[12,1024]{1,0:T(8,128)S(1)} %log_add_fusion, f32[12,1024,1024]{1,2,0:T(8,128)} %get-tuple-element.92, pred[1024,1024]{0,1:T(8,128)(4,1)S(1)} %copy-done.2), kind=kOutput, calls=%fused_computation.88 | convolution fusion | flops 1661730816 | bytes 54575104 | tf_op jit(solution)/shard_map/while/body/eval_jaxpr/hqk,qhd->khd/dot_general | solution.py:54
  790.6 35.5 %multiply_reduce_fusion = (f32[12,1024]{1,0:T(8,128)S(1)}, f32[12,1024,1024]{1,2,0:T(8,128)}) fusion(f32[12,1024]{1,0:T(8,128)S(1)} %log_add_fusion, f32[12,1024,1024]{1,2,0:T(8,128)} %get-tuple-element.92, pred[1024,1024]{0,1:T(8,128)(4,1)S(1)} %copy-done.2, bf16[1024,12,64]{0,2,1:T(8,128)(2,1)} %bitcast.126, bf16[1,1024,3,12,64]{1,4,3,2,0:T(8,128)(2,1)} %bitcast.114), kind=kOutput, calls=%fused_computation.5 | convolution fusion | flops 1673515008 | bytes 104955904 | tf_op jit(solution)/shard_map/while/body/eval_jaxpr/qhd,khd->hqk/dot_general | solution.py:60
  826.1 42.1 %multiply_convert_fusion = bf16[12,1024,1024]{1,2,0:T(8,128)(2,1)} fusion(f32[12,1024,1024]{1,2,0:T(8,128)} %get-tuple-element.97, f32[12,1024]{1,0:T(8,128)S(1)} %get-tuple-element.96, f32[12,1024]{1,0:T(8,128)S(1)} %log_add_fusion, f32[12,1024,1024]{1,2,0:T(8,128)} %get-tuple-element.92, pred[1024,1024]{0,1:T(8,128)(4,1)S(1)} %copy-done.2), kind=kLoop, calls=%fused_computation.4 | loop fusion | flops 75497472 | bytes 126976000 | tf_op jit(solution)/shard_map/while/body/eval_jaxpr/convert_element_type | solution.py:65
  868.3 14.1 %fusion.44 = bf16[1,1024,1,12,64]{1,4,3,2,0:T(8,128)(2,1)} fusion(bf16[12,1024,1024]{1,2,0:T(8,128)(2,1)} %multiply_convert_fusion, bf16[1,1024,3,12,64]{1,4,3,2,0:T(8,128)(2,1)} %bitcast.115), kind=kOutput, calls=%fused_computation.87 | convolution fusion | flops 1612185600 | bytes 28311552 | tf_op jit(solution)/shard_map/while/body/eval_jaxpr/hqk,qhd->khd/dot_general | solution.py:72
  882.4 13.4 %fusion.43 = bf16[1,1024,1,12,64]{1,4,3,2,0:T(8,128)(2,1)S(1)} fusion(bf16[12,1024,1024]{1,2,0:T(8,128)(2,1)} %multiply_convert_fusion, bf16[1,1024,3,12,64]{1,4,3,2,0:T(8,128)(2,1)} %bitcast.116), kind=kOutput, calls=%fused_computation.86 | convolution fusion | flops 1612185600 | bytes 28311552 | tf_op jit(solution)/shard_map/while/body/eval_jaxpr/hqk,khd->qhd/dot_general | solution.py:68
  898.7 6.2 fusion.61
  904.9 16.5 %convolution_bitcast_fusion = f32[1,768,768]{2,1,0:T(8,128)} fusion(bf16[8192,768]{1,0:T(8,128)(2,1)} %get-tuple-element.87, bf16[8192,768]{1,0:T(8,128)(2,1)} %all-gather.12.cloned.1.call-done), kind=kOutput, calls=%fused_computation.76 | convolution fusion | flops 9663676416 | bytes 27525120 | tf_op jit(solution)/shard_map/dot_general | solution.py:83
  921.4 16.3 %convolution_bitcast_fusion.1 = f32[1,768,768]{2,1,0:T(8,128)} fusion(bf16[8192,768]{1,0:T(8,128)(2,1)} %all-gather.10.cloned.1.call-done, bf16[8192,768]{1,0:T(8,128)(2,1)} %add_convert_fusion), kind=kOutput, calls=%fused_computation.77 | convolution fusion | flops 9663676416 | bytes 27525120 | tf_op jit(solution)/shard_map/dot_general | solution.py:83
  940.4 7.7 fusion.28
  954.4 37.7 %all-reduce = f32[2,768]{1,0:T(2,128)S(1)} all-reduce(f32[2,768]{1,0:T(2,128)S(1)} %pad_maximum_fusion.1), channel_id=6, replica_groups=mesh['expert'=8,'narrow'=4] {'expert','narrow'}, use_global_device_ids=true, to_apply=%region_22.23.clone | all-reduce | flops 1536 | bytes 12288
  992.7 56.6 %reduce-scatter.10.cloned.1.call-done = f32[24,2304]{1,0:T(8,128)} async-done(((f32[768,2304]{1,0:T(8,128)}), f32[24,2304]{1,0:T(8,128)}) %reduce-scatter.10.cloned.1.call-update) | async-done | bytes 221200 | tf_op jit(solution)/shard_map/reduce_scatter | solution.py:204
  (145 shorter events, 75.4 us)
Async XLA Ops:
  7.2 327.6 %copy-start = (bf16[1,768,768]{2,1,0:T(8,128)(2,1)S(1)}, bf16[1,768,768]{2,1,0:T(8,128)(2,1)}, u32[]{:S(2)}) copy-start(bf16[1,768,768]{2,1,0:T(8,128)(2,1)} %param.17) | copy-start | bytes 3538948
  7.2 66.7 %all-gather.6.cloned.1.call-start = ((), (), s32[]{:S(2)}) async-start(), calls=%async_computation.8 | async-start | bytes 3649536 | tf_op jit(solution)/shard_map/all_gather | solution.py:102
  7.9 145.8 %all-gather.8.cloned.1.call-start = ((), (), s32[]{:S(2)}) async-start(), calls=%async_computation.9 | async-start | bytes 1216512 | tf_op jit(solution)/shard_map/all_gather | solution.py:103
  8.7 326.1 %all-gather.10.cloned.1.call-start = ((), (), s32[]{:S(2)}) async-start(), calls=%async_computation.10 | async-start | bytes 15728640 | tf_op jit(solution)/shard_map/all_gather | solution.py:137
  52.1 30.4 %copy-start.29 = (f32[768]{0:T(1024)}, f32[768]{0:T(1024)S(1)}, u32[]{:S(2)}) copy-start(f32[768]{0:T(1024)S(1)} %get-tuple-element.86) | copy-start | bytes 9220
  52.1 105.8 %copy-start.21 = (f32[768]{0:T(1024)}, f32[768]{0:T(1024)S(1)}, u32[]{:S(2)}) copy-start(f32[768]{0:T(1024)S(1)} %get-tuple-element.85) | copy-start | bytes 9220
  57.0 194.6 %copy-start.34 = (s32[1024,1]{0,1:T(1,128)}, s32[1024,1]{0,1:T(1,128)S(1)}, u32[]{:S(2)}) copy-start(s32[1024,1]{0,1:T(1,128)S(1)} %compare_select_fusion) | copy-start | bytes 12292
  58.4 73.5 %copy-start.1 = (pred[1024,1024]{0,1:T(8,128)(4,1)}, pred[1024,1024]{0,1:T(8,128)(4,1)S(1)}, u32[]{:S(2)}) copy-start(pred[1024,1024]{0,1:T(8,128)(4,1)S(1)} %fusion.13) | copy-start | bytes 3145732
  63.1 19.5 %copy-start.25 = (f32[1024]{0:T(1024)}, f32[1024]{0:T(1024)S(1)}, u32[]{:S(2)}) copy-start(f32[1024]{0:T(1024)S(1)} %broadcast_multiply_fusion.5) | copy-start | bytes 12292
  64.9 17.6 %copy-start.31 = (f32[1024]{0:T(1024)}, f32[1024]{0:T(1024)S(1)}, u32[]{:S(2)}) copy-start(f32[1024]{0:T(1024)S(1)} %add_rsqrt_fusion.1) | copy-start | bytes 12292
  110.7 21.1 %copy-start.15 = (f32[12,1024]{1,0:T(8,128)}, f32[12,1024]{1,0:T(8,128)S(1)}, u32[]{:S(2)}) copy-start(f32[12,1024]{1,0:T(8,128)S(1)} %get-tuple-element.91) | copy-start | bytes 147460
  244.9 171.0 %all-gather.12.cloned.1.call-start = ((), (), s32[]{:S(2)}) async-start(), calls=%async_computation.12 | async-start | bytes 15728640 | tf_op jit(solution)/shard_map/all_gather | solution.py:165
  246.7 13.0 %copy-start.6 = (bf16[1024,768]{0,1:T(8,128)(2,1)}, bf16[1024,768]{0,1:T(8,128)(2,1)S(1)}, u32[]{:S(2)}) copy-start(bf16[1024,768]{0,1:T(8,128)(2,1)S(1)} %copy.50) | copy-start | bytes 4718596
  334.7 228.4 %reduce-scatter.8.cloned.1.call-start = ((), (), s32[]{:S(2)}) async-start(), calls=%async_computation.13 | async-start | bytes 15728640 | tf_op jit(solution)/shard_map/reduce_scatter | solution.py:170
  334.8 81.0 %copy-start.37 = (bf16[1,768,768]{2,1,0:T(8,128)(2,1)S(1)}, bf16[1,768,768]{2,1,0:T(8,128)(2,1)}, u32[]{:S(2)}) copy-start(bf16[1,768,768]{2,1,0:T(8,128)(2,1)} %param.18) | copy-start | bytes 3538948
  463.9 200.8 %reduce-scatter.6.cloned.1.call-start = ((), (), s32[]{:S(2)}) async-start(), calls=%async_computation.11 | async-start | bytes 15728640 | tf_op jit(solution)/shard_map/reduce_scatter | solution.py:140
  563.1 101.6 %all-to-all-start.3 = ((bf16[8,256,768]{2,1,0:T(8,128)(2,1)}), bf16[8,256,768]{2,1,0:T(8,128)(2,1)}, u32[]{:S(2)}, u32[]{:S(2)}) async-start(bf16[8,256,768]{2,1,0:T(8,128)(2,1)} %bitcast.124), calls=%async_computation.5 | async-start | bytes 6291456 | tf_op jit(solution)/shard_map/all_to_all | solution.py:176
  568.6 101.6 %copy-start.35 = (s32[1024,1]{0,1:T(1,128)S(1)}, s32[1024,1]{0,1:T(1,128)}, u32[]{:S(2)}) copy-start(s32[1024,1]{0,1:T(1,128)} %copy-done.34) | copy-start | bytes 12292
  568.6 101.6 %copy-start.16 = (f32[12,1024]{1,0:T(8,128)S(1)}, f32[12,1024]{1,0:T(8,128)}, u32[]{:S(2)}) copy-start(f32[12,1024]{1,0:T(8,128)} %copy-done.15) | copy-start | bytes 147460
  568.6 101.6 %copy-start.18 = (f32[12,1024]{1,0:T(8,128)S(1)}, f32[12,1024]{1,0:T(8,128)}, u32[]{:S(2)}) copy-start(f32[12,1024]{1,0:T(8,128)} %copy-done.17) | copy-start | bytes 147460
  664.7 76.3 %all-to-all-start.1 = ((bf16[8,256,768]{2,1,0:T(8,128)(2,1)}), bf16[8,256,768]{2,1,0:T(8,128)(2,1)}, u32[]{:S(2)}, u32[]{:S(2)}) async-start(bf16[8,256,768]{2,1,0:T(8,128)(2,1)} %bitcast.123), calls=%async_computation.2 | async-start | bytes 6291456 | tf_op jit(solution)/shard_map/all_to_all | solution.py:146
  670.2 322.5 %reduce-scatter.12.cloned.1.call-start = ((), (), s32[]{:S(2)}) async-start(), calls=%async_computation.15 | async-start | bytes 2433024 | tf_op jit(solution)/shard_map/reduce_scatter | solution.py:205
  741.0 10.6 %copy-start.20 = (f32[1024]{0:T(1024)S(1)}, f32[1024]{0:T(1024)}, u32[]{:S(2)}) copy-start(f32[1024]{0:T(1024)} %copy-done.19) | copy-start | bytes 12292
  741.0 10.6 %copy-start.22 = (f32[768]{0:T(1024)S(1)}, f32[768]{0:T(1024)}, u32[]{:S(2)}) copy-start(f32[768]{0:T(1024)} %copy-done.21) | copy-start | bytes 9220
  741.0 10.6 %copy-start.24 = (f32[1024]{0:T(1024)S(1)}, f32[1024]{0:T(1024)}, u32[]{:S(2)}) copy-start(f32[1024]{0:T(1024)} %copy-done.23) | copy-start | bytes 12292
  748.9 7.1 copy-start.7
  748.9 7.1 copy-start.28
  826.1 223.2 %reduce-scatter.10.cloned.1.call-start = ((), (), s32[]{:S(2)}) async-start(), calls=%async_computation.14 | async-start | bytes 7299072 | tf_op jit(solution)/shard_map/reduce_scatter | solution.py:204
  882.4 13.4 %copy-start.11 = (bf16[1,1024,1,12,64]{1,4,3,2,0:T(8,128)(2,1)S(1)}, bf16[1,1024,1,12,64]{1,4,3,2,0:T(8,128)(2,1)}, u32[]{:S(2)}) copy-start(bf16[1,1024,1,12,64]{1,4,3,2,0:T(8,128)(2,1)} %fusion.44) | copy-start | bytes 4718596
  882.4 13.4 %copy-start.13 = (bf16[1,1024,1,12,64]{1,4,3,2,0:T(8,128)(2,1)S(1)}, bf16[1,1024,1,12,64]{1,4,3,2,0:T(8,128)(2,1)}, u32[]{:S(2)}) copy-start(bf16[1,1024,1,12,64]{1,4,3,2,0:T(8,128)(2,1)} %fusion.45) | copy-start | bytes 4718596
  921.4 16.3 %copy-start.33 = (f32[768]{0:T(1024)S(1)}, f32[768]{0:T(1024)}, u32[]{:S(2)}) copy-start(f32[768]{0:T(1024)} %get-tuple-element.81) | copy-start | bytes 9220
  940.4 7.7 copy-start.10
  (17 other events, 43.7 us)
Sparse Core Ops, SparseCore 0:
  10.9 62.9 all-gather.5
  76.8 52.8 all-gather.7
  245.0 81.1 all-gather.9
  334.8 80.9 all-gather.11
  464.0 99.0 reduce-scatter.7
  565.6 99.0 reduce-scatter.5
  826.2 97.1 reduce-scatter.11
  930.6 118.6 reduce-scatter.9
where the time goes:
time: 1070 us; the launch traced here: 1060 us
  waiting for transfers between devices  323 us (30%)
  matrix products  323 us (30%)
  blocking collectives  232 us (22%)
  other arithmetic  87.2 us (8%)
  local copies, waits for them, and re-layouts  65.5 us (6%)
  between operations  15 us (1%)
  starting transfers between devices  11.4 us (1%)
    reduce_scatter x1, waiting for transfers between devices, local(): lax.psum_scatter(jnp.dot(activated, w_hid[0], preferred_element_type=jnp....  96 us
    reduce_scatter x1, waiting for transfers between devices, local(): lax.psum_scatter(over_columns(grad_pre, w_in[0]).astype(jnp.bfloat16), 'n...  81.2 us
    all_to_all x1, blocking collectives, local(): lax.all_to_all(to_slots(act_two), 'expert', split_axis=0, concat_axis=0,...  75.8 us
    all_to_all x1, blocking collectives, local(): lax.all_to_all(to_slots((gating * grad_final).astype(jnp.bfloat16)), 'exp...  75 us
    dot_general x1, matrix products, local(): pre_act = jnp.dot(all_rows, w_in[0], preferred_element_type=jnp.float32)  64.8 us
    all_to_all x1, waiting for transfers between devices, local(): lax.all_to_all(returned.reshape(n_expert, capacity, model_width), 'expert...  62.3 us
    dot_general x4, matrix products, over_columns(): lax.dot_general(left, right, (((1,), (1,)), ((), ())), preferred_element_...  59.5 us
    reduce_scatter x1, waiting for transfers between devices, local(): lax.psum_scatter(grad_qkv_w, ('expert', 'narrow'), scatter_dimension=0, t...  56.6 us
  transfers between devices with their start and end apart: 10, of which 6 were waited for; matrix products, arithmetic and copies ran while one was open for 31% of the time, Pallas kernels for 0%

commit v1 on v0

v1 whole, which is shorter than its diff:
```python
import functools

import jax
import jax.numpy as jnp
from jax import lax
from jax.experimental import pallas as pl
from jax.experimental.pallas import tpu as pltpu
from jax.sharding import PartitionSpec as P

HEAD_DIM = 64
SEQ = 1024
BLOCK = 256
LOOKBACK = 2
EPSILON = 1e-05
BIG_NEGATIVE = -1e30
F32 = jnp.float32
BF16 = jnp.bfloat16

TAIL_P = 0.3
TAIL_C = (
    0.11962923306946524,
    0.12075497050525577,
    0.0999071263144056,
    0.12858273368127124,
    -0.053723704944995426,
    0.20639718480180155,
    -0.1572285075725372,
    0.03568089149479804,
)


def dot(a, b):
    return lax.dot_general(a, b, (((1,), (0,)), ((), ())), preferred_element_type=F32)


def dot_t(a, b):
    return lax.dot_general(a, b, (((1,), (1,)), ((), ())), preferred_element_type=F32)


def t_dot(a, b):
    return lax.dot_general(a, b, (((0,), (0,)), ((), ())), preferred_element_type=F32)


def normalize(values):
    centre = jnp.mean(values, axis=-1, keepdims=True)
    shifted = values - centre
    factor = lax.rsqrt(jnp.mean(shifted * shifted, axis=-1, keepdims=True) + EPSILON)
    return shifted * factor, factor


def norm_back(grad_normed, normed, factor):
    return factor * (
        grad_normed
        - jnp.mean(grad_normed, axis=-1, keepdims=True)
        - normed * jnp.mean(grad_normed * normed, axis=-1, keepdims=True)
    )


def gelu_pair(u):
    size = jnp.abs(u)
    t = 1.0 / (1.0 + TAIL_P * size)
    poly = jnp.full_like(t, TAIL_C[-1])
    for c in TAIL_C[-2::-1]:
        poly = poly * t + c
    bell = jnp.exp(-0.5 * (u * u))
    tail = poly * t * bell
    phi = jnp.where(u >= 0, 1.0 - tail, tail)
    return u * phi, phi + u * (bell * 0.3989422804014327)


def iota(shape, dim):
    return lax.broadcasted_iota(jnp.int32, shape, dim)


def prep_kernel(capacity, experts, rrow_ref, rcol_ref, gate_ref, ct_ref, srow_ref, scol_ref, send_ref):
    tokens = ct_ref.shape[0]
    wide = max(8, experts)
    hot = (iota((wide, tokens), 0) == rrow_ref[...]).astype(F32)
    before = (iota((tokens, tokens), 0) < iota((tokens, tokens), 1)).astype(BF16)
    rank = dot(hot.astype(BF16), before)
    base = (iota((wide, tokens), 0) * capacity).astype(F32)
    srow = jnp.sum(hot * (rank + base), axis=0, keepdims=True)
    srow_ref[...] = jnp.broadcast_to(srow, srow_ref.shape)
    hot_c = (iota((tokens, 128), 1) == rcol_ref[...]).astype(F32)
    after = (iota((tokens, tokens), 1) < iota((tokens, tokens), 0)).astype(BF16)
    rank_c = dot(after, hot_c.astype(BF16))
    base_c = (iota((tokens, 128), 1) * capacity).astype(F32)
    scol_ref[...] = jnp.sum(hot_c * (rank_c + base_c), axis=1, keepdims=True)
    gated = (jax.nn.sigmoid(gate_ref[...]) * ct_ref[...].astype(F32)).astype(BF16)
    fill_slots(srow, gated, send_ref)


def fill_slots(srow, values, send_ref):
    rows = send_ref.shape[0]
    tokens = values.shape[0]

    @pl.loop(0, rows // BLOCK)
    def _(i):
        first = i * BLOCK
        ids = (iota((BLOCK, tokens), 0) + first).astype(F32)
        pick = (ids == srow).astype(BF16)
        send_ref[pl.ds(pl.multiple_of(first, BLOCK), BLOCK), :] = dot(pick, values).astype(BF16)


def prep(routes, gate_logit, cotangent, experts, capacity):
    tokens, width = cotangent.shape
    return pl.pallas_call(
        functools.partial(prep_kernel, capacity, experts),
        out_shape=(
            jax.ShapeDtypeStruct((8, tokens), F32),
            jax.ShapeDtypeStruct((tokens, 1), F32),
            jax.ShapeDtypeStruct((experts * capacity, width), BF16),
        ),
        compiler_params=pltpu.CompilerParams(vmem_limit_bytes=56 << 20),
        cost_estimate=pl.CostEstimate(flops=8 << 30, bytes_accessed=8 << 20, transcendentals=0),
    )(routes.reshape(1, tokens), routes, gate_logit.reshape(tokens, 1), cotangent)


def fwd_kernel(
    x_ref, w_ref, gain_ref, segr_ref, segc_ref, srow_ref, qkv_ref, c_ref, stat_ref, h_ref, send_ref, act_scr, bias_scr, col_scr
):
    tokens, width = x_ref.shape
    blocks = tokens // BLOCK
    pairs = width // 128
    gain_one = gain_ref[0:1, :]
    gain_two = gain_ref[1:2, :]

    @pl.loop(0, blocks)
    def _(i):
        rows = pl.ds(pl.multiple_of(i * BLOCK, BLOCK), BLOCK)
        normed, _f = normalize(x_ref[rows, :].astype(F32))
        act = (normed * gain_one).astype(BF16)
        qkv_ref[rows, :] = dot(act, w_ref[:, : 3 * width]).astype(BF16)

    col_scr[...] = jnp.zeros_like(col_scr)
    low = iota((BLOCK, 128), 1) < HEAD_DIM
    for qb in range(blocks):
        kb = max(0, qb - LOOKBACK)
        span = (qb - kb + 1) * BLOCK
        rows = pl.ds(qb * BLOCK, BLOCK)
        keys = pl.ds(kb * BLOCK, span)
        q_pos = iota((BLOCK, span), 0) + qb * BLOCK
        k_pos = iota((BLOCK, span), 1) + kb * BLOCK
        ok = (k_pos <= q_pos) & (segc_ref[rows, :] == segr_ref[0:1, keys])
        bias_scr[:, :span] = jnp.where(ok, 0.0, BIG_NEGATIVE)

        @pl.loop(0, pairs)
        def _(hp):
            at = pl.multiple_of(hp * 128, 128)
            q = qkv_ref[rows, pl.ds(at, 128)] * jnp.asarray(HEAD_DIM**-0.5, BF16)
            k = qkv_ref[keys, pl.ds(width + at, 128)]
            v = qkv_ref[keys, pl.ds(2 * width + at, 128)]
            outs = []
            col = col_scr[rows, :]
            for half in range(2):
                mine = low if half == 0 else ~low
                s = dot_t(jnp.where(mine, q, 0), k) + bias_scr[:, :span]
                top = jnp.max(s, axis=1, keepdims=True)
                raised = jnp.exp(s - top)
                total = jnp.sum(raised, axis=1, keepdims=True)
                outs.append(dot((raised * (1.0 / total)).astype(BF16), v))
                col = jnp.where(iota((BLOCK, 128), 1) == 2 * hp + half, top + jnp.log(total), col)
            col_scr[rows, :] = col
            c_ref[rows, pl.ds(at, 128)] = jnp.where(low, outs[0], outs[1]).astype(BF16)

    stat_ref[...] = col_scr[...].T

    @pl.loop(0, blocks)
    def _(i):
        rows = pl.ds(pl.multiple_of(i * BLOCK, BLOCK), BLOCK)
        hidden = x_ref[rows, :].astype(F32) + dot(c_ref[rows, :], w_ref[:, 3 * width : 4 * width])
        h_ref[rows, :] = hidden
        normed, _f = normalize(hidden)
        act_scr[rows, :] = (normed * gain_two).astype(BF16)

    fill_slots(srow_ref[0:1, :], act_scr[...], send_ref)


def attend_fwd(tokens_in, w_all, gains, segr, segc, srow, slot_rows):
    tokens, width = tokens_in.shape
    return pl.pallas_call(
        fwd_kernel,
        out_shape=(
            jax.ShapeDtypeStruct((tokens, 3 * width), BF16),
            jax.ShapeDtypeStruct((tokens, width), BF16),
            jax.ShapeDtypeStruct((128, tokens), F32),
            jax.ShapeDtypeStruct((tokens, width), F32),
            jax.ShapeDtypeStruct((slot_rows, width), BF16),
        ),
        scratch_shapes=[
            pltpu.VMEM((tokens, width), BF16),
            pltpu.VMEM((BLOCK, (LOOKBACK + 1) * BLOCK), F32),
            pltpu.VMEM((tokens, 128), F32),
        ],
        compiler_params=pltpu.CompilerParams(vmem_limit_bytes=56 << 20),
        cost_estimate=pl.CostEstimate(flops=40 << 30, bytes_accessed=24 << 20, transcendentals=0),
    )(tokens_in, w_all, gains, segr, segc, srow)


def expert_kernel(a_ref, dy_ref, win_ref, whid_ref, g_ref, du_ref, da_ref, acc_scr):
    a = a_ref[...]
    dy = dy_ref[...]
    parts = win_ref.shape[0]
    wide = win_ref.shape[2]
    acc_scr[...] = jnp.zeros_like(acc_scr)

    @pl.loop(0, parts)
    def _(j):
        cols = pl.ds(pl.multiple_of(j * wide, wide), wide)
        u = dot(a, win_ref[j])
        grad = dot_t(dy, whid_ref[j])
        g, slope = gelu_pair(u)
        g_ref[:, cols] = g.astype(BF16)
        du = (grad * slope).astype(BF16)
        du_ref[:, cols] = du
        acc_scr[...] += dot_t(du, win_ref[j])

    da_ref[...] = acc_scr[...].astype(BF16)


def experts(acts, grads, w_in, w_hid):
    rows, width = acts.shape
    parts, _, wide = w_in.shape
    hidden = parts * wide
    row_spec = pl.BlockSpec((BLOCK, width), lambda i: (i, 0))
    wide_spec = pl.BlockSpec((BLOCK, hidden), lambda i: (i, 0))
    return pl.pallas_call(
        expert_kernel,
        grid=(rows // BLOCK,),
        out_shape=(
            jax.ShapeDtypeStruct((rows, hidden), BF16),
            jax.ShapeDtypeStruct((rows, hidden), BF16),
            jax.ShapeDtypeStruct((rows, width), BF16),
        ),
        in_specs=[
            row_spec,
            row_spec,
            pl.BlockSpec(w_in.shape, lambda i: (0, 0, 0), pipeline_mode=pl.Buffered(1)),
            pl.BlockSpec(w_hid.shape, lambda i: (0, 0, 0), pipeline_mode=pl.Buffered(1)),
        ],
        out_specs=(wide_spec, wide_spec, row_spec),
        scratch_shapes=[pltpu.VMEM((BLOCK, width), F32)],
        compiler_params=pltpu.CompilerParams(vmem_limit_bytes=56 << 20),
        cost_estimate=pl.CostEstimate(flops=60 << 30, bytes_accessed=40 << 20, transcendentals=0),
    )(acts, grads, w_in, w_hid)


def out_kernel(ret_ref, scol_ref, h_ref, gate_ref, out_ref):
    tokens, rows = out_ref.shape[0], ret_ref.shape[0]
    pick = (iota((tokens, rows), 1).astype(F32) == scol_ref[...]).astype(BF16)
    y = dot(pick, ret_ref[...])
    out_ref[...] = (h_ref[...] + jax.nn.sigmoid(gate_ref[...]) * y).astype(BF16)


def block_output(returned, scol, hidden, gate_logit):
    rows, width = returned.shape
    tokens = hidden.shape[0]
    tile = pl.BlockSpec((BLOCK, width), lambda i: (i, 0))
    column = pl.BlockSpec((BLOCK, 1), lambda i: (i, 0))
    return pl.pallas_call(
        out_kernel,
        grid=(tokens // BLOCK,),
        out_shape=jax.ShapeDtypeStruct((tokens, width), BF16),
        in_specs=[pl.BlockSpec((rows, width), lambda i: (0, 0)), column, tile, column],
        out_specs=tile,
        compiler_params=pltpu.CompilerParams(vmem_limit_bytes=40 << 20),
        cost_estimate=pl.CostEstimate(flops=4 << 30, bytes_accessed=10 << 20, transcendentals=0),
    )(returned, scol, hidden, gate_logit.reshape(tokens, 1))


def bwd_kernel(
    ret_ref,
    scol_ref,
    x_ref,
    ct_ref,
    h_ref,
    qkv_ref,
    c_ref,
    stat_ref,
    w_ref,
    gain_ref,
    segr_ref,
    segc_ref,
    gt_ref,
    gw_ref,
    gg_ref,
    dc_scr,
    dhb_scr,
    dqkv_scr,
    act_scr,
    d_scr,
    dk_scr,
    dv_scr,
):
    tokens, width = x_ref.shape
    slots = ret_ref.shape[0]
    blocks = tokens // BLOCK
    pairs = width // 128
    gain_one = gain_ref[0:1, :]
    gain_two = gain_ref[1:2, :]
    gg_ref[...] = jnp.zeros_like(gg_ref)
    member = (iota((16, width), 1) // HEAD_DIM == iota((16, width), 0)).astype(F32)

    for i in range(blocks):
        rows = pl.ds(i * BLOCK, BLOCK)
        pick = (iota((BLOCK, slots), 1).astype(F32) == scol_ref[rows, :]).astype(BF16)
        da = dot(pick, ret_ref[...])
        normed, factor = normalize(h_ref[rows, :])
        gg_ref[1:2, :] += jnp.sum(da * normed, axis=0, keepdims=True)
        dh = ct_ref[rows, :].astype(F32) + norm_back(da * gain_two, normed, factor)
        gt_ref[rows, :] = dh
        dhb = dh.astype(BF16)
        dhb_scr[rows, :] = dhb
        dc = dot_t(dhb, w_ref[:, 3 * width : 4 * width]).astype(BF16)
        dc_scr[rows, :] = dc
        d_scr[:, rows] = lax.dot_general(
            member,
            dc.astype(F32) * c_ref[rows, :].astype(F32),
            (((1,), (1,)), ((), ())),
            precision=lax.Precision.HIGHEST,
            preferred_element_type=F32,
        )

    gw_ref[:, 3 * width : 4 * width] = t_dot(c_ref[...], dhb_scr[...])
    low = iota((BLOCK, 128), 1) < HEAD_DIM
    scale = HEAD_DIM**-0.5

    @pl.loop(0, pairs)
    def _(hp):
        at = pl.multiple_of(hp * 128, 128)
        dk_scr[...] = jnp.zeros_like(dk_scr)
        dv_scr[...] = jnp.zeros_like(dv_scr)
        for qb in range(blocks):
            rows = pl.ds(qb * BLOCK, BLOCK)
            q = qkv_ref[rows, pl.ds(at, 128)] * jnp.asarray(scale, BF16)
            dc = dc_scr[rows, pl.ds(at, 128)]
            q_half = [jnp.where(low, q, 0), jnp.where(low, 0, q)]
            dc_half = [jnp.where(low, dc, 0), jnp.where(low, 0, dc)]
            dq = jnp.zeros((BLOCK, 128), F32)
            for kb in range(max(0, qb - LOOKBACK), qb + 1):
                keys = pl.ds(kb * BLOCK, BLOCK)
                k = qkv_ref[keys, pl.ds(width + at, 128)]
                v = qkv_ref[keys, pl.ds(2 * width + at, 128)]
                ok = segc_ref[keys, :] == segr_ref[0:1, rows]
                if kb == qb:
                    ok = ok & (iota((BLOCK, BLOCK), 0) <= iota((BLOCK, BLOCK), 1))
                ps, dss = [], []
                for half in range(2):
                    s = dot_t(k, q_half[half])
                    p = jnp.where(ok, jnp.exp(s - stat_ref[pl.ds(2 * hp + half, 1), rows]), 0.0)
                    dp = dot_t(v, dc_half[half])
                    dss.append((p * (dp - d_scr[pl.ds(2 * hp + half, 1), rows])).astype(BF16))
                    ps.append(p.astype(BF16))
                dv_scr[keys, :] += dot(jnp.concatenate(ps, 1), jnp.concatenate(dc_half, 0))
                dk_scr[keys, :] += dot(jnp.concatenate(dss, 1), jnp.concatenate(q_half, 0))
                dq += jnp.where(low, t_dot(dss[0], k), t_dot(dss[1], k))
            dqkv_scr[rows, pl.ds(at, 128)] = (dq * scale).astype(BF16)
        dqkv_scr[:, pl.ds(width + at, 128)] = dk_scr[...].astype(BF16)
        dqkv_scr[:, pl.ds(2 * width + at, 128)] = dv_scr[...].astype(BF16)

    @pl.loop(0, blocks)
    def _(i):
        rows = pl.ds(pl.multiple_of(i * BLOCK, BLOCK), BLOCK)
        normed, factor = normalize(x_ref[rows, :].astype(F32))
        act_scr[rows, :] = (normed * gain_one).astype(BF16)
        dn = dot_t(dqkv_scr[rows, :], w_ref[:, : 3 * width])
        gg_ref[0:1, :] += jnp.sum(dn * normed, axis=0, keepdims=True)
        gt_ref[rows, :] += norm_back(dn * gain_one, normed, factor)

    gw_ref[:, : 3 * width] = t_dot(act_scr[...], dqkv_scr[...])


def attend_bwd(returned, scol, tokens_in, cotangent, hidden, qkv, context, stats, w_all, gains, segr, segc):
    tokens, width = tokens_in.shape
    return pl.pallas_call(
        bwd_kernel,
        out_shape=(
            jax.ShapeDtypeStruct((tokens, width), F32),
            jax.ShapeDtypeStruct((width, 4 * width), F32),
            jax.ShapeDtypeStruct((8, width), F32),
        ),
        scratch_shapes=[
            pltpu.VMEM((tokens, width), BF16),
            pltpu.VMEM((tokens, width), BF16),
            pltpu.VMEM((tokens, 3 * width), BF16),
            pltpu.VMEM((tokens, width), BF16),
            pltpu.VMEM((16, tokens), F32),
            pltpu.VMEM((tokens, 128), F32),
            pltpu.VMEM((tokens, 128), F32),
        ],
        compiler_params=pltpu.CompilerParams(vmem_limit_bytes=60 << 20),
        cost_estimate=pl.CostEstimate(flops=80 << 30, bytes_accessed=40 << 20, transcendentals=0),
    )(returned, scol, tokens_in, cotangent, hidden, qkv, context, stats, w_all, gains, segr, segc)


def local(tokens, segments, routes, gate_logit, w_qkv, w_out, norm_gains, w_in, w_hid, cotangent):
    tok_count, width = tokens.shape
    n_expert = lax.axis_size("expert")
    n_narrow = lax.axis_size("narrow")
    capacity = 2 * tok_count // n_expert
    slot_rows = n_expert * capacity
    everyone = ("expert", "narrow")

    gain_cols = jnp.pad(norm_gains.T, ((0, 0), (0, 126)))
    w_all = lax.all_gather(
        jnp.concatenate((w_qkv, w_out, gain_cols), axis=1), everyone, axis=0, tiled=True
    )
    gains = w_all[:, 4 * width : 4 * width + 2].T.astype(F32)
    w_in_all = lax.all_gather(w_in[0], "narrow", axis=0, tiled=False)
    w_hid_all = lax.all_gather(w_hid[0], "narrow", axis=0, tiled=False)

    def exchange(values):
        return lax.all_to_all(
            values.reshape(n_expert, capacity, width), "expert", split_axis=0, concat_axis=0, tiled=True
        ).reshape(slot_rows, width)

    segr = segments.reshape(1, tok_count)
    segc = segments.reshape(tok_count, 1)
    srow, scol, dy_slots = prep(routes, gate_logit, cotangent, n_expert, capacity)
    dy_rows = exchange(dy_slots)
    qkv, context, stats, hidden, act_slots = attend_fwd(tokens, w_all, gains, segr, segc, srow, slot_rows)
    act_rows = exchange(act_slots)
    activated, grad_pre, da_rows = experts(act_rows, dy_rows, w_in_all, w_hid_all)
    da_back = exchange(da_rows)
    hidden_units = activated.shape[1]
    y_rows = dot(activated, w_hid_all.reshape(hidden_units, width)).astype(BF16)
    y_back = exchange(y_rows)
    grad_hid = t_dot(activated, dy_rows).astype(BF16)
    grad_in = lax.dot_general(
        act_rows, grad_pre.reshape(slot_rows, n_narrow, -1), (((0,), (0,)), ((), ())), preferred_element_type=F32
    ).astype(BF16)
    grad_tokens, grad_w, grad_gains = attend_bwd(
        da_back, scol, tokens, cotangent, hidden, qkv, context, stats, w_all, gains, segr, segc
    )
    block_out = block_output(y_back, scol, hidden, gate_logit)
    grad_hid_w = lax.psum_scatter(grad_hid, "narrow", scatter_dimension=0, tiled=True).astype(F32)[None]
    grad_in_w = lax.psum_scatter(grad_in, "narrow", scatter_dimension=1, tiled=True).astype(F32)
    grad_in_w = grad_in_w.reshape(1, width, -1)
    packed = jnp.concatenate((grad_w, jnp.pad(grad_gains[:2].T, ((0, 0), (0, 126)))), axis=1)
    own = lax.psum_scatter(packed, everyone, scatter_dimension=0, tiled=True)
    return (
        block_out,
        grad_tokens,
        own[:, : 3 * width],
        own[:, 3 * width : 4 * width],
        own[:, 4 * width : 4 * width + 2].T,
        grad_in_w,
        grad_hid_w,
    )


def solution(mesh):
    placed = (
        P(("expert", "narrow"), None),
        P(("expert", "narrow"), None),
        P(("expert", "narrow"), None),
        P(("expert", "narrow")),
        P(("expert", "narrow"), None),
        P(("expert", "narrow"), None),
        P(None, ("expert", "narrow")),
        P("expert", None, "narrow"),
        P("expert", "narrow", None),
        P(("expert", "narrow"), None),
    )
    return jax.shard_map(
        local,
        mesh=mesh,
        in_specs=placed,
        out_specs=(
            P(("expert", "narrow"), None),
            P(("expert", "narrow"), None),
            P(("expert", "narrow"), None),
            P(("expert", "narrow"), None),
            P(None, ("expert", "narrow")),
            P("expert", None, "narrow"),
            P("expert", "narrow", None),
        ),
        check_vma=False,
    )
```

time: 1070 us -> 679 us (0.63)
  matrix products: 323 us -> 46.1 us
  blocking collectives: 232 us -> 0 us
  Pallas kernels: 0 us -> 173 us
  other arithmetic: 87.2 us -> 16.6 us
  waiting for transfers between devices: 323 us -> 384 us
  local copies, waits for them, and re-layouts: 65.5 us -> 15.6 us
    dot_general x18 -> x3, matrix products: 323 us -> 46.1 us  [the longest x1 15.5 us: local(): lax.dot_general(act_rows, grad_pre.reshape(slot_rows, n_narrow, -1), (((0...]
    reduce_scatter x4 -> x2, waiting for transfers between devices: 234 us -> 0.01 us  [the longest x1 0.01 us: local(): lax.psum_scatter(grad_in, 'narrow', scatter_dimension=1, tiled=True)]
    unnamed x8 -> x7, waiting for transfers between devices: 1.48 us -> 176 us
    pallas_call x0 -> x5, Pallas kernels: none -> 173 us  [the longest x1 56.9 us: experts(): pl.pallas_call(expert_kernel, grid=(rows // BLOCK,), out_shape=(jax.Shape...]
    all_to_all x2 -> x0, blocking collectives: 151 us -> none  [the longest x1 75.8 us: local(): lax.all_to_all(to_slots(act_two), 'expert', split_axis=0, concat_axis=0,...]
    all_gather x4 -> x3, waiting for transfers between devices: 25.2 us -> 112 us  [the longest x1 90.1 us: local(): lax.all_gather(jnp.concatenate((w_qkv, w_out, gain_cols), axis=1), everyo...]
    convert_element_type x4 -> x1, other arithmetic: 44.8 us -> 0.95 us  [local(): gains = w_all[:, 4 * width:4 * width + 2].T.astype(F32)]
    all_gather x1 -> x0, blocking collectives: 43.3 us -> none  [local(): lax.all_gather(norm_gains, ('expert', 'narrow'), axis=1, tiled=True)]
  transfers between devices with their start and end apart: 10 -> 10, of which waited for: 6 -> 6; matrix products, arithmetic and copies ran while one was open for 31% -> 8% of each run, Pallas kernels for 0% -> 17%
where the time goes in v1:
time: 679 us; the launch traced here: 672 us
  waiting for transfers between devices  384 us (57%)
  Pallas kernels  173 us (25%)
  matrix products  46.1 us (7%)
  starting transfers between devices  21.4 us (3%)
  other arithmetic  16.6 us (2%)
  local copies, waits for them, and re-layouts  15.6 us (2%)
  between operations  14.6 us (2%)
    unnamed x7, waiting for transfers between devices  176 us
    all_to_all x4, waiting for transfers between devices, exchange(): lax.all_to_all(values.reshape(n_expert, capacity, width), 'expert', split...  95.4 us
    all_gather x1, waiting for transfers between devices, local(): lax.all_gather(jnp.concatenate((w_qkv, w_out, gain_cols), axis=1), everyo...  90.1 us
    pallas_call x1, Pallas kernels, experts(): pl.pallas_call(expert_kernel, grid=(rows // BLOCK,), out_shape=(jax.Shape...  56.9 us
    pallas_call x1, Pallas kernels, attend_bwd(): pl.pallas_call(bwd_kernel, out_shape=(jax.ShapeDtypeStruct((tokens, width...  54.2 us
    pallas_call x1, Pallas kernels, attend_fwd(): pl.pallas_call(fwd_kernel, out_shape=(jax.ShapeDtypeStruct((tokens, 3 * w...  48.2 us
    all_gather x1, waiting for transfers between devices, local(): w_hid_all = lax.all_gather(w_hid[0], 'narrow', axis=0, tiled=False)  22.2 us
    all_to_all x4, starting transfers between devices, exchange(): lax.all_to_all(values.reshape(n_expert, capacity, width), 'expert', split...  20.3 us
  transfers between devices with their start and end apart: 10, of which 6 were waited for; matrix products, arithmetic and copies ran while one was open for 8% of the time, Pallas kernels for 17%

profile of v1, /device:TPU:0, one launch (start us, length us, event | category | flops | bytes accessed | tf_op | source)
XLA Modules:
  0.0 672.0 jit_solution(6358619984801587864)
XLA Ops:
  8.0 1.6 fusion.7
  10.3 1.7 copy.40.gate_ref
  12.0 1.7 copy.39.rcol_ref
  13.7 9.2 %shard_map.153 = (f32[8,1024]{1,0:T(8,128)}, f32[1024,1]{1,0:T(8,128)}, bf16[2048,768]{1,0:T(8,128)(2,1)}) custom-call(s32[1,1024]{1,0:T(1,128)} %bitcast.48, s32[1024,1]{1,0:T(8,128)} %copy.39.rcol_ref, f32[1024,1]{1,0:T(8,128)} %copy.40.gate_ref, bf16[1024,768]{1,0:T(8,128)(2,1)} %ct_ref.3), custom_call_target="tpu_custom_call" | custom-call | flops 8589934592 | bytes 8388608 | tf_op jit(solution)/shard_map/pallas_call | solution.py:107
  22.9 7.4 %all-to-all-start.1 = ((bf16[8,256,768]{2,1,0:T(8,128)(2,1)}), bf16[8,256,768]{2,1,0:T(8,128)(2,1)S(1)}, u32[]{:S(2)}, u32[]{:S(2)}) async-start(bf16[8,256,768]{2,1,0:T(8,128)(2,1)} %bitcast.42), calls=%async_computation.1 | async-start | bytes 6291456 | tf_op jit(solution)/shard_map/all_to_all | solution.py:413
  31.1 1.0 copy.41.segc_ref
  32.1 90.1 %all-gather.4.cloned.1.call-done.w_ref = bf16[768,3200]{1,0:T(8,128)(2,1)} async-done(((bf16[24,3200]{1,0:T(8,128)(2,1)}), bf16[768,3200]{1,0:T(8,128)(2,1)}) %all-gather.4.cloned.1.call-update) | async-done | bytes 4915216 | tf_op jit(solution)/shard_map/all_gather | solution.py:405
  122.2 1.0 slice_convert_fusion
  123.9 48.2 %shard_map.154 = (bf16[1024,2304]{1,0:T(8,128)(2,1)}, bf16[1024,768]{1,0:T(8,128)(2,1)}, f32[128,1024]{1,0:T(8,128)}, f32[1024,768]{1,0:T(8,128)}, bf16[2048,768]{1,0:T(8,128)(2,1)}) custom-call(bf16[1024,768]{1,0:T(8,128)(2,1)} %x_ref.3, bf16[768,3200]{1,0:T(8,128)(2,1)} %all-gather.4.cloned.1.call-done.w_ref, f32[2,768]{1,0:T(2,128)} %bitcast.45, ...), custom_call_target="tpu_custom_call" | custom-call | flops 42949672960 | bytes 25165824 | tf_op jit(solution)/shard_map/pallas_call | solution.py:181
  172.1 4.5 all-to-all-start
  177.2 22.2 %all-gather.8.cloned.1.call-done.whid_ref = bf16[4,768,768]{2,1,0:T(8,128)(2,1)} async-done(((bf16[1,768,768]{2,1,0:T(8,128)(2,1)}), bf16[4,768,768]{2,1,0:T(8,128)(2,1)}) %all-gather.8.cloned.1.call-update) | async-done | bytes 4718608 | tf_op jit(solution)/shard_map/all_gather | solution.py:410
  199.4 48.6 %all-to-all-done = bf16[8,256,768]{2,1,0:T(8,128)(2,1)} async-done(((bf16[8,256,768]{2,1,0:T(8,128)(2,1)}), bf16[8,256,768]{2,1,0:T(8,128)(2,1)}, u32[]{:S(2)}, u32[]{:S(2)}) %all-to-all-start) | async-done | bytes 3145760 | tf_op jit(solution)/shard_map/all_to_all | solution.py:413
  248.0 56.9 %shard_map.155 = (bf16[2048,3072]{1,0:T(8,128)(2,1)}, bf16[2048,3072]{1,0:T(8,128)(2,1)}, bf16[2048,768]{1,0:T(8,128)(2,1)}) custom-call(bf16[2048,768]{1,0:T(8,128)(2,1)} %bitcast.6.a_ref, bf16[2048,768]{1,0:T(8,128)(2,1)} %bitcast.38, bf16[4,768,768]{2,1,0:T(8,128)(2,1)} %all-gather.6.cloned.1.call-done.win_ref, ...), custom_call_target="tpu_custom_call" | custom-call | flops 64424509440 | bytes 41943040 | tf_op jit(solution)/shard_map/pallas_call | solution.py:227
  304.9 15.5 %fusion.3 = bf16[768,4,768]{2,0,1:T(8,128)(2,1)} fusion(bf16[2048,768,1]{1,0,2:T(8,128)(2,1)} %bitcast.16, bf16[256,4,8,768]{3,2,1,0:T(8,128)(2,1)} %bitcast.51), kind=kOutput, calls=%fused_computation.7 | convolution fusion | flops 9666035712 | bytes 20447232 | tf_op jit(solution)/shard_map/dot_general | solution.py:429
  320.5 4.7 all-to-all-start.3
  325.4 15.2 %convolution_convert_fusion = bf16[3072,768]{1,0:T(8,128)(2,1)} fusion(bf16[2048,3072]{1,0:T(8,128)(2,1)} %get-tuple-element.24, bf16[2048,768]{1,0:T(8,128)(2,1)S(1)} %bitcast.39), kind=kOutput, calls=%fused_computation.5 | convolution fusion | flops 9666035712 | bytes 20447232 | tf_op jit(solution)/shard_map/dot_general | solution.py:41
  340.7 15.4 %convolution_convert_fusion.1 = bf16[2048,768]{1,0:T(8,128)(2,1)} fusion(bf16[2048,3072]{1,0:T(8,128)(2,1)} %get-tuple-element.24, bf16[3072,768]{1,0:T(8,128)(2,1)} %bitcast.50), kind=kOutput, calls=%fused_computation.6 | convolution fusion | flops 9665249280 | bytes 20447232 | tf_op jit(solution)/shard_map/dot_general | solution.py:33
  356.1 39.6 %all-to-all-done.3 = bf16[8,256,768]{2,1,0:T(8,128)(2,1)} async-done(((bf16[8,256,768]{2,1,0:T(8,128)(2,1)}), bf16[8,256,768]{2,1,0:T(8,128)(2,1)}, u32[]{:S(2)}, u32[]{:S(2)}) %all-to-all-start.3) | async-done | bytes 3145760 | tf_op jit(solution)/shard_map/all_to_all | solution.py:413
  395.7 3.6 all-to-all-start.2
  399.6 54.2 %shard_map.157 = (f32[1024,768]{1,0:T(8,128)}, f32[768,3072]{1,0:T(8,128)}, f32[8,768]{1,0:T(8,128)}) custom-call(bf16[2048,768]{1,0:T(8,128)(2,1)} %bitcast.13.ret_ref, f32[1024,1]{1,0:T(8,128)} %get-tuple-element.25.scol_ref, bf16[1024,768]{1,0:T(8,128)(2,1)} %x_ref.3, bf16[1024,768]{1,0:T(8,128)(2,1)} %ct_ref.3, f32[1024,768]{1,0:T(8,128)} %get-tuple-element.26.h_ref, ...), custom_call_target="tpu_custom_call" | custom-call | flops 85899345920 | bytes 41943040 | tf_op jit(solution)/shard_map/pallas_call | solution.py:375
  454.7 8.3 %select_maximum_fusion = f32[768,3200]{1,0:T(8,128)} fusion(f32[768,2]{1,0:T(8,128)S(1)} %copy.48, f32[768,3072]{1,0:T(8,128)} %get-tuple-element.32), kind=kLoop, calls=%fused_computation.3 | loop fusion | flops 7372800 | bytes 19273728 | tf_op jit(solution)/shard_map/concatenate | solution.py:439
  463.0 7.2 %all-to-all-done.2 = bf16[8,256,768]{2,1,0:T(8,128)(2,1)S(1)} async-done(((bf16[8,256,768]{2,1,0:T(8,128)(2,1)}), bf16[8,256,768]{2,1,0:T(8,128)(2,1)S(1)}, u32[]{:S(2)}, u32[]{:S(2)}) %all-to-all-start.2) | async-done | bytes 3145760 | tf_op jit(solution)/shard_map/all_to_all | solution.py:413
  470.2 1.1 copy-done
  471.3 2.0 copy-done.1
  473.3 1.0 copy-done.2
  474.3 4.9 shard_map.156
  479.2 2.9 bitcast_convert_fusion.1
  482.1 2.9 bitcast_convert_fusion
  485.0 175.0 %all-reduce.5.cloned.1.call-done = f32[768,3200]{1,0:T(8,128)} async-done(((f32[768,3200]{1,0:T(8,128)}), f32[768,3200]{1,0:T(8,128)}) %all-reduce.5.cloned.1.call-update) | async-done | bytes 9830416
  660.0 0.8 dynamic-slice_bitcast_fusion
  661.4 1.6 constant_dynamic-slice_fusion
  663.1 1.6 dynamic-slice.2
  (30 shorter events, 5.7 us)
Async XLA Ops:
  7.2 115.1 %all-gather.4.cloned.1.call-start = ((), (), s32[]{:S(2)}) async-start(), calls=%async_computation.6 | async-start | bytes 5068800 | tf_op jit(solution)/shard_map/all_gather | solution.py:405
  9.6 167.6 %all-gather.6.cloned.1.call-start = ((), (), s32[]{:S(2)}) async-start(), calls=%async_computation.7 | async-start | bytes 5898240 | tf_op jit(solution)/shard_map/all_gather | solution.py:409
  22.9 8.2 %copy-start.5 = (s32[1,1024]{1,0:T(1,128)S(1)}, s32[1,1024]{1,0:T(1,128)}, u32[]{:S(2)}) copy-start(s32[1,1024]{1,0:T(1,128)} %segr_ref.3) | copy-start | bytes 12292
  22.9 149.2 %all-to-all-start.1 = ((bf16[8,256,768]{2,1,0:T(8,128)(2,1)}), bf16[8,256,768]{2,1,0:T(8,128)(2,1)S(1)}, u32[]{:S(2)}, u32[]{:S(2)}) async-start(bf16[8,256,768]{2,1,0:T(8,128)(2,1)} %bitcast.42), calls=%async_computation.1 | async-start | bytes 6291456 | tf_op jit(solution)/shard_map/all_to_all | solution.py:413
  30.4 169.0 %all-gather.8.cloned.1.call-start = ((), (), s32[]{:S(2)}) async-start(), calls=%async_computation.8 | async-start | bytes 5898240 | tf_op jit(solution)/shard_map/all_gather | solution.py:410
  172.1 75.9 %copy-start.3 = (bf16[8,256,768]{2,1,0:T(8,128)(2,1)}, bf16[8,256,768]{2,1,0:T(8,128)(2,1)S(1)}, u32[]{:S(2)}) copy-start(bf16[8,256,768]{2,1,0:T(8,128)(2,1)S(1)} %all-to-all-done.1) | copy-start | bytes 9437188
  172.1 75.9 %all-to-all-start = ((bf16[8,256,768]{2,1,0:T(8,128)(2,1)}), bf16[8,256,768]{2,1,0:T(8,128)(2,1)}, u32[]{:S(2)}, u32[]{:S(2)}) async-start(bf16[8,256,768]{2,1,0:T(8,128)(2,1)} %bitcast.43), calls=%async_computation | async-start | bytes 6291456 | tf_op jit(solution)/shard_map/all_to_all | solution.py:413
  176.6 302.6 %reduce-scatter.3.cloned.1.call-start = ((), (), s32[]{:S(2)}) async-start(), calls=%async_computation.9 | async-start | bytes 5898240 | tf_op jit(solution)/shard_map/reduce_scatter | solution.py:437
  320.4 5.0 copy-start.4
  320.5 75.2 %all-to-all-start.3 = ((bf16[8,256,768]{2,1,0:T(8,128)(2,1)}), bf16[8,256,768]{2,1,0:T(8,128)(2,1)}, u32[]{:S(2)}, u32[]{:S(2)}) async-start(bf16[8,256,768]{2,1,0:T(8,128)(2,1)} %bitcast.41), calls=%async_computation.3 | async-start | bytes 6291456 | tf_op jit(solution)/shard_map/all_to_all | solution.py:413
  325.2 156.9 %reduce-scatter.5.cloned.1.call-start = ((), (), s32[]{:S(2)}) async-start(), calls=%async_computation.10 | async-start | bytes 5898240 | tf_op jit(solution)/shard_map/reduce_scatter | solution.py:436
  395.7 74.5 %all-to-all-start.2 = ((bf16[8,256,768]{2,1,0:T(8,128)(2,1)}), bf16[8,256,768]{2,1,0:T(8,128)(2,1)S(1)}, u32[]{:S(2)}, u32[]{:S(2)}) async-start(bf16[8,256,768]{2,1,0:T(8,128)(2,1)} %bitcast.40), calls=%async_computation.2 | async-start | bytes 6291456 | tf_op jit(solution)/shard_map/all_to_all | solution.py:413
  399.4 260.7 %all-reduce.5.cloned.1.call-start = ((), (), s32[]{:S(2)}) async-start(), calls=%async_computation.11 | async-start | bytes 19660800
  470.2 1.1 copy-start
  471.3 2.0 copy-start.1
  473.3 1.0 copy-start.2
Sparse Core Ops, SparseCore 0:
  11.5 110.6 all-gather.3
  123.8 36.5 all-gather.5
  161.9 37.4 all-gather.7
  320.6 46.8 reduce-scatter.2
  370.0 47.8 reduce-scatter.4
  463.1 196.8 all-reduce.4

commit v2 on v1

--- a/solution.py
+++ b/solution.py
@@ -393,6 +393,394 @@
     )(returned, scol, tokens_in, cotangent, hidden, qkv, context, stats, w_all, gains, segr, segc)
 
 
+MESH = pl.DeviceIdType.MESH
+
+
+def place():
+    e, n = lax.axis_index("expert"), lax.axis_index("narrow")
+    return e // 2, lax.rem(e, 2), n // 2, lax.rem(n, 2)
+
+
+def device(z, y, x, c):
+    return (z * 2 + y, x * 2 + c)
+
+
+def across(z, k):
+    hi, lo = z // 2, lax.rem(z, 2)
+    hi = 1 - hi if k & 2 else hi
+    lo = 1 - lo if k & 1 else lo
+    return hi * 2 + lo
+
+
+class Links:
+    def __init__(self, send, recv):
+        self.send, self.recv, self.used = send, recv, 0
+
+    def make(self, src, dst, to):
+        i = self.used
+        self.used += 1
+        return pltpu.make_async_remote_copy(
+            src_ref=src, dst_ref=dst, send_sem=self.send.at[i], recv_sem=self.recv.at[i], device_id=to, device_id_type=MESH
+        )
+
+    def push(self, src, dst, to):
+        copy = self.make(src, dst, to)
+        copy.start()
+        return copy
+
+
+class Loads:
+    def __init__(self, sems):
+        self.sems, self.used = sems, 0
+
+    def start(self, src, dst):
+        copy = pltpu.make_async_copy(src, dst, self.sems.at[self.used])
+        self.used += 1
+        copy.start()
+        return copy
+
+
+def greet(peers):
+    barrier = pltpu.get_barrier_semaphore()
+    for peer in peers:
+        pl.semaphore_signal(barrier, inc=1, device_id=peer, device_id_type=MESH)
+    pl.semaphore_wait(barrier, len(peers))
+
+
+FLIPS = (6, 7, 4, 5, 2, 3, 1)
+
+
+def peers_of(z, y, x, c):
+    return [device(across(z, k >> 1), 1 - y if k & 1 else y, x, c) for k in FLIPS]
+
+
+def tail_kernel(
+    ret_hbm,
+    x_hbm,
+    ct_hbm,
+    h_hbm,
+    qkv_hbm,
+    c_hbm,
+    w_hbm,
+    yrow_hbm,
+    gin_hbm,
+    ghid_hbm,
+    scol_ref,
+    stat_ref,
+    gain_ref,
+    segr_ref,
+    segc_ref,
+    gt_hbm,
+    yback_hbm,
+    r1_hbm,
+    r2_hbm,
+    gin_out,
+    ghid_out,
+    own_ref,
+    gg_ref,
+    ret_ref,
+    x_ref,
+    ct_ref,
+    h_ref,
+    qkv_ref,
+    c_ref,
+    w_ref,
+    gt_ref,
+    dc_scr,
+    dhb_scr,
+    dqkv_scr,
+    act_scr,
+    d_scr,
+    dk_scr,
+    dv_scr,
+    gq,
+    rc,
+    r1a,
+    r1b,
+    r2a,
+    r2b,
+    r3,
+    fin,
+    r4,
+    ggs,
+    rg,
+    na,
+    nb,
+    nsum,
+    nout,
+    send_sems,
+    recv_sems,
+    load_sems,
+):
+    z, y, x, c = place()
+    me_e = z * 2 + y
+    tokens, width = x_ref.shape
+    slots = ret_ref.shape[0]
+    blocks = tokens // BLOCK
+    pairs = width // 128
+    core, xpeer, ypeer = device(z, y, x, 1 - c), device(z, y, 1 - x, c), device(z, 1 - y, x, c)
+    far = peers_of(z, y, x, c)
+    links = Links(send_sems, recv_sems)
+    loads = Loads(load_sems)
+
+    first = [
+        loads.start(a, b)
+        for a, b in ((ret_hbm, ret_ref), (h_hbm, h_ref), (ct_hbm, ct_ref), (c_hbm, c_ref), (w_hbm, w_ref))
+    ]
+    second = [loads.start(a, b) for a, b in ((qkv_hbm, qkv_ref), (x_hbm, x_ref))]
+    own_y = loads.start(yrow_hbm.at[me_e], yback_hbm.at[me_e])
+
+    greet(far + [core, xpeer])
+
+    y_copies = [links.push(yrow_hbm.at[to[0]], yback_hbm.at[me_e], to) for to in far]
+    w_copies = []
+    for a, src in enumerate((gin_hbm, ghid_hbm)):
+        for xx in range(2):
+            w_copies.append(links.push(src.at[xx * 2 + 1 - c], r1_hbm.at[a, xx], core))
+
+    gain_one = gain_ref[0:1, :]
+    gain_two = gain_ref[1:2, :]
+    member = (iota((16, width), 1) // HEAD_DIM == iota((16, width), 0)).astype(F32)
+    for copy in first:
+        copy.wait()
+    ggs[...] = jnp.zeros_like(ggs)
+
+    @pl.loop(0, blocks)
+    def _(i):
+        rows = pl.ds(pl.multiple_of(i * BLOCK, BLOCK), BLOCK)
+        pick = (iota((BLOCK, slots), 1).astype(F32) == scol_ref[rows, :]).astype(BF16)
+        da = dot(pick, ret_ref[...])
+        normed, factor = normalize(h_ref[rows, :])
+        ggs[0, 1:2, :] += jnp.sum(da * normed, axis=0, keepdims=True)
+        dh = ct_ref[rows, :].astype(F32) + norm_back(da * gain_two, normed, factor)
+        gt_ref[rows, :] = dh
+        dhb = dh.astype(BF16)
+        dhb_scr[rows, :] = dhb
+        dc = dot_t(dhb, w_ref[:, 3 * width : 4 * width]).astype(BF16)
+        dc_scr[rows, :] = dc
+        d_scr[:, rows] = lax.dot_general(
+            member,
+            dc.astype(F32) * c_ref[rows, :].astype(F32),
+            (((1,), (1,)), ((), ())),
+            precision=lax.Precision.HIGHEST,
+            preferred_element_type=F32,
+        )
+
+    for copy in w_copies:
+        copy.wait()
+    x_copies = []
+    for a, src in enumerate((gin_hbm, ghid_hbm)):
+        for step in range(2):
+            xx = 1 - x if step == 0 else x
+            la = loads.start(src.at[xx * 2 + c], na)
+            lb = loads.start(r1_hbm.at[a, xx], nb)
+            la.wait()
+            lb.wait()
+            nsum[step, a] = (na[...].astype(F32) + nb[...].astype(F32)).astype(BF16)
+            if step == 0:
+                x_copies.append(links.push(nsum.at[0, a], r2_hbm.at[a], xpeer))
+
+    def put_quarter(j, value):
+        for chip in range(16):
+            gq[j, chip // 4, chip // 2 % 2, chip % 2] = value[chip * 48 : chip * 48 + 48, :].astype(BF16)
+
+    put_quarter(3, t_dot(c_ref[...], dhb_scr[...]))
+    for copy in second:
+        copy.wait()
+    low = iota((BLOCK, 128), 1) < HEAD_DIM
+    scale = HEAD_DIM**-0.5
+
+    @pl.loop(0, pairs)
+    def _(hp):
+        at = pl.multiple_of(hp * 128, 128)
+        dk_scr[...] = jnp.zeros_like(dk_scr)
+        dv_scr[...] = jnp.zeros_like(dv_scr)
+        for qb in range(blocks):
+            rows = pl.ds(qb * BLOCK, BLOCK)
+            q = qkv_ref[rows, pl.ds(at, 128)] * jnp.asarray(scale, BF16)
+            dc = dc_scr[rows, pl.ds(at, 128)]
+            q_half = [jnp.where(low, q, 0), jnp.where(low, 0, q)]
+            dc_half = [jnp.where(low, dc, 0), jnp.where(low, 0, dc)]
+            dq = jnp.zeros((BLOCK, 128), F32)
+            for kb in range(max(0, qb - LOOKBACK), qb + 1):
+                keys = pl.ds(kb * BLOCK, BLOCK)
+                k = qkv_ref[keys, pl.ds(width + at, 128)]
+                v = qkv_ref[keys, pl.ds(2 * width + at, 128)]
+                ok = segc_ref[keys, :] == segr_ref[0:1, rows]
+                if kb == qb:
+                    ok = ok & (iota((BLOCK, BLOCK), 0) <= iota((BLOCK, BLOCK), 1))
+                ps, dss = [], []
+                for half in range(2):
+                    s = dot_t(k, q_half[half])
+                    p = jnp.where(ok, jnp.exp(s - stat_ref[pl.ds(2 * hp + half, 1), rows]), 0.0)
+                    dp = dot_t(v, dc_half[half])
+                    dss.append((p * (dp - d_scr[pl.ds(2 * hp + half, 1), rows])).astype(BF16))
+                    ps.append(p.astype(BF16))
+                dv_scr[keys, :] += dot(jnp.concatenate(ps, 1), jnp.concatenate(dc_half, 0))
+                dk_scr[keys, :] += dot(jnp.concatenate(dss, 1), jnp.concatenate(q_half, 0))
+                dq += jnp.where(low, t_dot(dss[0], k), t_dot(dss[1], k))
+            dqkv_scr[rows, pl.ds(at, 128)] = (dq * scale).astype(BF16)
+        dqkv_scr[:, pl.ds(width + at, 128)] = dk_scr[...].astype(BF16)
+        dqkv_scr[:, pl.ds(2 * width + at, 128)] = dv_scr[...].astype(BF16)
+
+    @pl.loop(0, blocks)
+    def _(i):
+        rows = pl.ds(pl.multiple_of(i * BLOCK, BLOCK), BLOCK)
+        normed, _f = normalize(x_ref[rows, :].astype(F32))
+        act_scr[rows, :] = (normed * gain_one).astype(BF16)
+
+    for j in range(3):
+        put_quarter(j, t_dot(act_scr[...], dqkv_scr[:, j * width : (j + 1) * width]))
+    core_copies = [links.push(gq.at[2 * (1 - c) + p], rc.at[p], core) for p in range(2)]
+
+    @pl.loop(0, blocks)
+    def _(i):
+        rows = pl.ds(pl.multiple_of(i * BLOCK, BLOCK), BLOCK)
+        normed, factor = normalize(x_ref[rows, :].astype(F32))
+        dn = dot_t(dqkv_scr[rows, :], w_ref[:, : 3 * width])
+        ggs[0, 0:1, :] += jnp.sum(dn * normed, axis=0, keepdims=True)
+        gt_ref[rows, :] += norm_back(dn * gain_one, normed, factor)
+
+    store_gt = loads.start(gt_ref, gt_hbm)
+    gains_copy = links.push(ggs.at[0], rg.at[0], core)
+    for copy in core_copies:
+        copy.wait()
+    qa, qb_ = 2 * c, 2 * c + 1
+
+    @pl.loop(0, 4)
+    def _(k):
+        for p in range(2):
+            gq[2 * c + p, k] = (gq[2 * c + p, k].astype(F32) + rc[p, k].astype(F32)).astype(BF16)
+
+    copies = [
+        links.push(gq.at[qa, :, :, 1 - x], r1a, xpeer),
+        links.push(gq.at[qb_, :, 1 - y], r1b, ypeer),
+    ]
+    gains_copy.wait()
+    ggs[1] = ggs[0] + rg[0]
+    gains_copy = links.push(ggs.at[1], rg.at[1], xpeer)
+    for copy in copies:
+        copy.wait()
+
+    @pl.loop(0, 4)
+    def _(k):
+        for i in range(2):
+            gq[qa, k, i, x] = (gq[qa, k, i, x].astype(F32) + r1a[k, i].astype(F32)).astype(BF16)
+            gq[qb_, k, y, i] = (gq[qb_, k, y, i].astype(F32) + r1b[k, i].astype(F32)).astype(BF16)
+
+    copies = [
+        links.push(gq.at[qa, :, 1 - y, x], r2a, ypeer),
+        links.push(gq.at[qb_, :, y, 1 - x], r2b, xpeer),
+    ]
+    gains_copy.wait()
+    ggs[2] = ggs[1] + rg[1]
+    gains_copy = links.push(ggs.at[2], rg.at[2], ypeer)
+    for copy in copies:
+        copy.wait()
+
+    @pl.loop(0, 4)
+    def _(k):
+        gq[qa, k, y, x] = (gq[qa, k, y, x].astype(F32) + r2a[k].astype(F32)).astype(BF16)
+        gq[qb_, k, y, x] = (gq[qb_, k, y, x].astype(F32) + r2b[k].astype(F32)).astype(BF16)
+
+    copies = []
+    for k in (2, 3, 1):
+        zz = across(z, k)
+        for p in range(2):
+            copies.append(links.push(gq.at[2 * c + p, zz, y, x], r3.at[p, k - 1], device(zz, y, x, c)))
+    gains_copy.wait()
+    ggs[3] = ggs[2] + rg[2]
+    for k in (2, 3, 1):
+        copies.append(links.push(ggs.at[3], rg.at[2 + k], device(across(z, k), y, x, c)))
+
+    for copy in x_copies:
+        copy.wait()
+    stores = []
+    for a, out in enumerate((gin_out, ghid_out)):
+        lb = loads.start(r2_hbm.at[a], nb)
+        lb.wait()
+        nout[a] = nsum[1, a].astype(F32) + nb[...].astype(F32)
+        stores.append(loads.start(nout.at[a], out))
+
+    for copy in copies:
+        copy.wait()
+    for p in range(2):
+        total = gq[2 * c + p, z, y, x].astype(F32)
+        for k in range(3):
+            total = total + r3[p, k].astype(F32)
+        fin[p] = total
+    last = links.push(fin.at[:, pl.ds(pl.multiple_of((1 - c) * 24, 8), 24)], r4, core)
+    gg_ref[...] = ggs[3] + rg[3] + rg[4] + rg[5]
+    for p in range(2):
+        own_ref[2 * c + p] = fin[p, pl.ds(pl.multiple_of(c * 24, 8), 24), :]
+    last.wait()
+    for p in range(2):
+        own_ref[2 * (1 - c) + p] = r4[p]
+    for copy in stores + y_copies:
+        copy.wait()
+    own_y.wait()
+    store_gt.wait()
+
+
+def tail(returned, scol, tokens_in, cotangent, hidden, qkv, context, stats, w_all, gains, segr, segc, y_rows, gin, ghid):
+    tokens, width = tokens_in.shape
+    slots = returned.shape[0]
+    any_spec = pl.BlockSpec(memory_space=pl.ANY)
+    vmem = pl.BlockSpec(memory_space=pltpu.VMEM)
+    return pl.pallas_call(
+        tail_kernel,
+        out_shape=(
+            jax.ShapeDtypeStruct((tokens, width), F32),
+            jax.ShapeDtypeStruct(y_rows.shape, BF16),
+            jax.ShapeDtypeStruct((2, 2) + gin.shape[1:], BF16),
+            jax.ShapeDtypeStruct((2,) + gin.shape[1:], BF16),
+            jax.ShapeDtypeStruct(gin.shape[1:], F32),
+            jax.ShapeDtypeStruct(ghid.shape[1:], F32),
+            jax.ShapeDtypeStruct((4, 24, width), F32),
+            jax.ShapeDtypeStruct((8, width), F32),
+        ),
+        in_specs=[any_spec] * 10 + [vmem] * 5,
+        out_specs=(any_spec,) * 6 + (vmem,) * 2,
+        scratch_shapes=[
+            pltpu.VMEM((slots, width), BF16),
+            pltpu.VMEM((tokens, width), BF16),
+            pltpu.VMEM((tokens, width), BF16),
+            pltpu.VMEM((tokens, width), F32),
+            pltpu.VMEM((tokens, 3 * width), BF16),
+            pltpu.VMEM((tokens, width), BF16),
+            pltpu.VMEM(w_all.shape, BF16),
+            pltpu.VMEM((tokens, width), F32),
+            pltpu.VMEM((tokens, width), BF16),
+            pltpu.VMEM((tokens, width), BF16),
+            pltpu.VMEM((tokens, 3 * width), BF16),
+            pltpu.VMEM((tokens, width), BF16),
+            pltpu.VMEM((16, tokens), F32),
+            pltpu.VMEM((tokens, 128), F32),
+            pltpu.VMEM((tokens, 128), F32),
+            pltpu.VMEM((4, 4, 2, 2, 48, width), BF16),
+            pltpu.VMEM((2, 4, 2, 2, 48, width), BF16),
+            pltpu.VMEM((4, 2, 48, width), BF16),
+            pltpu.VMEM((4, 2, 48, width), BF16),
+            pltpu.VMEM((4, 48, width), BF16),
+            pltpu.VMEM((4, 48, width), BF16),
+            pltpu.VMEM((2, 3, 48, width), BF16),
+            pltpu.VMEM((2, 48, width), F32),
+            pltpu.VMEM((2, 24, width), F32),
+            pltpu.VMEM((4, 8, width), F32),
+            pltpu.VMEM((6, 8, width), F32),
+            pltpu.VMEM(gin.shape[1:], BF16),
+            pltpu.VMEM(gin.shape[1:], BF16),
+            pltpu.VMEM((2, 2) + gin.shape[1:], BF16),
+            pltpu.VMEM((2,) + gin.shape[1:], F32),
+            pltpu.SemaphoreType.DMA((40,)),
+            pltpu.SemaphoreType.DMA((40,)),
+            pltpu.SemaphoreType.DMA((24,)),
+        ],
+        compiler_params=pltpu.CompilerParams(vmem_limit_bytes=62 << 20, collective_id=2, has_side_effects=True),
+        cost_estimate=pl.CostEstimate(flops=80 << 30, bytes_accessed=40 << 20, transcendentals=0),
+    )(returned, tokens_in, cotangent, hidden, qkv, context, w_all, y_rows, gin, ghid, scol, stats, gains, segr, segc)
+
+
 def local(tokens, segments, routes, gate_logit, w_qkv, w_out, norm_gains, w_in, w_hid, cotangent):
     tok_count, width = tokens.shape
     n_expert = lax.axis_size("expert")
@@ -424,11 +812,43 @@
     da_back = exchange(da_rows)
     hidden_units = activated.shape[1]
     y_rows = dot(activated, w_hid_all.reshape(hidden_units, width)).astype(BF16)
-    y_back = exchange(y_rows)
     grad_hid = t_dot(activated, dy_rows).astype(BF16)
     grad_in = lax.dot_general(
         act_rows, grad_pre.reshape(slot_rows, n_narrow, -1), (((0,), (0,)), ((), ())), preferred_element_type=F32
     ).astype(BF16)
+    if n_expert == 8 and n_narrow == 4:
+        gin = grad_in.transpose(1, 0, 2)
+        ghid = grad_hid.reshape(n_narrow, -1, width)
+        grad_tokens, y_back, _r1, _r2, gin_own, ghid_own, own, gg = tail(
+            da_back,
+            scol,
+            tokens,
+            cotangent,
+            hidden,
+            qkv,
+            context,
+            stats,
+            w_all,
+            gains,
+            segr,
+            segc,
+            y_rows.reshape(n_expert, capacity, width),
+            gin,
+            ghid,
+        )
+        block_out = block_output(y_back.reshape(slot_rows, width), scol, hidden, gate_logit)
+        me = lax.axis_index("expert") * n_narrow + lax.axis_index("narrow")
+        share = width // (n_expert * n_narrow)
+        return (
+            block_out,
+            grad_tokens,
+            own[:3].transpose(1, 0, 2).reshape(share, 3 * width),
+            own[3],
+            lax.dynamic_slice_in_dim(gg[:2], me * share, share, axis=1),
+            gin_own[None],
+            ghid_own[None],
+        )
+    y_back = exchange(y_rows)
     grad_tokens, grad_w, grad_gains = attend_bwd(
         da_back, scol, tokens, cotangent, hidden, qkv, context, stats, w_all, gains, segr, segc
     )

time: 679 us -> 527 us (0.78)
  waiting for transfers between devices: 384 us -> 189 us
  Pallas kernels: 173 us -> 229 us
  other arithmetic: 16.6 us -> 2.55 us
  local copies, waits for them, and re-layouts: 15.6 us -> 22.7 us
    unnamed x7 -> x3, waiting for transfers between devices: 176 us -> 1.39 us
    pallas_call x1, Pallas kernels: 54.2 us -> 109 us  [tail(): pl.pallas_call(tail_kernel, out_shape=(jax.ShapeDtypeStruct((tokens, widt...]
    all_gather x1, waiting for transfers between devices: 22.2 us -> 0.01 us  [local(): w_hid_all = lax.all_gather(w_hid[0], 'narrow', axis=0, tiled=False)]
    all_gather x1, waiting for transfers between devices: 0.02 us -> 21.1 us  [local(): w_in_all = lax.all_gather(w_in[0], 'narrow', axis=0, tiled=False)]
    all_to_all x4 -> x3, waiting for transfers between devices: 95.4 us -> 76.4 us  [exchange(): lax.all_to_all(values.reshape(n_expert, capacity, width), 'expert', split...]
    concatenate x1 -> x0, other arithmetic: 8.25 us -> none  [local(): jnp.concatenate((grad_w, jnp.pad(grad_gains[:2].T, ((0, 0), (0, 126)))),...]
    unnamed x17 -> x33, local copies, waits for them, and re-layouts: 8.14 us -> 16.3 us
    all_to_all x4 -> x3, starting transfers between devices: 20.3 us -> 16.9 us  [exchange(): lax.all_to_all(values.reshape(n_expert, capacity, width), 'expert', split...]
  transfers between devices with their start and end apart: 10 -> 6, of which waited for: 6 -> 4; matrix products, arithmetic and copies ran while one was open for 8% -> 10% of each run, Pallas kernels for 17% -> 11%
where the time goes in v2:
time: 527 us; the launch traced here: 518 us
  Pallas kernels  229 us (43%)
  waiting for transfers between devices  189 us (36%)
  matrix products  44.2 us (8%)
  local copies, waits for them, and re-layouts  22.7 us (4%)
  starting transfers between devices  17 us (3%)
  between operations  14.3 us (3%)
    pallas_call x1, Pallas kernels, tail(): pl.pallas_call(tail_kernel, out_shape=(jax.ShapeDtypeStruct((tokens, widt...  109 us
    all_gather x1, waiting for transfers between devices, local(): lax.all_gather(jnp.concatenate((w_qkv, w_out, gain_cols), axis=1), everyo...  90 us
    all_to_all x3, waiting for transfers between devices, exchange(): lax.all_to_all(values.reshape(n_expert, capacity, width), 'expert', split...  76.4 us
    pallas_call x1, Pallas kernels, experts(): pl.pallas_call(expert_kernel, grid=(rows // BLOCK,), out_shape=(jax.Shape...  57 us
    pallas_call x1, Pallas kernels, attend_fwd(): pl.pallas_call(fwd_kernel, out_shape=(jax.ShapeDtypeStruct((tokens, 3 * w...  48.2 us
    all_gather x1, waiting for transfers between devices, local(): w_in_all = lax.all_gather(w_in[0], 'narrow', axis=0, tiled=False)  21.1 us
    all_to_all x3, starting transfers between devices, exchange(): lax.all_to_all(values.reshape(n_expert, capacity, width), 'expert', split...  16.9 us
    unnamed x33, local copies, waits for them, and re-layouts  16.3 us
  transfers between devices with their start and end apart: 6, of which 4 were waited for; matrix products, arithmetic and copies ran while one was open for 10% of the time, Pallas kernels for 11%

profile of v2, /device:TPU:0, one launch (start us, length us, event | category | flops | bytes accessed | tf_op | source)
XLA Modules:
  0.0 518.4 jit_solution(6516369950048331401)
XLA Ops:
  7.2 0.7 copy.34
  8.0 1.6 fusion.6
  10.3 1.7 copy.37.gate_ref
  12.0 1.7 copy.36.rcol_ref
  13.7 9.2 %shard_map.153 = (f32[8,1024]{1,0:T(8,128)}, f32[1024,1]{1,0:T(8,128)}, bf16[2048,768]{1,0:T(8,128)(2,1)}) custom-call(s32[1,1024]{1,0:T(1,128)} %bitcast.51, s32[1024,1]{1,0:T(8,128)} %copy.36.rcol_ref, f32[1024,1]{1,0:T(8,128)} %copy.37.gate_ref, bf16[1024,768]{1,0:T(8,128)(2,1)} %ct_hbm.1), custom_call_target="tpu_custom_call" | custom-call | flops 8589934592 | bytes 8388608 | tf_op jit(solution)/shard_map/pallas_call | solution.py:107
  22.9 7.5 %all-to-all-start.1 = ((bf16[8,256,768]{2,1,0:T(8,128)(2,1)}), bf16[8,256,768]{2,1,0:T(8,128)(2,1)S(1)}, u32[]{:S(2)}, u32[]{:S(2)}) async-start(bf16[8,256,768]{2,1,0:T(8,128)(2,1)} %bitcast.42), calls=%async_computation.1 | async-start | bytes 6291456 | tf_op jit(solution)/shard_map/all_to_all | solution.py:801
  31.2 1.0 copy.38.segc_ref
  32.2 90.0 %all-gather.4.cloned.1.call-done.w_ref.w_hbm = bf16[768,3200]{1,0:T(8,128)(2,1)} async-done(((bf16[24,3200]{1,0:T(8,128)(2,1)}), bf16[768,3200]{1,0:T(8,128)(2,1)}) %all-gather.4.cloned.1.call-update) | async-done | bytes 4915216 | tf_op jit(solution)/shard_map/all_gather | solution.py:793
  122.2 1.0 slice_convert_fusion
  123.2 0.7 copy.46
  123.9 48.2 %shard_map.154 = (bf16[1024,2304]{1,0:T(8,128)(2,1)}, bf16[1024,768]{1,0:T(8,128)(2,1)}, f32[128,1024]{1,0:T(8,128)}, f32[1024,768]{1,0:T(8,128)}, bf16[2048,768]{1,0:T(8,128)(2,1)}) custom-call(bf16[1024,768]{1,0:T(8,128)(2,1)} %x_hbm.1, bf16[768,3200]{1,0:T(8,128)(2,1)} %all-gather.4.cloned.1.call-done.w_ref.w_hbm, f32[2,768]{1,0:T(2,128)} %bitcast.48, ...), custom_call_target="tpu_custom_call" | custom-call | flops 42949672960 | bytes 25165824 | tf_op jit(solution)/shard_map/pallas_call | solution.py:181
  172.1 1.7 copy-done.4
  173.7 4.5 all-to-all-start
  178.3 21.1 %all-gather.6.cloned.1.call-done.win_ref = bf16[4,768,768]{2,1,0:T(8,128)(2,1)} async-done(((bf16[1,768,768]{2,1,0:T(8,128)(2,1)}), bf16[4,768,768]{2,1,0:T(8,128)(2,1)}) %all-gather.6.cloned.1.call-update) | async-done | bytes 4718608 | tf_op jit(solution)/shard_map/all_gather | solution.py:797
  199.4 50.2 %all-to-all-done = bf16[8,256,768]{2,1,0:T(8,128)(2,1)} async-done(((bf16[8,256,768]{2,1,0:T(8,128)(2,1)}), bf16[8,256,768]{2,1,0:T(8,128)(2,1)}, u32[]{:S(2)}, u32[]{:S(2)}) %all-to-all-start) | async-done | bytes 3145760 | tf_op jit(solution)/shard_map/all_to_all | solution.py:801
  249.7 57.0 %shard_map.155 = (bf16[2048,3072]{1,0:T(8,128)(2,1)}, bf16[2048,3072]{1,0:T(8,128)(2,1)}, bf16[2048,768]{1,0:T(8,128)(2,1)}) custom-call(bf16[2048,768]{1,0:T(8,128)(2,1)} %bitcast.6.a_ref, bf16[2048,768]{1,0:T(8,128)(2,1)} %bitcast.39, bf16[4,768,768]{2,1,0:T(8,128)(2,1)} %all-gather.6.cloned.1.call-done.win_ref, ...), custom_call_target="tpu_custom_call" | custom-call | flops 64424509440 | bytes 41943040 | tf_op jit(solution)/shard_map/pallas_call | solution.py:227
  306.6 4.9 all-to-all-start.2
  311.6 14.6 %convolution_convert_fusion = bf16[3072,768]{1,0:T(8,128)(2,1)} fusion(bf16[2048,3072]{1,0:T(8,128)(2,1)} %get-tuple-element.31, bf16[2048,768]{1,0:T(8,128)(2,1)S(1)} %bitcast.40), kind=kOutput, calls=%fused_computation.3 | convolution fusion | flops 9666035712 | bytes 20447232 | tf_op jit(solution)/shard_map/dot_general | solution.py:41
  326.2 15.5 %convolution_convert_fusion.1 = bf16[2048,768]{1,0:T(8,128)(2,1)} fusion(bf16[2048,3072]{1,0:T(8,128)(2,1)} %get-tuple-element.31, bf16[3072,768]{1,0:T(8,128)(2,1)} %bitcast.53), kind=kOutput, calls=%fused_computation.5 | convolution fusion | flops 9665249280 | bytes 20447232 | tf_op jit(solution)/shard_map/dot_general | solution.py:33
  341.7 14.1 %convert_bitcast_fusion.gin_hbm = bf16[4,768,768]{2,1,0:T(8,128)(2,1)} fusion(bf16[2048,768,1]{1,0,2:T(8,128)(2,1)} %bitcast.13, bf16[256,4,8,768]{3,2,1,0:T(8,128)(2,1)S(1)} %bitcast.56), kind=kOutput, calls=%fused_computation.4 | convolution fusion | flops 9666035712 | bytes 20447232 | tf_op jit(solution)/shard_map/dot_general | solution.py:816
  355.8 26.2 %all-to-all-done.2 = bf16[8,256,768]{2,1,0:T(8,128)(2,1)} async-done(((bf16[8,256,768]{2,1,0:T(8,128)(2,1)}), bf16[8,256,768]{2,1,0:T(8,128)(2,1)}, u32[]{:S(2)}, u32[]{:S(2)}) %all-to-all-start.2) | async-done | bytes 3145760 | tf_op jit(solution)/shard_map/all_to_all | solution.py:801
  382.0 109.4 %shard_map.156 = (f32[1024,768]{1,0:T(8,128)}, bf16[8,256,768]{2,1,0:T(8,128)(2,1)}, bf16[2,2,768,768]{3,2,1,0:T(8,128)(2,1)}, bf16[2,768,768]{2,1,0:T(8,128)(2,...) custom-call(bf16[2048,768]{1,0:T(8,128)(2,1)} %bitcast.10.ret_hbm, ...), custom_call_target="tpu_custom_call" | custom-call | flops 85899345920 | bytes 41943040 | tf_op jit(solution)/shard_map/pallas_call | solution.py:730
  491.4 1.0 slice_bitcast_fusion
  492.3 1.5 slice_bitcast_fusion.1
  493.8 1.9 copy-done.1
  495.7 1.9 copy-done.2
  497.6 5.0 shard_map.157
  504.7 1.7 copy.56
  506.4 1.1 copy-done.8
  507.5 1.4 copy.57
  508.9 1.1 copy-done.7
  510.0 1.4 copy.58
  (33 shorter events, 3.6 us)
Async XLA Ops:
  7.2 115.0 %all-gather.4.cloned.1.call-start = ((), (), s32[]{:S(2)}) async-start(), calls=%async_computation.3 | async-start | bytes 5068800 | tf_op jit(solution)/shard_map/all_gather | solution.py:793
  9.6 168.7 %all-gather.8.cloned.1.call-start = ((), (), s32[]{:S(2)}) async-start(), calls=%async_computation.5 | async-start | bytes 5898240 | tf_op jit(solution)/shard_map/all_gather | solution.py:798
  22.9 8.2 %copy-start.9 = (s32[1,1024]{1,0:T(1,128)S(1)}, s32[1,1024]{1,0:T(1,128)}, u32[]{:S(2)}) copy-start(s32[1,1024]{1,0:T(1,128)} %segr_ref.3) | copy-start | bytes 12292
  22.9 149.1 %all-to-all-start.1 = ((bf16[8,256,768]{2,1,0:T(8,128)(2,1)}), bf16[8,256,768]{2,1,0:T(8,128)(2,1)S(1)}, u32[]{:S(2)}, u32[]{:S(2)}) async-start(bf16[8,256,768]{2,1,0:T(8,128)(2,1)} %bitcast.42), calls=%async_computation.1 | async-start | bytes 6291456 | tf_op jit(solution)/shard_map/all_to_all | solution.py:801
  30.4 169.0 %all-gather.6.cloned.1.call-start = ((), (), s32[]{:S(2)}) async-start(), calls=%async_computation.4 | async-start | bytes 5898240 | tf_op jit(solution)/shard_map/all_gather | solution.py:797
  172.1 1.7 copy-start.4
  173.7 75.9 %all-to-all-start = ((bf16[8,256,768]{2,1,0:T(8,128)(2,1)}), bf16[8,256,768]{2,1,0:T(8,128)(2,1)}, u32[]{:S(2)}, u32[]{:S(2)}) async-start(bf16[8,256,768]{2,1,0:T(8,128)(2,1)} %bitcast.41), calls=%async_computation | async-start | bytes 6291456 | tf_op jit(solution)/shard_map/all_to_all | solution.py:801
  306.6 4.9 copy-start.5
  306.6 75.4 %all-to-all-start.2 = ((bf16[8,256,768]{2,1,0:T(8,128)(2,1)}), bf16[8,256,768]{2,1,0:T(8,128)(2,1)}, u32[]{:S(2)}, u32[]{:S(2)}) async-start(bf16[8,256,768]{2,1,0:T(8,128)(2,1)} %bitcast.43), calls=%async_computation.2 | async-start | bytes 6291456 | tf_op jit(solution)/shard_map/all_to_all | solution.py:801
  311.5 30.2 %slice-start = ((s8[12582912]{0:T(1024)(128)(4,1)}), s8[4194304]{0:T(1024)(128)(4,1)S(1)}, s32[]{:S(2)}) async-start(s8[12582912]{0:T(1024)(128)(4,1)} %bitcast.54), calls=%async_computation.6 | async-start | bytes 8388608
  311.5 30.1 %slice-start.1 = ((s8[12582912]{0:T(1024)(128)(4,1)}), s8[4194304]{0:T(1024)(128)(4,1)S(1)}, s32[]{:S(2)}) async-start(s8[12582912]{0:T(1024)(128)(4,1)} %bitcast.54), calls=%async_computation.7 | async-start | bytes 8388608
  326.2 15.5 %slice-start.2 = ((s8[12582912]{0:T(1024)(128)(4,1)}), s8[4194304]{0:T(1024)(128)(4,1)S(1)}, s32[]{:S(2)}) async-start(s8[12582912]{0:T(1024)(128)(4,1)} %bitcast.54), calls=%async_computation.8 | async-start | bytes 8388608
  382.0 111.9 %copy-start = (f32[1024,1]{1,0:T(8,128)S(1)}, f32[1024,1]{1,0:T(8,128)}, u32[]{:S(2)}) copy-start(f32[1024,1]{1,0:T(8,128)} %copy.37.gate_ref) | copy-start | bytes 12292
  382.0 111.9 %copy-start.3 = (f32[1024,1]{1,0:T(8,128)S(1)}, f32[1024,1]{1,0:T(8,128)}, u32[]{:S(2)}) copy-start(f32[1024,1]{1,0:T(8,128)} %get-tuple-element.33.scol_ref) | copy-start | bytes 12292
  493.8 1.9 copy-start.1
  495.7 1.9 copy-start.2
  497.6 7.1 %copy-start.6 = (f32[1024,768]{1,0:T(8,128)S(1)}, f32[1024,768]{1,0:T(8,128)}, u32[]{:S(2)}) copy-start(f32[1024,768]{1,0:T(8,128)} %get-tuple-element.49) | copy-start | bytes 9437188
  504.7 2.8 copy-start.8
  507.5 2.5 copy-start.7
Sparse Core Ops, SparseCore 0:
  11.5 110.6 all-gather.3
  123.8 36.5 all-gather.7
  161.9 37.4 all-gather.5

commit v3 on v2

--- a/solution.py
+++ b/solution.py
@@ -447,11 +447,286 @@
     pl.semaphore_wait(barrier, len(peers))
 
 
-FLIPS = (6, 7, 4, 5, 2, 3, 1)
+FLIPS = (1, 2, 3, 4, 5, 6, 7)
 
 
 def peers_of(z, y, x, c):
     return [device(across(z, k >> 1), 1 - y if k & 1 else y, x, c) for k in FLIPS]
+
+
+def weight(blocks, first, count):
+    half = blocks.shape[-1]
+    rows = blocks.shape[1] * blocks.shape[2] * blocks.shape[3] * blocks.shape[4]
+    return jnp.concatenate([blocks[b].reshape(rows, half) for b in range(first, first + count)], axis=1)
+
+
+def head_kernel(
+    capacity,
+    experts,
+    x_hbm,
+    ct_hbm,
+    shard_hbm,
+    win_hbm,
+    whid_hbm,
+    rrow_ref,
+    rcol_ref,
+    gate_ref,
+    segr_ref,
+    segc_ref,
+    qkv_hbm,
+    c_hbm,
+    h_hbm,
+    act_hbm,
+    w_hbm,
+    dyrow_hbm,
+    win4_hbm,
+    whid4_hbm,
+    stat_ref,
+    scol_ref,
+    gain_ref,
+    x_ref,
+    ct_ref,
+    st,
+    wq,
+    wg,
+    qkv_ref,
+    c_ref,
+    h_ref,
+    a_scr,
+    act_ref,
+    dy_ref,
+    bias_scr,
+    col_scr,
+    send_sems,
+    recv_sems,
+    load_sems,
+):
+    z, y, x, c = place()
+    me_e = z * 2 + y
+    me_n = x * 2 + c
+    tokens, width = x_ref.shape
+    blocks = tokens // BLOCK
+    pairs = width // 128
+    half = width // 2
+    core, xpeer, ypeer = device(z, y, x, 1 - c), device(z, y, 1 - x, c), device(z, 1 - y, x, c)
+    links = Links(send_sems, recv_sems)
+    loads = Loads(load_sems)
+    loading_ct = loads.start(ct_hbm, ct_ref)
+    loading_x = loads.start(x_hbm, x_ref)
+    own_shard = loads.start(shard_hbm.at[c], st.at[c])
+    own_in = loads.start(win_hbm, win4_hbm.at[me_n])
+    own_hid = loads.start(whid_hbm, whid4_hbm.at[me_n])
+
+    greet(peers_of(z, y, x, c) + [core, xpeer])
+    zero = links.push(shard_hbm.at[1 - c], st.at[c], core)
+
+    wide = max(8, experts)
+    hot = (iota((wide, tokens), 0) == rrow_ref[...]).astype(F32)
+    before = (iota((tokens, tokens), 0) < iota((tokens, tokens), 1)).astype(BF16)
+    rank = dot(hot.astype(BF16), before)
+    base = (iota((wide, tokens), 0) * capacity).astype(F32)
+    srow = jnp.sum(hot * (rank + base), axis=0, keepdims=True)
+
+    zero.wait()
+    own_shard.wait()
+    rows48 = jnp.concatenate((st[0], st[1]), axis=0)
+    for j in range(4):
+        wq[2 * j + c, z, y, x] = rows48[:, j * half : (j + 1) * half].astype(BF16)
+    wg[z, y, x] = rows48[:, 4 * half :].astype(BF16)
+    ring_z = []
+    for piece in range(2):
+        group = []
+        for k in (1, 2, 3):
+            to = device(across(z, k), y, x, c)
+            for j in (2 * piece, 2 * piece + 1):
+                part = wq.at[2 * j + c, z, y, x]
+                group.append(links.push(part, part, to))
+            if piece == 0:
+                group.append(links.push(wg.at[z, y, x], wg.at[z, y, x], to))
+        ring_z.append(group)
+
+    hot_c = (iota((tokens, 128), 1) == rcol_ref[...]).astype(F32)
+    after = (iota((tokens, tokens), 1) < iota((tokens, tokens), 0)).astype(BF16)
+    rank_c = dot(after, hot_c.astype(BF16))
+    base_c = (iota((tokens, 128), 1) * capacity).astype(F32)
+    scol_ref[...] = jnp.sum(hot_c * (rank_c + base_c), axis=1, keepdims=True)
+
+    def fill(values, out):
+        @pl.loop(0, out.shape[0])
+        def _(i):
+            ids = (iota((capacity, tokens), 0) + i * capacity).astype(F32)
+            out[i] = dot((ids == srow).astype(BF16), values).astype(BF16)
+
+    loading_ct.wait()
+    fill((jax.nn.sigmoid(gate_ref[...]) * ct_ref[...].astype(F32)).astype(BF16), dy_ref)
+
+    ring_2 = []
+    for piece in range(2):
+        for copy in ring_z[piece]:
+            copy.wait()
+        ja, jb = 2 * (2 * piece) + c, 2 * (2 * piece + 1) + c
+        group = [
+            links.push(wq.at[ja, :, y, x], wq.at[ja, :, y, x], ypeer),
+            links.push(wq.at[jb, :, y, x], wq.at[jb, :, y, x], xpeer),
+        ]
+        if piece == 0:
+            group.append(links.push(wg.at[:, y, x], wg.at[:, y, x], ypeer))
+        ring_2.append(group)
+    dy_copies = []
+    for k in FLIPS:
+        zz, yy = across(z, k >> 1), (1 - y if k & 1 else y)
+        dy_copies.append(links.push(dy_ref.at[zz * 2 + yy], dyrow_hbm.at[me_e], device(zz, yy, x, c)))
+    own_dy = loads.start(dy_ref.at[me_e], dyrow_hbm.at[me_e])
+    ring_3 = []
+    for piece in range(2):
+        for copy in ring_2[piece]:
+            copy.wait()
+        ja, jb = 2 * (2 * piece) + c, 2 * (2 * piece + 1) + c
+        group = [
+            links.push(wq.at[ja, :, :, x], wq.at[ja, :, :, x], xpeer),
+            links.push(wq.at[jb, :, y], wq.at[jb, :, y], ypeer),
+        ]
+        if piece == 0:
+            group.append(links.push(wg.at[:, :, x], wg.at[:, :, x], xpeer))
+        ring_3.append(group)
+    ring_4 = []
+    for piece in range(2):
+        for copy in ring_3[piece]:
+            copy.wait()
+        ring_4.append([links.push(wq.at[2 * j + c], wq.at[2 * j + c], core) for j in (2 * piece, 2 * piece + 1)])
+
+    slices = []
+    for src, dst in ((win_hbm, win4_hbm), (whid_hbm, whid4_hbm)):
+        slices.append((links.push(src, dst.at[me_n], xpeer), dst))
+    core_slices = [links.push(src, dst.at[me_n], core) for src, dst in ((win_hbm, win4_hbm), (whid_hbm, whid4_hbm))]
+
+    gains = jnp.transpose(wg[...].reshape(width, 128).astype(F32))[0:8, :]
+    gain_ref[...] = gains
+    gain_one = gains[0:1, :]
+    gain_two = gains[1:2, :]
+    loading_x.wait()
+    for piece in range(2):
+        for copy in ring_4[piece]:
+            copy.wait()
+    storing = [loads.start(wq, w_hbm)]
+
+    @pl.loop(0, blocks)
+    def _(i):
+        rows = pl.ds(pl.multiple_of(i * BLOCK, BLOCK), BLOCK)
+        normed, _f = normalize(x_ref[rows, :].astype(F32))
+        act = (normed * gain_one).astype(BF16)
+        qkv_ref[rows, :] = dot(act, weight(wq, 0, 6)).astype(BF16)
+
+    storing.append(loads.start(qkv_ref, qkv_hbm))
+    col_scr[...] = jnp.zeros_like(col_scr)
+    low = iota((BLOCK, 128), 1) < HEAD_DIM
+    for qb in range(blocks):
+        kb = max(0, qb - LOOKBACK)
+        span = (qb - kb + 1) * BLOCK
+        rows = pl.ds(qb * BLOCK, BLOCK)
+        keys = pl.ds(kb * BLOCK, span)
+        q_pos = iota((BLOCK, span), 0) + qb * BLOCK
+        k_pos = iota((BLOCK, span), 1) + kb * BLOCK
+        ok = (k_pos <= q_pos) & (segc_ref[rows, :] == segr_ref[0:1, keys])
+        bias_scr[:, :span] = jnp.where(ok, 0.0, BIG_NEGATIVE)
+
+        @pl.loop(0, pairs)
+        def _(hp):
+            at = pl.multiple_of(hp * 128, 128)
+            q = qkv_ref[rows, pl.ds(at, 128)] * jnp.asarray(HEAD_DIM**-0.5, BF16)
+            k = qkv_ref[keys, pl.ds(width + at, 128)]
+            v = qkv_ref[keys, pl.ds(2 * width + at, 128)]
+            outs = []
+            col = col_scr[rows, :]
+            for side in range(2):
+                mine = low if side == 0 else ~low
+                s = dot_t(jnp.where(mine, q, 0), k) + bias_scr[:, :span]
+                top = jnp.max(s, axis=1, keepdims=True)
+                raised = jnp.exp(s - top)
+                total = jnp.sum(raised, axis=1, keepdims=True)
+                outs.append(dot((raised * (1.0 / total)).astype(BF16), v))
+                col = jnp.where(iota((BLOCK, 128), 1) == 2 * hp + side, top + jnp.log(total), col)
+            col_scr[rows, :] = col
+            c_ref[rows, pl.ds(at, 128)] = jnp.where(low, outs[0], outs[1]).astype(BF16)
+
+        if qb == 0:
+            for copy, dst in slices:
+                copy.wait()
+                core_slices.append(links.push(dst.at[(1 - x) * 2 + c], dst.at[(1 - x) * 2 + c], core))
+
+    storing.append(loads.start(c_ref, c_hbm))
+    stat_ref[...] = col_scr[...].T
+
+    @pl.loop(0, blocks)
+    def _(i):
+        rows = pl.ds(pl.multiple_of(i * BLOCK, BLOCK), BLOCK)
+        hidden = x_ref[rows, :].astype(F32) + dot(c_ref[rows, :], weight(wq, 6, 2))
+        h_ref[rows, :] = hidden
+        normed, _f = normalize(hidden)
+        a_scr[rows, :] = (normed * gain_two).astype(BF16)
+
+    storing.append(loads.start(h_ref, h_hbm))
+    fill(a_scr[...], act_ref)
+    storing.append(loads.start(act_ref, act_hbm))
+    for copy in storing + [own_in, own_hid, own_dy] + core_slices + dy_copies:
+        copy.wait()
+
+
+def head(tokens_in, cotangent, shard, w_in, w_hid, routes, gate_logit, segr, segc, experts, capacity):
+    tokens, width = tokens_in.shape
+    any_spec = pl.BlockSpec(memory_space=pl.ANY)
+    vmem = pl.BlockSpec(memory_space=pltpu.VMEM)
+    slots = (experts, capacity, width)
+    blocks = (8, 4, 2, 2, 48, width // 2)
+    return pl.pallas_call(
+        functools.partial(head_kernel, capacity, experts),
+        out_shape=(
+            jax.ShapeDtypeStruct((tokens, 3 * width), BF16),
+            jax.ShapeDtypeStruct((tokens, width), BF16),
+            jax.ShapeDtypeStruct((tokens, width), F32),
+            jax.ShapeDtypeStruct(slots, BF16),
+            jax.ShapeDtypeStruct(blocks, BF16),
+            jax.ShapeDtypeStruct(slots, BF16),
+            jax.ShapeDtypeStruct((4,) + w_in.shape, BF16),
+            jax.ShapeDtypeStruct((4,) + w_hid.shape, BF16),
+            jax.ShapeDtypeStruct((128, tokens), F32),
+            jax.ShapeDtypeStruct((tokens, 1), F32),
+            jax.ShapeDtypeStruct((8, width), F32),
+        ),
+        in_specs=[any_spec] * 5 + [vmem] * 5,
+        out_specs=(any_spec,) * 8 + (vmem,) * 3,
+        scratch_shapes=[
+            pltpu.VMEM((tokens, width), BF16),
+            pltpu.VMEM((tokens, width), BF16),
+            pltpu.VMEM(shard.shape, F32),
+            pltpu.VMEM(blocks, BF16),
+            pltpu.VMEM((4, 2, 2, 48, 128), BF16),
+            pltpu.VMEM((tokens, 3 * width), BF16),
+            pltpu.VMEM((tokens, width), BF16),
+            pltpu.VMEM((tokens, width), F32),
+            pltpu.VMEM((tokens, width), BF16),
+            pltpu.VMEM(slots, BF16),
+            pltpu.VMEM(slots, BF16),
+            pltpu.VMEM((BLOCK, (LOOKBACK + 1) * BLOCK), F32),
+            pltpu.VMEM((tokens, 128), F32),
+            pltpu.SemaphoreType.DMA((48,)),
+            pltpu.SemaphoreType.DMA((48,)),
+            pltpu.SemaphoreType.DMA((16,)),
+        ],
+        compiler_params=pltpu.CompilerParams(vmem_limit_bytes=62 << 20, collective_id=0, has_side_effects=True),
+        cost_estimate=pl.CostEstimate(flops=60 << 30, bytes_accessed=40 << 20, transcendentals=0),
+    )(
+        tokens_in,
+        cotangent,
+        shard,
+        w_in,
+        w_hid,
+        routes.reshape(1, tokens),
+        routes,
+        gate_logit.reshape(tokens, 1),
+        segr,
+        segc,
+    )
 
 
 def tail_kernel(
@@ -556,7 +831,7 @@
         gt_ref[rows, :] = dh
         dhb = dh.astype(BF16)
         dhb_scr[rows, :] = dhb
-        dc = dot_t(dhb, w_ref[:, 3 * width : 4 * width]).astype(BF16)
+        dc = dot_t(dhb, weight(w_ref, 6, 2)).astype(BF16)
         dc_scr[rows, :] = dc
         d_scr[:, rows] = lax.dot_general(
             member,
@@ -637,7 +912,7 @@
     def _(i):
         rows = pl.ds(pl.multiple_of(i * BLOCK, BLOCK), BLOCK)
         normed, factor = normalize(x_ref[rows, :].astype(F32))
-        dn = dot_t(dqkv_scr[rows, :], w_ref[:, : 3 * width])
+        dn = dot_t(dqkv_scr[rows, :], weight(w_ref, 0, 6))
         ggs[0, 0:1, :] += jnp.sum(dn * normed, axis=0, keepdims=True)
         gt_ref[rows, :] += norm_back(dn * gain_one, normed, factor)
 
@@ -781,6 +1056,193 @@
     )(returned, tokens_in, cotangent, hidden, qkv, context, w_all, y_rows, gin, ghid, scol, stats, gains, segr, segc)
 
 
+def flipped(z, y, k):
+    hi, lo = z // 2, lax.rem(z, 2)
+    zz = lax.rem(hi + k // 4, 2) * 2 + lax.rem(lo + lax.rem(k // 2, 2), 2)
+    return zz, lax.rem(y + lax.rem(k, 2), 2)
+
+
+def swap_kernel(
+    act_hbm,
+    dy_hbm,
+    win_hbm,
+    whid_hbm,
+    ret_hbm,
+    y_hbm,
+    gin_hbm,
+    ghid_hbm,
+    a_ref,
+    dy_ref,
+    win_ref,
+    whid_ref,
+    g_ref,
+    du_ref,
+    da_ref,
+    us,
+    gs,
+    stage,
+    send_sems,
+    recv_sems,
+    load_sems,
+):
+    z, y, x, c = place()
+    me = z * 2 + y
+    count, cap, width = a_ref.shape
+    parts = win_ref.shape[0]
+    wide = win_ref.shape[2]
+    loads = Loads(load_sems)
+    first = [
+        loads.start(a, b)
+        for a, b in (
+            (act_hbm.at[me], a_ref.at[me]),
+            (win_hbm, win_ref),
+            (whid_hbm, whid_ref),
+            (dy_hbm, dy_ref),
+        )
+    ]
+
+    def partner(k):
+        zz, yy = flipped(z, y, k)
+        return zz * 2 + yy, device(zz, yy, x, c)
+
+    def outward(k):
+        e, to = partner(k)
+        return pltpu.make_async_remote_copy(
+            src_ref=act_hbm.at[e],
+            dst_ref=a_ref.at[me],
+            send_sem=send_sems.at[k],
+            recv_sem=recv_sems.at[k],
+            device_id=to,
+            device_id_type=MESH,
+        )
+
+    def homeward(k):
+        e, to = partner(k)
+        return pltpu.make_async_remote_copy(
+            src_ref=da_ref.at[e],
+            dst_ref=ret_hbm.at[me],
+            send_sem=send_sems.at[8 + k],
+            recv_sem=recv_sems.at[8 + k],
+            device_id=to,
+            device_id_type=MESH,
+        )
+
+    greet([partner(k)[1] for k in range(1, 8)])
+    for k in FLIPS:
+        outward(k).start()
+    for copy in first:
+        copy.wait()
+
+    @pl.loop(0, count)
+    def _(k):
+        @pl.when(k > 0)
+        def _():
+            outward(k).wait_recv()
+
+        e, _to = partner(k)
+        a = a_ref[e]
+        dy = dy_ref[e]
+        rows = pl.ds(pl.multiple_of(e * cap, cap), cap)
+
+        def enter(j):
+            us[j % 2] = dot(a, win_ref[j])
+            gs[j % 2] = dot_t(dy, whid_ref[j])
+
+        def bend(j):
+            g, slope = gelu_pair(us[j % 2])
+            g_ref[rows, j * wide : (j + 1) * wide] = g.astype(BF16)
+            du_ref[rows, j * wide : (j + 1) * wide] = (gs[j % 2] * slope).astype(BF16)
+
+        def leave(j):
+            return dot_t(du_ref[rows, j * wide : (j + 1) * wide], win_ref[j])
+
+        enter(0)
+        total = None
+        for j in range(parts):
+            if j + 1 < parts:
+                enter(j + 1)
+            bend(j)
+            if j > 0:
+                term = leave(j - 1)
+                total = term if total is None else total + term
+        da_ref[e] = (total + leave(parts - 1)).astype(BF16)
+
+        @pl.when(k > 0)
+        def _():
+            homeward(k).start()
+
+    own = loads.start(da_ref.at[me], ret_hbm.at[me])
+
+    def put(i, out):
+        return pltpu.make_async_copy(stage.at[lax.rem(i, 2)], out, load_sems.at[8 + lax.rem(i, 2)])
+
+    acts = a_ref[...].reshape(count * cap, width)
+    dys = dy_ref[...].reshape(count * cap, width)
+
+    @pl.loop(0, parts)
+    def _(j):
+        cols = pl.ds(pl.multiple_of(j * wide, wide), wide)
+
+        @pl.when(j >= 1)
+        def _():
+            put(0, gin_hbm.at[j - 1]).wait()
+            put(1, ghid_hbm.at[j - 1]).wait()
+
+        stage[0] = t_dot(acts, du_ref[:, cols]).astype(BF16)
+        put(0, gin_hbm.at[j]).start()
+        stage[1] = t_dot(g_ref[:, cols], dys).astype(BF16)
+        put(1, ghid_hbm.at[j]).start()
+
+    @pl.loop(0, count)
+    def _(i):
+        rows = pl.ds(pl.multiple_of(i * cap, cap), cap)
+        a_ref[i] = dot(g_ref[rows, :], whid_ref[...].reshape(parts * wide, width)).astype(BF16)
+
+    out = loads.start(a_ref, y_hbm)
+    put(0, gin_hbm.at[parts - 1]).wait()
+    put(1, ghid_hbm.at[parts - 1]).wait()
+    for k in range(1, 8):
+        outward(k).wait_send()
+        homeward(k).wait()
+    own.wait()
+    out.wait()
+
+
+def swap(act_slots, dy_rows, w_in, w_hid):
+    count, cap, width = act_slots.shape
+    parts, _, wide = w_in.shape
+    hidden = parts * wide
+    any_spec = pl.BlockSpec(memory_space=pl.ANY)
+    return pl.pallas_call(
+        swap_kernel,
+        out_shape=(
+            jax.ShapeDtypeStruct((count, cap, width), BF16),
+            jax.ShapeDtypeStruct((count, cap, width), BF16),
+            jax.ShapeDtypeStruct((parts, width, wide), BF16),
+            jax.ShapeDtypeStruct((parts, wide, width), BF16),
+        ),
+        in_specs=[any_spec] * 4,
+        out_specs=(any_spec,) * 4,
+        scratch_shapes=[
+            pltpu.VMEM((count, cap, width), BF16),
+            pltpu.VMEM((count, cap, width), BF16),
+            pltpu.VMEM(w_in.shape, BF16),
+            pltpu.VMEM(w_hid.shape, BF16),
+            pltpu.VMEM((count * cap, hidden), BF16),
+            pltpu.VMEM((count * cap, hidden), BF16),
+            pltpu.VMEM((count, cap, width), BF16),
+            pltpu.VMEM((2, cap, wide), F32),
+            pltpu.VMEM((2, cap, wide), F32),
+            pltpu.VMEM((2, width, wide), BF16),
+            pltpu.SemaphoreType.DMA((16,)),
+            pltpu.SemaphoreType.DMA((16,)),
+            pltpu.SemaphoreType.DMA((10,)),
+        ],
+        compiler_params=pltpu.CompilerParams(vmem_limit_bytes=62 << 20, collective_id=1, has_side_effects=True),
+        cost_estimate=pl.CostEstimate(flops=100 << 30, bytes_accessed=60 << 20, transcendentals=0),
+    )(act_slots, dy_rows, w_in, w_hid)
+
+
 def local(tokens, segments, routes, gate_logit, w_qkv, w_out, norm_gains, w_in, w_hid, cotangent):
     tok_count, width = tokens.shape
     n_expert = lax.axis_size("expert")
@@ -789,6 +1251,46 @@
     slot_rows = n_expert * capacity
     everyone = ("expert", "narrow")
 
+    if n_expert == 8 and n_narrow == 4:
+        share = w_qkv.shape[0]
+        halves = jnp.concatenate((w_qkv, w_out), axis=1).reshape(share, 4, 2, width // 2)
+        halves = halves.transpose(2, 0, 1, 3).reshape(2, share, 2 * width)
+        gain_cols = jnp.broadcast_to(jnp.pad(norm_gains.T, ((0, 0), (0, 126))), (2, share, 128))
+        shard = jnp.concatenate((halves, gain_cols), axis=2).astype(F32)
+        segr = segments.reshape(1, tok_count)
+        segc = segments.reshape(tok_count, 1)
+        qkv, context, hidden, act_slots, w_blocks, dy_rows, w_in_all, w_hid_all, stats, scol, gains = head(
+            tokens, cotangent, shard, w_in[0], w_hid[0], routes, gate_logit, segr, segc, n_expert, capacity
+        )
+        da_back, y_rows, gin, ghid = swap(act_slots, dy_rows, w_in_all, w_hid_all)
+        grad_tokens, y_back, _r1, _r2, gin_own, ghid_own, own, gg = tail(
+            da_back.reshape(slot_rows, width),
+            scol,
+            tokens,
+            cotangent,
+            hidden,
+            qkv,
+            context,
+            stats,
+            w_blocks,
+            gains,
+            segr,
+            segc,
+            y_rows,
+            gin,
+            ghid,
+        )
+        block_out = block_output(y_back.reshape(slot_rows, width), scol, hidden, gate_logit)
+        me = lax.axis_index("expert") * n_narrow + lax.axis_index("narrow")
+        return (
+            block_out,
+            grad_tokens,
+            own[:3].transpose(1, 0, 2).reshape(share, 3 * width),
+            own[3],
+            lax.dynamic_slice_in_dim(gg[:2], me * share, share, axis=1),
+            gin_own[None],
+            ghid_own[None],
+        )
     gain_cols = jnp.pad(norm_gains.T, ((0, 0), (0, 126)))
     w_all = lax.all_gather(
         jnp.concatenate((w_qkv, w_out, gain_cols), axis=1), everyone, axis=0, tiled=True
@@ -816,38 +1318,6 @@
     grad_in = lax.dot_general(
         act_rows, grad_pre.reshape(slot_rows, n_narrow, -1), (((0,), (0,)), ((), ())), preferred_element_type=F32
     ).astype(BF16)
-    if n_expert == 8 and n_narrow == 4:
-        gin = grad_in.transpose(1, 0, 2)
-        ghid = grad_hid.reshape(n_narrow, -1, width)
-        grad_tokens, y_back, _r1, _r2, gin_own, ghid_own, own, gg = tail(
-            da_back,
-            scol,
-            tokens,
-            cotangent,
-            hidden,
-            qkv,
-            context,
-            stats,
-            w_all,
-            gains,
-            segr,
-            segc,
-            y_rows.reshape(n_expert, capacity, width),
-            gin,
-            ghid,
-        )
-        block_out = block_output(y_back.reshape(slot_rows, width), scol, hidden, gate_logit)
-        me = lax.axis_index("expert") * n_narrow + lax.axis_index("narrow")
-        share = width // (n_expert * n_narrow)
-        return (
-            block_out,
-            grad_tokens,
-            own[:3].transpose(1, 0, 2).reshape(share, 3 * width),
-            own[3],
-            lax.dynamic_slice_in_dim(gg[:2], me * share, share, axis=1),
-            gin_own[None],
-            ghid_own[None],
-        )
     y_back = exchange(y_rows)
     grad_tokens, grad_w, grad_gains = attend_bwd(
         da_back, scol, tokens, cotangent, hidden, qkv, context, stats, w_all, gains, segr, segc

time: 527 us -> 437 us (0.83); the launches traced: 518 us -> 437 us
  waiting for transfers between devices: 189 us -> 0 us
  Pallas kernels: 229 us -> 414 us
  matrix products: 44.2 us -> 0 us
  starting transfers between devices: 17 us -> 0 us
  between operations: 14.3 us -> 0.74 us
    pallas_call x3 -> x2, Pallas kernels: 114 us -> 278 us  [the longest x1 149 us: head(): pl.pallas_call(functools.partial(head_kernel, capacity, experts), out_sha...]
    all_gather x3 -> x0, waiting for transfers between devices: 111 us -> none  [the longest x1 90 us: local(): lax.all_gather(jnp.concatenate((w_qkv, w_out, gain_cols), axis=1), everyo...]
    all_to_all x3 -> x0, waiting for transfers between devices: 76.4 us -> none  [exchange(): lax.all_to_all(values.reshape(n_expert, capacity, width), 'expert', split...]
    dot_general x3 -> x0, matrix products: 44.2 us -> none  [the longest x1 15.5 us: dot(): lax.dot_general(a, b, (((1,), (0,)), ((), ())), preferred_element_type=F32)]
    pallas_call x1, Pallas kernels: 109 us -> 131 us  [tail(): pl.pallas_call(tail_kernel, out_shape=(jax.ShapeDtypeStruct((tokens, widt...]
    all_to_all x3 -> x0, starting transfers between devices: 16.9 us -> none  [exchange(): lax.all_to_all(values.reshape(n_expert, capacity, width), 'expert', split...]
    unnamed x33 -> x20, local copies, waits for them, and re-layouts: 16.3 us -> 14.1 us
  transfers between devices with their start and end apart: 6 -> 0, of which waited for: 4 -> 0; matrix products, arithmetic and copies ran while one was open for 10% -> 0% of each run, Pallas kernels for 11% -> 0%
where the time goes in v3:
time: 437 us
  Pallas kernels  414 us (95%)
  local copies, waits for them, and re-layouts  20.4 us (5%)
    pallas_call x1, Pallas kernels, head(): pl.pallas_call(functools.partial(head_kernel, capacity, experts), out_sha...  149 us
    pallas_call x1, Pallas kernels, tail(): pl.pallas_call(tail_kernel, out_shape=(jax.ShapeDtypeStruct((tokens, widt...  131 us
    pallas_call x1, Pallas kernels, swap(): pl.pallas_call(swap_kernel, out_shape=(jax.ShapeDtypeStruct((count, cap,...  129 us
    unnamed x20, local copies, waits for them, and re-layouts  14.1 us

profile of v3, /device:TPU:0, one launch (start us, length us, event | category | flops | bytes accessed | tf_op | source)
XLA Modules:
  0.0 436.6 jit_solution(2444220363635908800)
XLA Ops:
  0.6 1.7 copy.23.gate_ref
  2.3 1.7 copy.24.segc_ref
  4.0 0.9 pad_maximum_fusion
  5.0 0.1 reshape.39
  5.1 0.1 copy.31
  5.1 0.1 reshape.40
  5.2 0.7 copy.28
  6.0 0.7 maximum_convert_fusion.shard_hbm
  6.7 1.7 copy.22.rcol_ref
  8.4 149.3 %shard_map.153 = (bf16[1024,2304]{1,0:T(8,128)(2,1)}, bf16[1024,768]{1,0:T(8,128)(2,1)}, f32[1024,768]{1,0:T(8,128)}, bf16[8,256,768]{2,1,0:T(8,128)(2,1)}, bf16...) custom-call(bf16[1024,768]{1,0:T(8,128)(2,1)} %x_hbm.3, ...), custom_call_target="tpu_custom_call" | custom-call | flops 64424509440 | bytes 41943040 | tf_op jit(solution)/shard_map/pallas_call | solution.py:681
  157.7 129.1 %shard_map.154 = (bf16[8,256,768]{2,1,0:T(8,128)(2,1)}, bf16[8,256,768]{2,1,0:T(8,128)(2,1)}, bf16[4,768,768]{2,1,0:T(8,128)(2,1)}, bf16[4,768,768]{2,1,0:T(8,128)(2,1)}) custom-call(bf16[8,256,768]{2,1,0:T(8,128)(2,1)} %get-tuple-element.28.act_hbm, bf16[8,256,768]{2,1,0:T(8,128)(2,1)} %get-tuple-element.29.dy_hbm, ...), custom_call_target="tpu_custom_call" | custom-call | flops 107374182400 | bytes 62914560 | tf_op jit(solution)/shard_map/pallas_call | solution.py:1216
  286.8 0.0 copy-start
  286.8 0.0 copy-start.3
  286.8 130.5 %shard_map.155 = (f32[1024,768]{1,0:T(8,128)}, bf16[8,256,768]{2,1,0:T(8,128)(2,1)}, bf16[2,2,768,768]{3,2,1,0:T(8,128)(2,1)}, bf16[2,768,768]{2,1,0:T(8,128)(2,...) custom-call(bf16[2048,768]{1,0:T(8,128)(2,1)} %bitcast.30, ...), custom_call_target="tpu_custom_call" | custom-call | flops 85899345920 | bytes 41943040 | tf_op jit(solution)/shard_map/pallas_call | solution.py:1005
  417.4 0.0 copy-done
  417.4 0.0 copy-done.3
  417.4 0.0 copy-start.1
  417.4 1.9 copy-done.1
  419.3 0.0 copy-start.2
  419.3 1.9 copy-done.2
  421.2 0.0 copy-start.6
  421.2 4.9 %shard_map.156 = bf16[1024,768]{1,0:T(8,128)(2,1)} custom-call(bf16[2048,768]{1,0:T(8,128)(2,1)S(1)} %bitcast.19, f32[1024,1]{1,0:T(8,128)S(1)} %copy-done.3, f32[1024,768]{1,0:T(8,128)S(1)} %copy-done.2, f32[1024,1]{1,0:T(8,128)S(1)} %copy-done), custom_call_target="tpu_custom_call" | custom-call | flops 4294967296 | bytes 10485760 | tf_op jit(solution)/shard_map/pallas_call | solution.py:260
  426.1 0.0 copy-done.6
  426.1 0.7 copy.29
  426.8 0.6 slice_bitcast_fusion.1
  427.4 0.7 slice.11
  428.2 0.6 constant_dynamic-slice_fusion
  428.8 3.9 copy.35
  432.7 0.0 copy-done.5
  432.7 1.4 copy.36
  434.1 1.1 copy-done.4
  435.2 1.4 copy.37
  (5 shorter events, 0.0 us)
Async XLA Ops:
  286.8 130.6 %copy-start = (f32[1024,1]{1,0:T(8,128)S(1)}, f32[1024,1]{1,0:T(8,128)}, u32[]{:S(2)}) copy-start(f32[1024,1]{1,0:T(8,128)} %copy.23.gate_ref) | copy-start | bytes 12292
  286.8 130.6 %copy-start.3 = (f32[1024,1]{1,0:T(8,128)S(1)}, f32[1024,1]{1,0:T(8,128)}, u32[]{:S(2)}) copy-start(f32[1024,1]{1,0:T(8,128)} %get-tuple-element.40.scol_ref) | copy-start | bytes 12292
  417.4 1.9 copy-start.1
  419.3 1.9 copy-start.2
  421.2 4.9 %copy-start.6 = (f32[4,24,768]{2,1,0:T(8,128)S(1)}, f32[4,24,768]{2,1,0:T(8,128)}, u32[]{:S(2)}) copy-start(f32[4,24,768]{2,1,0:T(8,128)} %get-tuple-element.45) | copy-start | bytes 884740
  428.8 3.9 copy-start.5
  432.7 2.5 copy-start.4

commit v4 on v3

--- a/solution.py
+++ b/solution.py
@@ -468,11 +468,7 @@
     shard_hbm,
     win_hbm,
     whid_hbm,
-    rrow_ref,
-    rcol_ref,
-    gate_ref,
-    segr_ref,
-    segc_ref,
+    row_ref,
     qkv_hbm,
     c_hbm,
     h_hbm,
@@ -482,7 +478,7 @@
     win4_hbm,
     whid4_hbm,
     stat_ref,
-    scol_ref,
+    col_ref,
     gain_ref,
     x_ref,
     ct_ref,
@@ -514,14 +510,24 @@
     loading_ct = loads.start(ct_hbm, ct_ref)
     loading_x = loads.start(x_hbm, x_ref)
     own_shard = loads.start(shard_hbm.at[c], st.at[c])
-    own_in = loads.start(win_hbm, win4_hbm.at[me_n])
-    own_hid = loads.start(whid_hbm, whid4_hbm.at[me_n])
 
     greet(peers_of(z, y, x, c) + [core, xpeer])
     zero = links.push(shard_hbm.at[1 - c], st.at[c], core)
 
+    deep = width // 2
+    upper, lower = pl.ds(0, deep), pl.ds(deep, deep)
+
+    def hand(src, dst, rows):
+        return links.push(src.at[rows], dst.at[me_n, rows], xpeer)
+
+    def onward(dst, rows):
+        part = dst.at[(1 - x) * 2 + c, rows]
+        return links.push(part, part, core)
+
+    parts = [(hand(win_hbm, win4_hbm, upper), win4_hbm, upper)]
+
     wide = max(8, experts)
-    hot = (iota((wide, tokens), 0) == rrow_ref[...]).astype(F32)
+    hot = (iota((wide, tokens), 0).astype(F32) == row_ref[0:1, :]).astype(F32)
     before = (iota((tokens, tokens), 0) < iota((tokens, tokens), 1)).astype(BF16)
     rank = dot(hot.astype(BF16), before)
     base = (iota((wide, tokens), 0) * capacity).astype(F32)
@@ -545,11 +551,13 @@
                 group.append(links.push(wg.at[z, y, x], wg.at[z, y, x], to))
         ring_z.append(group)
 
-    hot_c = (iota((tokens, 128), 1) == rcol_ref[...]).astype(F32)
+    listed = row_ref[...].T
+    hot_c = (iota((tokens, 128), 1).astype(F32) == listed[:, 0:1]).astype(F32)
     after = (iota((tokens, tokens), 1) < iota((tokens, tokens), 0)).astype(BF16)
     rank_c = dot(after, hot_c.astype(BF16))
     base_c = (iota((tokens, 128), 1) * capacity).astype(F32)
-    scol_ref[...] = jnp.sum(hot_c * (rank_c + base_c), axis=1, keepdims=True)
+    scol = jnp.sum(hot_c * (rank_c + base_c), axis=1, keepdims=True)
+    col_ref[...] = jnp.where(iota(listed.shape, 1) == 0, scol, listed)
 
     def fill(values, out):
         @pl.loop(0, out.shape[0])
@@ -558,8 +566,13 @@
             out[i] = dot((ids == srow).astype(BF16), values).astype(BF16)
 
     loading_ct.wait()
-    fill((jax.nn.sigmoid(gate_ref[...]) * ct_ref[...].astype(F32)).astype(BF16), dy_ref)
-
+    fill((jax.nn.sigmoid(listed[:, 1:2]) * ct_ref[...].astype(F32)).astype(BF16), dy_ref)
+
+    dy_copies = []
+    for k in FLIPS:
+        zz, yy = across(z, k >> 1), (1 - y if k & 1 else y)
+        dy_copies.append(links.push(dy_ref.at[zz * 2 + yy], dyrow_hbm.at[me_e], device(zz, yy, x, c)))
+    own_dy = loads.start(dy_ref.at[me_e], dyrow_hbm.at[me_e])
     ring_2 = []
     for piece in range(2):
         for copy in ring_z[piece]:
@@ -572,11 +585,6 @@
         if piece == 0:
             group.append(links.push(wg.at[:, y, x], wg.at[:, y, x], ypeer))
         ring_2.append(group)
-    dy_copies = []
-    for k in FLIPS:
-        zz, yy = across(z, k >> 1), (1 - y if k & 1 else y)
-        dy_copies.append(links.push(dy_ref.at[zz * 2 + yy], dyrow_hbm.at[me_e], device(zz, yy, x, c)))
-    own_dy = loads.start(dy_ref.at[me_e], dyrow_hbm.at[me_e])
     ring_3 = []
     for piece in range(2):
         for copy in ring_2[piece]:
@@ -589,16 +597,13 @@
         if piece == 0:
             group.append(links.push(wg.at[:, :, x], wg.at[:, :, x], xpeer))
         ring_3.append(group)
+    for src, dst, rows in ((win_hbm, win4_hbm, lower), (whid_hbm, whid4_hbm, upper), (whid_hbm, whid4_hbm, lower)):
+        parts.append((hand(src, dst, rows), dst, rows))
     ring_4 = []
     for piece in range(2):
         for copy in ring_3[piece]:
             copy.wait()
         ring_4.append([links.push(wq.at[2 * j + c], wq.at[2 * j + c], core) for j in (2 * piece, 2 * piece + 1)])
-
-    slices = []
-    for src, dst in ((win_hbm, win4_hbm), (whid_hbm, whid4_hbm)):
-        slices.append((links.push(src, dst.at[me_n], xpeer), dst))
-    core_slices = [links.push(src, dst.at[me_n], core) for src, dst in ((win_hbm, win4_hbm), (whid_hbm, whid4_hbm))]
 
     gains = jnp.transpose(wg[...].reshape(width, 128).astype(F32))[0:8, :]
     gain_ref[...] = gains
@@ -609,6 +614,14 @@
         for copy in ring_4[piece]:
             copy.wait()
     storing = [loads.start(wq, w_hbm)]
+    core_slices = [links.push(src, dst.at[me_n], core) for src, dst in ((win_hbm, win4_hbm), (whid_hbm, whid4_hbm))]
+
+    def pass_on(i):
+        copy, dst, rows = parts[i]
+        copy.wait()
+        core_slices.append(onward(dst, rows))
+
+    pass_on(0)
 
     @pl.loop(0, blocks)
     def _(i):
@@ -627,7 +640,7 @@
         keys = pl.ds(kb * BLOCK, span)
         q_pos = iota((BLOCK, span), 0) + qb * BLOCK
         k_pos = iota((BLOCK, span), 1) + kb * BLOCK
-        ok = (k_pos <= q_pos) & (segc_ref[rows, :] == segr_ref[0:1, keys])
+        ok = (k_pos <= q_pos) & (col_ref[rows, 2:3] == row_ref[2:3, keys])
         bias_scr[:, :span] = jnp.where(ok, 0.0, BIG_NEGATIVE)
 
         @pl.loop(0, pairs)
@@ -649,11 +662,6 @@
             col_scr[rows, :] = col
             c_ref[rows, pl.ds(at, 128)] = jnp.where(low, outs[0], outs[1]).astype(BF16)
 
-        if qb == 0:
-            for copy, dst in slices:
-                copy.wait()
-                core_slices.append(links.push(dst.at[(1 - x) * 2 + c], dst.at[(1 - x) * 2 + c], core))
-
     storing.append(loads.start(c_ref, c_hbm))
     stat_ref[...] = col_scr[...].T
 
@@ -668,11 +676,13 @@
     storing.append(loads.start(h_ref, h_hbm))
     fill(a_scr[...], act_ref)
     storing.append(loads.start(act_ref, act_hbm))
-    for copy in storing + [own_in, own_hid, own_dy] + core_slices + dy_copies:
+    for i in range(1, 4):
+        pass_on(i)
+    for copy in storing + [own_dy] + core_slices + dy_copies:
         copy.wait()
 
 
-def head(tokens_in, cotangent, shard, w_in, w_hid, routes, gate_logit, segr, segc, experts, capacity):
+def head(tokens_in, cotangent, shard, w_in, w_hid, listed, experts, capacity):
     tokens, width = tokens_in.shape
     any_spec = pl.BlockSpec(memory_space=pl.ANY)
     vmem = pl.BlockSpec(memory_space=pltpu.VMEM)
@@ -690,10 +700,10 @@
             jax.ShapeDtypeStruct((4,) + w_in.shape, BF16),
             jax.ShapeDtypeStruct((4,) + w_hid.shape, BF16),
             jax.ShapeDtypeStruct((128, tokens), F32),
-            jax.ShapeDtypeStruct((tokens, 1), F32),
+            jax.ShapeDtypeStruct((tokens, 8), F32),
             jax.ShapeDtypeStruct((8, width), F32),
         ),
-        in_specs=[any_spec] * 5 + [vmem] * 5,
+        in_specs=[any_spec] * 5 + [vmem],
         out_specs=(any_spec,) * 8 + (vmem,) * 3,
         scratch_shapes=[
             pltpu.VMEM((tokens, width), BF16),
@@ -715,18 +725,120 @@
         ],
         compiler_params=pltpu.CompilerParams(vmem_limit_bytes=62 << 20, collective_id=0, has_side_effects=True),
         cost_estimate=pl.CostEstimate(flops=60 << 30, bytes_accessed=40 << 20, transcendentals=0),
-    )(
-        tokens_in,
-        cotangent,
-        shard,
-        w_in,
-        w_hid,
-        routes.reshape(1, tokens),
-        routes,
-        gate_logit.reshape(tokens, 1),
-        segr,
-        segc,
-    )
+    )(tokens_in, cotangent, shard, w_in, w_hid, listed)
+
+
+class Reduce:
+    def __init__(self, spot, ph, gq, rc, r1, r2, r3, fin, r4, send_sems, recv_sems):
+        self.z, self.y, self.x, self.c = spot
+        self.gq, self.rc, self.r1, self.r2, self.r3, self.fin, self.r4 = (
+            gq.at[ph],
+            rc.at[ph],
+            r1.at[ph],
+            r2.at[ph],
+            r3.at[ph],
+            fin.at[ph],
+            r4.at[ph],
+        )
+        self.base = ph * 7
+        self.send, self.recv = send_sems, recv_sems
+
+    def copy(self, i, src, dst, to):
+        return pltpu.make_async_remote_copy(
+            src_ref=src,
+            dst_ref=dst,
+            send_sem=self.send.at[self.base + i],
+            recv_sem=self.recv.at[self.base + i],
+            device_id=to,
+            device_id_type=MESH,
+        )
+
+    def turn(self, i):
+        return i * (1 - self.c) + self.y * self.c, self.x * (1 - self.c) + i * self.c
+
+    def add(self, where, term):
+        self.gq[where] = (self.gq[where].astype(F32) + term.astype(F32)).astype(BF16)
+
+    def cores(self):
+        z, y, x, c = self.z, self.y, self.x, self.c
+        return self.copy(0, self.gq.at[1 - c], self.rc, device(z, y, x, 1 - c))
+
+    def by_core(self, go, first, second):
+        @pl.when(self.c == 0)
+        def _():
+            go(first)
+
+        @pl.when(self.c == 1)
+        def _():
+            go(second)
+
+    def one(self, go):
+        z, y, x, c = self.z, self.y, self.x, self.c
+        self.by_core(
+            go,
+            self.copy(1, self.gq.at[0, :, :, 1 - x], self.r1, device(z, y, 1 - x, c)),
+            self.copy(1, self.gq.at[1, :, 1 - y], self.r1, device(z, 1 - y, x, c)),
+        )
+
+    def two(self, go):
+        z, y, x, c = self.z, self.y, self.x, self.c
+        self.by_core(
+            go,
+            self.copy(2, self.gq.at[0, :, 1 - y, x], self.r2, device(z, 1 - y, x, c)),
+            self.copy(2, self.gq.at[1, :, y, 1 - x], self.r2, device(z, y, 1 - x, c)),
+        )
+
+    def three(self):
+        z, y, x, c = self.z, self.y, self.x, self.c
+        return [
+            self.copy(2 + k, self.gq.at[c, across(z, k), y, x], self.r3.at[k - 1], device(across(z, k), y, x, c))
+            for k in (1, 2, 3)
+        ]
+
+    def four(self):
+        z, y, x, c = self.z, self.y, self.x, self.c
+        rows = pl.ds(pl.multiple_of((1 - c) * 24, 8), 24)
+        return self.copy(6, self.fin.at[rows], self.r4, device(z, y, x, 1 - c))
+
+    def step(self, stage):
+        z, y, x, c = self.z, self.y, self.x, self.c
+        if stage == 0:
+            self.cores().start()
+        if stage == 1:
+            self.cores().wait()
+
+            @pl.loop(0, 4)
+            def _(k):
+                self.add((c, k), self.rc[k])
+
+            self.one(lambda copy: copy.start())
+        if stage == 2:
+            self.one(lambda copy: copy.wait())
+
+            @pl.loop(0, 4)
+            def _(k):
+                for i in range(2):
+                    yy, xx = self.turn(i)
+                    self.add((c, k, yy, xx), self.r1[k, i])
+
+            self.two(lambda copy: copy.start())
+        if stage == 3:
+            self.two(lambda copy: copy.wait())
+
+            @pl.loop(0, 4)
+            def _(k):
+                self.add((c, k, y, x), self.r2[k])
+
+            for copy in self.three():
+                copy.start()
+        if stage == 4:
+            for copy in self.three():
+                copy.wait()
+            total = self.gq[c, z, y, x].astype(F32)
+            for k in range(3):
+                total = total + self.r3[k].astype(F32)
+            self.fin[...] = total
+            self.four().start()
 
 
 def tail_kernel(
@@ -738,19 +850,16 @@
     c_hbm,
     w_hbm,
     yrow_hbm,
-    gin_hbm,
-    ghid_hbm,
-    scol_ref,
+    gw_hbm,
+    col_ref,
+    row_ref,
     stat_ref,
     gain_ref,
-    segr_ref,
-    segc_ref,
     gt_hbm,
-    yback_hbm,
     r1_hbm,
     r2_hbm,
-    gin_out,
-    ghid_out,
+    gw_out,
+    out_hbm,
     own_ref,
     gg_ref,
     ret_ref,
@@ -764,54 +873,53 @@
     dc_scr,
     dhb_scr,
     dqkv_scr,
-    act_scr,
+    actt_scr,
     d_scr,
     dk_scr,
     dv_scr,
     gq,
     rc,
-    r1a,
-    r1b,
-    r2a,
-    r2b,
-    r3,
+    q1,
+    q2,
+    q3,
     fin,
-    r4,
+    q4,
     ggs,
     rg,
     na,
     nb,
     nsum,
-    nout,
+    yback,
     send_sems,
     recv_sems,
+    red_send,
+    red_recv,
     load_sems,
 ):
-    z, y, x, c = place()
+    spot = place()
+    z, y, x, c = spot
     me_e = z * 2 + y
     tokens, width = x_ref.shape
-    slots = ret_ref.shape[0]
+    slots, _w = ret_ref.shape
     blocks = tokens // BLOCK
-    pairs = width // 128
+    half = width // 2
     core, xpeer, ypeer = device(z, y, x, 1 - c), device(z, y, 1 - x, c), device(z, 1 - y, x, c)
     far = peers_of(z, y, x, c)
     links = Links(send_sems, recv_sems)
     loads = Loads(load_sems)
 
+    def reduce(ph):
+        return Reduce(spot, ph, gq, rc, q1, q2, q3, fin, q4, red_send, red_recv)
+
     first = [
         loads.start(a, b)
-        for a, b in ((ret_hbm, ret_ref), (h_hbm, h_ref), (ct_hbm, ct_ref), (c_hbm, c_ref), (w_hbm, w_ref))
+        for a, b in ((ret_hbm, ret_ref), (h_hbm, h_ref), (ct_hbm, ct_ref), (c_hbm, c_ref), (w_hbm, w_ref), (x_hbm, x_ref))
     ]
-    second = [loads.start(a, b) for a, b in ((qkv_hbm, qkv_ref), (x_hbm, x_ref))]
-    own_y = loads.start(yrow_hbm.at[me_e], yback_hbm.at[me_e])
-
+    second = [loads.start(qkv_hbm, qkv_ref), loads.start(yrow_hbm.at[me_e], yback.at[me_e])]
     greet(far + [core, xpeer])
 
-    y_copies = [links.push(yrow_hbm.at[to[0]], yback_hbm.at[me_e], to) for to in far]
-    w_copies = []
-    for a, src in enumerate((gin_hbm, ghid_hbm)):
-        for xx in range(2):
-            w_copies.append(links.push(src.at[xx * 2 + 1 - c], r1_hbm.at[a, xx], core))
+    w_copies = [links.push(gw_hbm.at[xx * 2 + 1 - c], r1_hbm.at[xx], core) for xx in range(2)]
+    y_copies = [links.push(yrow_hbm.at[to[0]], yback.at[me_e], to) for to in far]
 
     gain_one = gain_ref[0:1, :]
     gain_two = gain_ref[1:2, :]
@@ -820,11 +928,13 @@
         copy.wait()
     ggs[...] = jnp.zeros_like(ggs)
 
+    def picks(rows):
+        return (iota((BLOCK, slots), 1).astype(F32) == col_ref[rows, 0:1]).astype(BF16)
+
     @pl.loop(0, blocks)
     def _(i):
         rows = pl.ds(pl.multiple_of(i * BLOCK, BLOCK), BLOCK)
-        pick = (iota((BLOCK, slots), 1).astype(F32) == scol_ref[rows, :]).astype(BF16)
-        da = dot(pick, ret_ref[...])
+        da = dot(picks(rows), ret_ref[...])
         normed, factor = normalize(h_ref[rows, :])
         ggs[0, 1:2, :] += jnp.sum(da * normed, axis=0, keepdims=True)
         dh = ct_ref[rows, :].astype(F32) + norm_back(da * gain_two, normed, factor)
@@ -841,72 +951,92 @@
             preferred_element_type=F32,
         )
 
+    def put(ph, value):
+        for owner in range(2):
+            for chip in range(16):
+                gq[ph, owner, chip // 4, chip // 2 % 2, chip % 2] = value[
+                    chip * 48 : chip * 48 + 48, owner * half : (owner + 1) * half
+                ].astype(BF16)
+
+    put(0, t_dot(c_ref[...], dhb_scr[...]))
+    reduce(0).step(0)
+
     for copy in w_copies:
         copy.wait()
     x_copies = []
-    for a, src in enumerate((gin_hbm, ghid_hbm)):
-        for step in range(2):
-            xx = 1 - x if step == 0 else x
-            la = loads.start(src.at[xx * 2 + c], na)
-            lb = loads.start(r1_hbm.at[a, xx], nb)
-            la.wait()
-            lb.wait()
-            nsum[step, a] = (na[...].astype(F32) + nb[...].astype(F32)).astype(BF16)
-            if step == 0:
-                x_copies.append(links.push(nsum.at[0, a], r2_hbm.at[a], xpeer))
-
-    def put_quarter(j, value):
-        for chip in range(16):
-            gq[j, chip // 4, chip // 2 % 2, chip % 2] = value[chip * 48 : chip * 48 + 48, :].astype(BF16)
-
-    put_quarter(3, t_dot(c_ref[...], dhb_scr[...]))
+    for step in range(2):
+        xx = 1 - x if step == 0 else x
+        la = loads.start(gw_hbm.at[xx * 2 + c], na)
+        lb = loads.start(r1_hbm.at[xx], nb)
+        la.wait()
+        lb.wait()
+        nsum[step] = (na[...].astype(F32) + nb[...].astype(F32)).astype(BF16)
+        if step == 0:
+            x_copies.append(links.push(nsum.at[0], r2_hbm, xpeer))
+
+    @pl.loop(0, blocks)
+    def _(i):
+        rows = pl.ds(pl.multiple_of(i * BLOCK, BLOCK), BLOCK)
+        normed, _f = normalize(x_ref[rows, :].astype(F32))
+        dhb_scr[rows, :] = (normed * gain_one).astype(BF16)
+
+    actt_scr[...] = dhb_scr[...].T
     for copy in second:
         copy.wait()
     low = iota((BLOCK, 128), 1) < HEAD_DIM
     scale = HEAD_DIM**-0.5
 
-    @pl.loop(0, pairs)
-    def _(hp):
-        at = pl.multiple_of(hp * 128, 128)
-        dk_scr[...] = jnp.zeros_like(dk_scr)
-        dv_scr[...] = jnp.zeros_like(dv_scr)
-        for qb in range(blocks):
-            rows = pl.ds(qb * BLOCK, BLOCK)
-            q = qkv_ref[rows, pl.ds(at, 128)] * jnp.asarray(scale, BF16)
-            dc = dc_scr[rows, pl.ds(at, 128)]
-            q_half = [jnp.where(low, q, 0), jnp.where(low, 0, q)]
-            dc_half = [jnp.where(low, dc, 0), jnp.where(low, 0, dc)]
-            dq = jnp.zeros((BLOCK, 128), F32)
-            for kb in range(max(0, qb - LOOKBACK), qb + 1):
-                keys = pl.ds(kb * BLOCK, BLOCK)
-                k = qkv_ref[keys, pl.ds(width + at, 128)]
-                v = qkv_ref[keys, pl.ds(2 * width + at, 128)]
-                ok = segc_ref[keys, :] == segr_ref[0:1, rows]
-                if kb == qb:
-                    ok = ok & (iota((BLOCK, BLOCK), 0) <= iota((BLOCK, BLOCK), 1))
-                ps, dss = [], []
-                for half in range(2):
-                    s = dot_t(k, q_half[half])
-                    p = jnp.where(ok, jnp.exp(s - stat_ref[pl.ds(2 * hp + half, 1), rows]), 0.0)
-                    dp = dot_t(v, dc_half[half])
-                    dss.append((p * (dp - d_scr[pl.ds(2 * hp + half, 1), rows])).astype(BF16))
-                    ps.append(p.astype(BF16))
-                dv_scr[keys, :] += dot(jnp.concatenate(ps, 1), jnp.concatenate(dc_half, 0))
-                dk_scr[keys, :] += dot(jnp.concatenate(dss, 1), jnp.concatenate(q_half, 0))
-                dq += jnp.where(low, t_dot(dss[0], k), t_dot(dss[1], k))
-            dqkv_scr[rows, pl.ds(at, 128)] = (dq * scale).astype(BF16)
-        dqkv_scr[:, pl.ds(width + at, 128)] = dk_scr[...].astype(BF16)
-        dqkv_scr[:, pl.ds(2 * width + at, 128)] = dv_scr[...].astype(BF16)
-
-    @pl.loop(0, blocks)
-    def _(i):
-        rows = pl.ds(pl.multiple_of(i * BLOCK, BLOCK), BLOCK)
-        normed, _f = normalize(x_ref[rows, :].astype(F32))
-        act_scr[rows, :] = (normed * gain_one).astype(BF16)
-
-    for j in range(3):
-        put_quarter(j, t_dot(act_scr[...], dqkv_scr[:, j * width : (j + 1) * width]))
-    core_copies = [links.push(gq.at[2 * (1 - c) + p], rc.at[p], core) for p in range(2)]
+    @pl.loop(0, 3)
+    def _(t):
+        @pl.loop(0, 2)
+        def _(inner):
+            hp = 2 * t + inner
+            at = pl.multiple_of(hp * 128, 128)
+            dk_scr[...] = jnp.zeros_like(dk_scr)
+            dv_scr[...] = jnp.zeros_like(dv_scr)
+            for qb in range(blocks):
+                rows = pl.ds(qb * BLOCK, BLOCK)
+                q = qkv_ref[rows, pl.ds(at, 128)] * jnp.asarray(scale, BF16)
+                dc = dc_scr[rows, pl.ds(at, 128)]
+                q_half = [jnp.where(low, q, 0), jnp.where(low, 0, q)]
+                dc_half = [jnp.where(low, dc, 0), jnp.where(low, 0, dc)]
+                dq = jnp.zeros((BLOCK, 128), F32)
+                for kb in range(max(0, qb - LOOKBACK), qb + 1):
+                    keys = pl.ds(kb * BLOCK, BLOCK)
+                    k = qkv_ref[keys, pl.ds(width + at, 128)]
+                    v = qkv_ref[keys, pl.ds(2 * width + at, 128)]
+                    ok = col_ref[keys, 2:3] == row_ref[2:3, rows]
+                    if kb == qb:
+                        ok = ok & (iota((BLOCK, BLOCK), 0) <= iota((BLOCK, BLOCK), 1))
+                    ps, dss = [], []
+                    for side in range(2):
+                        s = dot_t(k, q_half[side])
+                        p = jnp.where(ok, jnp.exp(s - stat_ref[pl.ds(2 * hp + side, 1), rows]), 0.0)
+                        dp = dot_t(v, dc_half[side])
+                        dss.append((p * (dp - d_scr[pl.ds(2 * hp + side, 1), rows])).astype(BF16))
+                        ps.append(p.astype(BF16))
+                    dv_scr[keys, :] += dot(jnp.concatenate(ps, 1), jnp.concatenate(dc_half, 0))
+                    dk_scr[keys, :] += dot(jnp.concatenate(dss, 1), jnp.concatenate(q_half, 0))
+                    dq += jnp.where(low, t_dot(dss[0], k), t_dot(dss[1], k))
+                dqkv_scr[rows, pl.ds(at, 128)] = (dq * scale).astype(BF16)
+            dqkv_scr[:, pl.ds(width + at, 128)] = dk_scr[...].astype(BF16)
+            dqkv_scr[:, pl.ds(2 * width + at, 128)] = dv_scr[...].astype(BF16)
+
+        columns = []
+        for inner in range(2):
+            at = pl.multiple_of((2 * t + inner) * 128, 128)
+            columns += [dqkv_scr[:, pl.ds(j * width + at, 128)] for j in range(3)]
+        put(t + 1, dot(actt_scr[...], jnp.concatenate(columns, axis=1)))
+        reduce(t + 1).step(0)
+        reduce(t).step(1)
+
+        @pl.when(t >= 1)
+        def _():
+            reduce(t - 1).step(2)
+
+        @pl.when(t >= 2)
+        def _():
+            reduce(t - 2).step(3)
 
     @pl.loop(0, blocks)
     def _(i):
@@ -916,106 +1046,75 @@
         ggs[0, 0:1, :] += jnp.sum(dn * normed, axis=0, keepdims=True)
         gt_ref[rows, :] += norm_back(dn * gain_one, normed, factor)
 
-    store_gt = loads.start(gt_ref, gt_hbm)
+    stores = [loads.start(gt_ref, gt_hbm)]
     gains_copy = links.push(ggs.at[0], rg.at[0], core)
-    for copy in core_copies:
-        copy.wait()
-    qa, qb_ = 2 * c, 2 * c + 1
-
-    @pl.loop(0, 4)
-    def _(k):
-        for p in range(2):
-            gq[2 * c + p, k] = (gq[2 * c + p, k].astype(F32) + rc[p, k].astype(F32)).astype(BF16)
-
-    copies = [
-        links.push(gq.at[qa, :, :, 1 - x], r1a, xpeer),
-        links.push(gq.at[qb_, :, 1 - y], r1b, ypeer),
-    ]
+    reduce(3).step(1)
+    reduce(2).step(2)
+    reduce(1).step(3)
+    reduce(0).step(4)
     gains_copy.wait()
     ggs[1] = ggs[0] + rg[0]
     gains_copy = links.push(ggs.at[1], rg.at[1], xpeer)
-    for copy in copies:
+
+    def finish(lo, hi):
+        @pl.loop(lo, hi)
+        def _(i):
+            rows = pl.ds(pl.multiple_of(i * BLOCK, BLOCK), BLOCK)
+            got = dot(picks(rows), yback[...].reshape(slots, width))
+            ct_ref[rows, :] = (h_ref[rows, :] + jax.nn.sigmoid(col_ref[rows, 1:2]) * got).astype(BF16)
+
+    for copy in y_copies:
         copy.wait()
-
-    @pl.loop(0, 4)
-    def _(k):
-        for i in range(2):
-            gq[qa, k, i, x] = (gq[qa, k, i, x].astype(F32) + r1a[k, i].astype(F32)).astype(BF16)
-            gq[qb_, k, y, i] = (gq[qb_, k, y, i].astype(F32) + r1b[k, i].astype(F32)).astype(BF16)
-
-    copies = [
-        links.push(gq.at[qa, :, 1 - y, x], r2a, ypeer),
-        links.push(gq.at[qb_, :, y, 1 - x], r2b, xpeer),
-    ]
+    finish(0, 2)
+    reduce(3).step(2)
+    reduce(2).step(3)
+    reduce(1).step(4)
     gains_copy.wait()
     ggs[2] = ggs[1] + rg[1]
     gains_copy = links.push(ggs.at[2], rg.at[2], ypeer)
-    for copy in copies:
-        copy.wait()
-
-    @pl.loop(0, 4)
-    def _(k):
-        gq[qa, k, y, x] = (gq[qa, k, y, x].astype(F32) + r2a[k].astype(F32)).astype(BF16)
-        gq[qb_, k, y, x] = (gq[qb_, k, y, x].astype(F32) + r2b[k].astype(F32)).astype(BF16)
-
-    copies = []
-    for k in (2, 3, 1):
-        zz = across(z, k)
-        for p in range(2):
-            copies.append(links.push(gq.at[2 * c + p, zz, y, x], r3.at[p, k - 1], device(zz, y, x, c)))
+    finish(2, blocks)
+    stores.append(loads.start(ct_ref, out_hbm))
+    reduce(3).step(3)
+    reduce(2).step(4)
     gains_copy.wait()
     ggs[3] = ggs[2] + rg[2]
-    for k in (2, 3, 1):
-        copies.append(links.push(ggs.at[3], rg.at[2 + k], device(across(z, k), y, x, c)))
-
+    gain_copies = [links.push(ggs.at[3], rg.at[2 + k], device(across(z, k), y, x, c)) for k in (1, 2, 3)]
     for copy in x_copies:
         copy.wait()
-    stores = []
-    for a, out in enumerate((gin_out, ghid_out)):
-        lb = loads.start(r2_hbm.at[a], nb)
-        lb.wait()
-        nout[a] = nsum[1, a].astype(F32) + nb[...].astype(F32)
-        stores.append(loads.start(nout.at[a], out))
-
-    for copy in copies:
+    lb = loads.start(r2_hbm, nb)
+    lb.wait()
+    gw_out[...] = nsum[1].astype(F32) + nb[...].astype(F32)
+    reduce(3).step(4)
+    for copy in gain_copies:
         copy.wait()
-    for p in range(2):
-        total = gq[2 * c + p, z, y, x].astype(F32)
-        for k in range(3):
-            total = total + r3[p, k].astype(F32)
-        fin[p] = total
-    last = links.push(fin.at[:, pl.ds(pl.multiple_of((1 - c) * 24, 8), 24)], r4, core)
     gg_ref[...] = ggs[3] + rg[3] + rg[4] + rg[5]
-    for p in range(2):
-        own_ref[2 * c + p] = fin[p, pl.ds(pl.multiple_of(c * 24, 8), 24), :]
-    last.wait()
-    for p in range(2):
-        own_ref[2 * (1 - c) + p] = r4[p]
-    for copy in stores + y_copies:
+    for ph in range(4):
+        own_ref[ph, c] = fin[ph, pl.ds(pl.multiple_of(c * 24, 8), 24), :]
+        reduce(ph).four().wait()
+        own_ref[ph, 1 - c] = q4[ph]
+    for copy in stores:
         copy.wait()
-    own_y.wait()
-    store_gt.wait()
-
-
-def tail(returned, scol, tokens_in, cotangent, hidden, qkv, context, stats, w_all, gains, segr, segc, y_rows, gin, ghid):
+
+
+def tail(returned, cols, rows, tokens_in, cotangent, hidden, qkv, context, stats, w_blocks, gains, y_rows, gw):
     tokens, width = tokens_in.shape
     slots = returned.shape[0]
+    half = width // 2
     any_spec = pl.BlockSpec(memory_space=pl.ANY)
     vmem = pl.BlockSpec(memory_space=pltpu.VMEM)
     return pl.pallas_call(
         tail_kernel,
         out_shape=(
             jax.ShapeDtypeStruct((tokens, width), F32),
-            jax.ShapeDtypeStruct(y_rows.shape, BF16),
-            jax.ShapeDtypeStruct((2, 2) + gin.shape[1:], BF16),
-            jax.ShapeDtypeStruct((2,) + gin.shape[1:], BF16),
-            jax.ShapeDtypeStruct(gin.shape[1:], F32),
-            jax.ShapeDtypeStruct(ghid.shape[1:], F32),
-            jax.ShapeDtypeStruct((4, 24, width), F32),
+            jax.ShapeDtypeStruct((2,) + gw.shape[1:], BF16),
+            jax.ShapeDtypeStruct(gw.shape[1:], BF16),
+            jax.ShapeDtypeStruct(gw.shape[1:], F32),
+            jax.ShapeDtypeStruct((tokens, width), BF16),
+            jax.ShapeDtypeStruct((4, 2, 24, half), F32),
             jax.ShapeDtypeStruct((8, width), F32),
         ),
-        in_specs=[any_spec] * 10 + [vmem] * 5,
-        out_specs=(any_spec,) * 6 + (vmem,) * 2,
+        in_specs=[any_spec] * 9 + [vmem] * 4,
+        out_specs=(any_spec, any_spec, any_spec, vmem, any_spec, vmem, vmem),
         scratch_shapes=[
             pltpu.VMEM((slots, width), BF16),
             pltpu.VMEM((tokens, width), BF16),
@@ -1023,37 +1122,37 @@
             pltpu.VMEM((tokens, width), F32),
             pltpu.VMEM((tokens, 3 * width), BF16),
             pltpu.VMEM((tokens, width), BF16),
-            pltpu.VMEM(w_all.shape, BF16),
+            pltpu.VMEM(w_blocks.shape, BF16),
             pltpu.VMEM((tokens, width), F32),
             pltpu.VMEM((tokens, width), BF16),
             pltpu.VMEM((tokens, width), BF16),
             pltpu.VMEM((tokens, 3 * width), BF16),
-            pltpu.VMEM((tokens, width), BF16),
+            pltpu.VMEM((width, tokens), BF16),
             pltpu.VMEM((16, tokens), F32),
             pltpu.VMEM((tokens, 128), F32),
             pltpu.VMEM((tokens, 128), F32),
-            pltpu.VMEM((4, 4, 2, 2, 48, width), BF16),
-            pltpu.VMEM((2, 4, 2, 2, 48, width), BF16),
-            pltpu.VMEM((4, 2, 48, width), BF16),
-            pltpu.VMEM((4, 2, 48, width), BF16),
-            pltpu.VMEM((4, 48, width), BF16),
-            pltpu.VMEM((4, 48, width), BF16),
-            pltpu.VMEM((2, 3, 48, width), BF16),
-            pltpu.VMEM((2, 48, width), F32),
-            pltpu.VMEM((2, 24, width), F32),
+            pltpu.VMEM((4, 2, 4, 2, 2, 48, half), BF16),
+            pltpu.VMEM((4, 4, 2, 2, 48, half), BF16),
+            pltpu.VMEM((4, 4, 2, 48, half), BF16),
+            pltpu.VMEM((4, 4, 48, half), BF16),
+            pltpu.VMEM((4, 3, 48, half), BF16),
+            pltpu.VMEM((4, 48, half), F32),
+            pltpu.VMEM((4, 24, half), F32),
             pltpu.VMEM((4, 8, width), F32),
             pltpu.VMEM((6, 8, width), F32),
-            pltpu.VMEM(gin.shape[1:], BF16),
-            pltpu.VMEM(gin.shape[1:], BF16),
-            pltpu.VMEM((2, 2) + gin.shape[1:], BF16),
-            pltpu.VMEM((2,) + gin.shape[1:], F32),
-            pltpu.SemaphoreType.DMA((40,)),
-            pltpu.SemaphoreType.DMA((40,)),
-            pltpu.SemaphoreType.DMA((24,)),
+            pltpu.VMEM(gw.shape[1:], BF16),
+            pltpu.VMEM(gw.shape[1:], BF16),
+            pltpu.VMEM((2,) + gw.shape[1:], BF16),
+            pltpu.VMEM(y_rows.shape, BF16),
+            pltpu.SemaphoreType.DMA((20,)),
+            pltpu.SemaphoreType.DMA((20,)),
+            pltpu.SemaphoreType.DMA((28,)),
+            pltpu.SemaphoreType.DMA((28,)),
+            pltpu.SemaphoreType.DMA((16,)),
         ],
         compiler_params=pltpu.CompilerParams(vmem_limit_bytes=62 << 20, collective_id=2, has_side_effects=True),
         cost_estimate=pl.CostEstimate(flops=80 << 30, bytes_accessed=40 << 20, transcendentals=0),
-    )(returned, tokens_in, cotangent, hidden, qkv, context, w_all, y_rows, gin, ghid, scol, stats, gains, segr, segc)
+    )(returned, tokens_in, cotangent, hidden, qkv, context, w_blocks, y_rows, gw, cols, rows, stats, gains)
 
 
 def flipped(z, y, k):
@@ -1067,6 +1166,8 @@
     dy_hbm,
     win_hbm,
     whid_hbm,
+    own_in_hbm,
+    own_hid_hbm,
     ret_hbm,
     y_hbm,
     gin_hbm,
@@ -1081,12 +1182,15 @@
     us,
     gs,
     stage,
+    near,
+    next_x,
     send_sems,
     recv_sems,
     load_sems,
 ):
     z, y, x, c = place()
     me = z * 2 + y
+    me_n = x * 2 + c
     count, cap, width = a_ref.shape
     parts = win_ref.shape[0]
     wide = win_ref.shape[2]
@@ -1095,11 +1199,14 @@
         loads.start(a, b)
         for a, b in (
             (act_hbm.at[me], a_ref.at[me]),
-            (win_hbm, win_ref),
-            (whid_hbm, whid_ref),
+            (own_in_hbm, win_ref.at[me_n]),
+            (own_hid_hbm, whid_ref.at[me_n]),
             (dy_hbm, dy_ref),
         )
     ]
+    for i in range(1, parts):
+        n = lax.rem(me_n + i, parts)
+        first += [loads.start(win_hbm.at[n], win_ref.at[n]), loads.start(whid_hbm.at[n], whid_ref.at[n])]
 
     def partner(k):
         zz, yy = flipped(z, y, k)
@@ -1127,7 +1234,8 @@
             device_id_type=MESH,
         )
 
-    greet([partner(k)[1] for k in range(1, 8)])
+    core, xpeer = device(z, y, x, 1 - c), device(z, y, 1 - x, c)
+    greet([partner(k)[1] for k in range(1, 8)] + [core, xpeer])
     for k in FLIPS:
         outward(k).start()
     for copy in first:
@@ -1174,24 +1282,48 @@
     own = loads.start(da_ref.at[me], ret_hbm.at[me])
 
     def put(i, out):
-        return pltpu.make_async_copy(stage.at[lax.rem(i, 2)], out, load_sems.at[8 + lax.rem(i, 2)])
+        return pltpu.make_async_copy(stage.at[i], out, load_sems.at[16 + i])
+
+    def third(i, src, dst, to):
+        return pltpu.make_async_remote_copy(
+            src_ref=src,
+            dst_ref=dst,
+            send_sem=send_sems.at[16 + i],
+            recv_sem=recv_sems.at[16 + i],
+            device_id=to,
+            device_id_type=MESH,
+        )
 
     acts = a_ref[...].reshape(count * cap, width)
-    dys = dy_ref[...].reshape(count * cap, width)
 
     @pl.loop(0, parts)
     def _(j):
         cols = pl.ds(pl.multiple_of(j * wide, wide), wide)
-
-        @pl.when(j >= 1)
-        def _():
-            put(0, gin_hbm.at[j - 1]).wait()
-            put(1, ghid_hbm.at[j - 1]).wait()
-
-        stage[0] = t_dot(acts, du_ref[:, cols]).astype(BF16)
-        put(0, gin_hbm.at[j]).start()
-        stage[1] = t_dot(g_ref[:, cols], dys).astype(BF16)
-        put(1, ghid_hbm.at[j]).start()
+        win_ref[j] = t_dot(acts, du_ref[:, cols]).astype(BF16)
+
+    to_core = [third(xx, win_ref.at[xx * 2 + 1 - c], near.at[xx], core) for xx in range(2)]
+    for copy in to_core:
+        copy.start()
+
+    @pl.loop(0, parts // 2)
+    def _(jj):
+        for i in range(2):
+            j = 2 * jj + i
+            cols = pl.ds(pl.multiple_of(j * wide, wide), wide)
+
+            @pl.when(jj >= 1)
+            def _():
+                put(i, ghid_hbm.at[j - 2]).wait()
+
+            stage[i] = t_dot(g_ref[:, cols], dy_ref[...].reshape(count * cap, width)).astype(BF16)
+            put(i, ghid_hbm.at[j]).start()
+
+    for copy in to_core:
+        copy.wait()
+    other = (1 - x) * 2 + c
+    win_ref[other] = (win_ref[other].astype(F32) + near[1 - x].astype(F32)).astype(BF16)
+    to_x = third(2, win_ref.at[other], next_x, xpeer)
+    to_x.start()
 
     @pl.loop(0, count)
     def _(i):
@@ -1199,16 +1331,22 @@
         a_ref[i] = dot(g_ref[rows, :], whid_ref[...].reshape(parts * wide, width)).astype(BF16)
 
     out = loads.start(a_ref, y_hbm)
-    put(0, gin_hbm.at[parts - 1]).wait()
-    put(1, ghid_hbm.at[parts - 1]).wait()
+    for i in range(2):
+        put(i, ghid_hbm.at[parts - 2 + i]).wait()
+    to_x.wait()
+    tiles = []
+    for i, tile in enumerate((us.at[0], us.at[1], gs.at[0])):
+        rows = pl.ds(i * cap, cap)
+        tile[...] = win_ref[me_n, rows].astype(F32) + near[x, rows].astype(F32) + next_x[rows].astype(F32)
+        tiles.append(loads.start(tile, gin_hbm.at[rows]))
     for k in range(1, 8):
         outward(k).wait_send()
         homeward(k).wait()
-    own.wait()
-    out.wait()
-
-
-def swap(act_slots, dy_rows, w_in, w_hid):
+    for copy in tiles + [own, out]:
+        copy.wait()
+
+
+def swap(act_slots, dy_rows, w_in, w_hid, own_in, own_hid):
     count, cap, width = act_slots.shape
     parts, _, wide = w_in.shape
     hidden = parts * wide
@@ -1218,10 +1356,10 @@
         out_shape=(
             jax.ShapeDtypeStruct((count, cap, width), BF16),
             jax.ShapeDtypeStruct((count, cap, width), BF16),
-            jax.ShapeDtypeStruct((parts, width, wide), BF16),
+            jax.ShapeDtypeStruct((width, wide), F32),
             jax.ShapeDtypeStruct((parts, wide, width), BF16),
         ),
-        in_specs=[any_spec] * 4,
+        in_specs=[any_spec] * 6,
         out_specs=(any_spec,) * 4,
         scratch_shapes=[
             pltpu.VMEM((count, cap, width), BF16),
@@ -1234,13 +1372,15 @@
             pltpu.VMEM((2, cap, wide), F32),
             pltpu.VMEM((2, cap, wide), F32),
             pltpu.VMEM((2, width, wide), BF16),
-            pltpu.SemaphoreType.DMA((16,)),
-            pltpu.SemaphoreType.DMA((16,)),
-            pltpu.SemaphoreType.DMA((10,)),
+            pltpu.VMEM((2, width, wide), BF16),
+            pltpu.VMEM((width, wide), BF16),
+            pltpu.SemaphoreType.DMA((20,)),
+            pltpu.SemaphoreType.DMA((20,)),
+            pltpu.SemaphoreType.DMA((18,)),
         ],
         compiler_params=pltpu.CompilerParams(vmem_limit_bytes=62 << 20, collective_id=1, has_side_effects=True),
         cost_estimate=pl.CostEstimate(flops=100 << 30, bytes_accessed=60 << 20, transcendentals=0),
-    )(act_slots, dy_rows, w_in, w_hid)
+    )(act_slots, dy_rows, w_in, w_hid, own_in, own_hid)
 
 
 def local(tokens, segments, routes, gate_logit, w_qkv, w_out, norm_gains, w_in, w_hid, cotangent):
@@ -1257,15 +1397,22 @@
         halves = halves.transpose(2, 0, 1, 3).reshape(2, share, 2 * width)
         gain_cols = jnp.broadcast_to(jnp.pad(norm_gains.T, ((0, 0), (0, 126))), (2, share, 128))
         shard = jnp.concatenate((halves, gain_cols), axis=2).astype(F32)
-        segr = segments.reshape(1, tok_count)
-        segc = segments.reshape(tok_count, 1)
-        qkv, context, hidden, act_slots, w_blocks, dy_rows, w_in_all, w_hid_all, stats, scol, gains = head(
-            tokens, cotangent, shard, w_in[0], w_hid[0], routes, gate_logit, segr, segc, n_expert, capacity
+        listed = jnp.concatenate(
+            (
+                routes.reshape(1, tok_count).astype(F32),
+                gate_logit.reshape(1, tok_count),
+                segments.reshape(1, tok_count).astype(F32),
+                jnp.zeros((5, tok_count), F32),
+            )
         )
-        da_back, y_rows, gin, ghid = swap(act_slots, dy_rows, w_in_all, w_hid_all)
-        grad_tokens, y_back, _r1, _r2, gin_own, ghid_own, own, gg = tail(
+        qkv, context, hidden, act_slots, w_blocks, dy_rows, w_in_all, w_hid_all, stats, cols, gains = head(
+            tokens, cotangent, shard, w_in[0], w_hid[0], listed, n_expert, capacity
+        )
+        da_back, y_rows, gin_own, ghid = swap(act_slots, dy_rows, w_in_all, w_hid_all, w_in[0], w_hid[0])
+        grad_tokens, _r1, _r2, ghid_own, block_out, own, gg = tail(
             da_back.reshape(slot_rows, width),
-            scol,
+            cols,
+            listed,
             tokens,
             cotangent,
             hidden,
@@ -1274,19 +1421,16 @@
             stats,
             w_blocks,
             gains,
-            segr,
-            segc,
             y_rows,
-            gin,
             ghid,
         )
-        block_out = block_output(y_back.reshape(slot_rows, width), scol, hidden, gate_logit)
         me = lax.axis_index("expert") * n_narrow + lax.axis_index("narrow")
+        heads = own[1:].reshape(6, share, 3, 128).transpose(1, 2, 0, 3)
         return (
             block_out,
             grad_tokens,
-            own[:3].transpose(1, 0, 2).reshape(share, 3 * width),
-            own[3],
+            heads.reshape(share, 3 * width),
+            own[0].transpose(1, 0, 2).reshape(share, width),
             lax.dynamic_slice_in_dim(gg[:2], me * share, share, axis=1),
             gin_own[None],
             ghid_own[None],

time: 437 us -> 387 us (0.89)
  Pallas kernels: 414 us -> 362 us
    pallas_call x1, Pallas kernels: 149 us -> 107 us  [head(): pl.pallas_call(functools.partial(head_kernel, capacity, experts), out_sha...]
    pallas_call x1, Pallas kernels: 131 us -> 124 us  [tail(): pl.pallas_call(tail_kernel, out_shape=(jax.ShapeDtypeStruct((tokens, widt...]
    pallas_call x1 -> x0, Pallas kernels: 4.88 us -> none  [block_output(): pl.pallas_call(out_kernel, grid=(tokens // BLOCK,), out_shape=jax.ShapeDt...]
    unnamed x20 -> x12, local copies, waits for them, and re-layouts: 14.1 us -> 11 us
where the time goes in v4:
time: 387 us; the launch traced here: 385 us
  Pallas kernels  362 us (94%)
  local copies, waits for them, and re-layouts  17.1 us (4%)
  other arithmetic  4.43 us (1%)
    pallas_call x1, Pallas kernels, swap(): pl.pallas_call(swap_kernel, out_shape=(jax.ShapeDtypeStruct((count, cap,...  132 us
    pallas_call x1, Pallas kernels, tail(): pl.pallas_call(tail_kernel, out_shape=(jax.ShapeDtypeStruct((tokens, widt...  124 us
    pallas_call x1, Pallas kernels, head(): pl.pallas_call(functools.partial(head_kernel, capacity, experts), out_sha...  107 us
    unnamed x12, local copies, waits for them, and re-layouts  11 us

profile of v4, /device:TPU:0, one launch (start us, length us, event | category | flops | bytes accessed | tf_op | source)
XLA Modules:
  0.0 384.7 jit_solution(11136792810905014041)
XLA Ops:
  0.6 0.7 convert_bitcast_fusion
  1.3 0.7 convert_element_type.25
  2.0 0.1 pad.8.clone
  2.1 1.4 maximum_maximum_fusion.row_ref
  3.5 0.9 pad_maximum_fusion
  4.4 0.1 reshape.49
  4.5 0.1 copy.27
  4.6 0.1 reshape.50
  4.6 0.7 copy.24
  5.4 0.7 maximum_convert_fusion.shard_hbm
  6.1 107.2 %shard_map.153 = (bf16[1024,2304]{1,0:T(8,128)(2,1)}, bf16[1024,768]{1,0:T(8,128)(2,1)}, f32[1024,768]{1,0:T(8,128)}, bf16[8,256,768]{2,1,0:T(8,128)(2,1)}, bf16...) custom-call(bf16[1024,768]{1,0:T(8,128)(2,1)} %x_hbm.3, ...), custom_call_target="tpu_custom_call" | custom-call | flops 64424509440 | bytes 41943040 | tf_op jit(solution)/shard_map/pallas_call | solution.py:691
  113.3 131.6 %shard_map.154 = (bf16[8,256,768]{2,1,0:T(8,128)(2,1)}, bf16[8,256,768]{2,1,0:T(8,128)(2,1)}, f32[768,768]{1,0:T(8,128)}, bf16[4,768,768]{2,1,0:T(8,128)(2,1)}) custom-call(bf16[8,256,768]{2,1,0:T(8,128)(2,1)} %get-tuple-element.27.act_hbm, bf16[8,256,768]{2,1,0:T(8,128)(2,1)} %get-tuple-element.28.dy_hbm, bf16[4,768,768]{2,1,0:T(8,128)(2,1)} %get-tuple-element.29.win_hbm, ...), custom_call_target="tpu_custom_call" | custom-call | flops 107374182400 | bytes 62914560 | tf_op jit(solution)/shard_map/pallas_call | solution.py:1354
  244.9 123.7 %shard_map.155 = (f32[1024,768]{1,0:T(8,128)}, bf16[2,768,768]{2,1,0:T(8,128)(2,1)}, bf16[768,768]{1,0:T(8,128)(2,1)}, f32[768,768]{1,0:T(8,128)}, bf16[1024,768...) custom-call(bf16[2048,768]{1,0:T(8,128)(2,1)} %bitcast.32, bf16[1024,768]{1,0:T(8,128)(2,1)} %x_hbm.3, ...), custom_call_target="tpu_custom_call" | custom-call | flops 85899345920 | bytes 41943040 | tf_op jit(solution)/shard_map/pallas_call | solution.py:1105
  368.6 1.0 slice.9
  369.5 0.1 reshape.53
  369.6 0.0 copy-start
  369.7 0.8 copy.22
  370.5 1.9 reshape.54
  372.4 0.9 slice_bitcast_fusion
  373.3 0.6 copy.25
  373.9 0.7 slice.11
  374.7 0.6 constant_dynamic-slice_fusion
  375.3 2.7 copy.32
  377.9 0.0 copy-done
  377.9 0.0 copy-start.1
  378.0 1.7 copy.33
  379.6 1.1 copy-done.1
  380.8 0.0 copy-start.2
  380.8 1.4 copy.34
  382.2 1.1 copy-done.2
  383.3 1.4 copy.35
  (3 shorter events, 0.0 us)
Async XLA Ops:
  369.6 8.3 %copy-start = (f32[1024,768]{1,0:T(8,128)S(1)}, f32[1024,768]{1,0:T(8,128)}, u32[]{:S(2)}) copy-start(f32[1024,768]{1,0:T(8,128)} %get-tuple-element.55) | copy-start | bytes 9437188
  377.9 2.8 copy-start.1
  380.8 2.5 copy-start.2

commit v5 on v4

--- a/solution.py
+++ b/solution.py
@@ -447,17 +447,15 @@
     pl.semaphore_wait(barrier, len(peers))
 
 
-FLIPS = (1, 2, 3, 4, 5, 6, 7)
+FLIPS = (4, 2, 6, 1, 5, 3, 7)
 
 
 def peers_of(z, y, x, c):
     return [device(across(z, k >> 1), 1 - y if k & 1 else y, x, c) for k in FLIPS]
 
 
-def weight(blocks, first, count):
-    half = blocks.shape[-1]
-    rows = blocks.shape[1] * blocks.shape[2] * blocks.shape[3] * blocks.shape[4]
-    return jnp.concatenate([blocks[b].reshape(rows, half) for b in range(first, first + count)], axis=1)
+def weight(ref, lo, hi):
+    return ref[:, :, :, :, lo:hi].reshape(-1, hi - lo)
 
 
 def head_kernel(
@@ -465,10 +463,12 @@
     experts,
     x_hbm,
     ct_hbm,
-    shard_hbm,
     win_hbm,
     whid_hbm,
     row_ref,
+    wqkv_ref,
+    wout_ref,
+    gshard_ref,
     qkv_hbm,
     c_hbm,
     h_hbm,
@@ -482,7 +482,9 @@
     gain_ref,
     x_ref,
     ct_ref,
+    sh,
     st,
+    square,
     wq,
     wg,
     qkv_ref,
@@ -509,10 +511,19 @@
     loads = Loads(load_sems)
     loading_ct = loads.start(ct_hbm, ct_ref)
     loading_x = loads.start(x_hbm, x_ref)
-    own_shard = loads.start(shard_hbm.at[c], st.at[c])
+
+    square[...] = jnp.zeros_like(square)
+    square[0:2, 0 : gshard_ref.shape[1]] = gshard_ref[...].astype(F32)
+    gain_cols = square[...].T
+    for side in range(2):
+        for j in range(4):
+            src, at = (wqkv_ref, j * width) if j < 3 else (wout_ref, 0)
+            sh[side, :, j * half : (j + 1) * half] = src[:, at + side * half : at + (side + 1) * half].astype(F32)
+        sh[side, :, 4 * half :] = gain_cols[0 : gshard_ref.shape[1], :]
+    st[c] = sh[c]
 
     greet(peers_of(z, y, x, c) + [core, xpeer])
-    zero = links.push(shard_hbm.at[1 - c], st.at[c], core)
+    zero = links.push(sh.at[1 - c], st.at[c], core)
 
     deep = width // 2
     upper, lower = pl.ds(0, deep), pl.ds(deep, deep)
@@ -533,11 +544,13 @@
     base = (iota((wide, tokens), 0) * capacity).astype(F32)
     srow = jnp.sum(hot * (rank + base), axis=0, keepdims=True)
 
+    def cols(j):
+        return pl.ds(pl.multiple_of((2 * j + c) * half, 128), half)
+
     zero.wait()
-    own_shard.wait()
     rows48 = jnp.concatenate((st[0], st[1]), axis=0)
     for j in range(4):
-        wq[2 * j + c, z, y, x] = rows48[:, j * half : (j + 1) * half].astype(BF16)
+        wq[z, y, x, :, cols(j)] = rows48[:, j * half : (j + 1) * half].astype(BF16)
     wg[z, y, x] = rows48[:, 4 * half :].astype(BF16)
     ring_z = []
     for piece in range(2):
@@ -545,7 +558,7 @@
         for k in (1, 2, 3):
             to = device(across(z, k), y, x, c)
             for j in (2 * piece, 2 * piece + 1):
-                part = wq.at[2 * j + c, z, y, x]
+                part = wq.at[z, y, x, :, cols(j)]
                 group.append(links.push(part, part, to))
             if piece == 0:
                 group.append(links.push(wg.at[z, y, x], wg.at[z, y, x], to))
@@ -568,31 +581,31 @@
     loading_ct.wait()
     fill((jax.nn.sigmoid(listed[:, 1:2]) * ct_ref[...].astype(F32)).astype(BF16), dy_ref)
 
+    ring_2 = []
+    for piece in range(2):
+        for copy in ring_z[piece]:
+            copy.wait()
+        ca, cb = cols(2 * piece), cols(2 * piece + 1)
+        group = [
+            links.push(wq.at[:, y, x, :, ca], wq.at[:, y, x, :, ca], ypeer),
+            links.push(wq.at[:, y, x, :, cb], wq.at[:, y, x, :, cb], xpeer),
+        ]
+        if piece == 0:
+            group.append(links.push(wg.at[:, y, x], wg.at[:, y, x], ypeer))
+        ring_2.append(group)
     dy_copies = []
     for k in FLIPS:
         zz, yy = across(z, k >> 1), (1 - y if k & 1 else y)
         dy_copies.append(links.push(dy_ref.at[zz * 2 + yy], dyrow_hbm.at[me_e], device(zz, yy, x, c)))
     own_dy = loads.start(dy_ref.at[me_e], dyrow_hbm.at[me_e])
-    ring_2 = []
-    for piece in range(2):
-        for copy in ring_z[piece]:
-            copy.wait()
-        ja, jb = 2 * (2 * piece) + c, 2 * (2 * piece + 1) + c
-        group = [
-            links.push(wq.at[ja, :, y, x], wq.at[ja, :, y, x], ypeer),
-            links.push(wq.at[jb, :, y, x], wq.at[jb, :, y, x], xpeer),
-        ]
-        if piece == 0:
-            group.append(links.push(wg.at[:, y, x], wg.at[:, y, x], ypeer))
-        ring_2.append(group)
     ring_3 = []
     for piece in range(2):
         for copy in ring_2[piece]:
             copy.wait()
-        ja, jb = 2 * (2 * piece) + c, 2 * (2 * piece + 1) + c
+        ca, cb = cols(2 * piece), cols(2 * piece + 1)
         group = [
-            links.push(wq.at[ja, :, :, x], wq.at[ja, :, :, x], xpeer),
-            links.push(wq.at[jb, :, y], wq.at[jb, :, y], ypeer),
+            links.push(wq.at[:, :, x, :, ca], wq.at[:, :, x, :, ca], xpeer),
+            links.push(wq.at[:, y, :, :, cb], wq.at[:, y, :, :, cb], ypeer),
         ]
         if piece == 0:
             group.append(links.push(wg.at[:, :, x], wg.at[:, :, x], xpeer))
@@ -603,7 +616,7 @@
     for piece in range(2):
         for copy in ring_3[piece]:
             copy.wait()
-        ring_4.append([links.push(wq.at[2 * j + c], wq.at[2 * j + c], core) for j in (2 * piece, 2 * piece + 1)])
+        ring_4.append([links.push(wq.at[:, :, :, :, cols(j)], wq.at[:, :, :, :, cols(j)], core) for j in (2 * piece, 2 * piece + 1)])
 
     gains = jnp.transpose(wg[...].reshape(width, 128).astype(F32))[0:8, :]
     gain_ref[...] = gains
@@ -628,7 +641,7 @@
         rows = pl.ds(pl.multiple_of(i * BLOCK, BLOCK), BLOCK)
         normed, _f = normalize(x_ref[rows, :].astype(F32))
         act = (normed * gain_one).astype(BF16)
-        qkv_ref[rows, :] = dot(act, weight(wq, 0, 6)).astype(BF16)
+        qkv_ref[rows, :] = dot(act, weight(wq, 0, 3 * width)).astype(BF16)
 
     storing.append(loads.start(qkv_ref, qkv_hbm))
     col_scr[...] = jnp.zeros_like(col_scr)
@@ -668,7 +681,7 @@
     @pl.loop(0, blocks)
     def _(i):
         rows = pl.ds(pl.multiple_of(i * BLOCK, BLOCK), BLOCK)
-        hidden = x_ref[rows, :].astype(F32) + dot(c_ref[rows, :], weight(wq, 6, 2))
+        hidden = x_ref[rows, :].astype(F32) + dot(c_ref[rows, :], weight(wq, 3 * width, 4 * width))
         h_ref[rows, :] = hidden
         normed, _f = normalize(hidden)
         a_scr[rows, :] = (normed * gain_two).astype(BF16)
@@ -682,12 +695,13 @@
         copy.wait()
 
 
-def head(tokens_in, cotangent, shard, w_in, w_hid, listed, experts, capacity):
+def head(tokens_in, cotangent, w_in, w_hid, listed, w_qkv, w_out, gain_shard, experts, capacity):
     tokens, width = tokens_in.shape
     any_spec = pl.BlockSpec(memory_space=pl.ANY)
     vmem = pl.BlockSpec(memory_space=pltpu.VMEM)
     slots = (experts, capacity, width)
-    blocks = (8, 4, 2, 2, 48, width // 2)
+    blocks = (4, 2, 2, 48, 4 * width)
+    shard = (2, w_qkv.shape[0], 2 * width + 128)
     return pl.pallas_call(
         functools.partial(head_kernel, capacity, experts),
         out_shape=(
@@ -703,12 +717,14 @@
             jax.ShapeDtypeStruct((tokens, 8), F32),
             jax.ShapeDtypeStruct((8, width), F32),
         ),
-        in_specs=[any_spec] * 5 + [vmem],
+        in_specs=[any_spec] * 4 + [vmem] * 4,
         out_specs=(any_spec,) * 8 + (vmem,) * 3,
         scratch_shapes=[
             pltpu.VMEM((tokens, width), BF16),
             pltpu.VMEM((tokens, width), BF16),
-            pltpu.VMEM(shard.shape, F32),
+            pltpu.VMEM(shard, F32),
+            pltpu.VMEM(shard, F32),
+            pltpu.VMEM((128, 128), F32),
             pltpu.VMEM(blocks, BF16),
             pltpu.VMEM((4, 2, 2, 48, 128), BF16),
             pltpu.VMEM((tokens, 3 * width), BF16),
@@ -725,7 +741,7 @@
         ],
         compiler_params=pltpu.CompilerParams(vmem_limit_bytes=62 << 20, collective_id=0, has_side_effects=True),
         cost_estimate=pl.CostEstimate(flops=60 << 30, bytes_accessed=40 << 20, transcendentals=0),
-    )(tokens_in, cotangent, shard, w_in, w_hid, listed)
+    )(tokens_in, cotangent, w_in, w_hid, listed, w_qkv, w_out, gain_shard)
 
 
 class Reduce:
@@ -860,7 +876,8 @@
     r2_hbm,
     gw_out,
     out_hbm,
-    own_ref,
+    ownq_ref,
+    owno_ref,
     gg_ref,
     ret_ref,
     x_ref,
@@ -913,9 +930,23 @@
 
     first = [
         loads.start(a, b)
-        for a, b in ((ret_hbm, ret_ref), (h_hbm, h_ref), (ct_hbm, ct_ref), (c_hbm, c_ref), (w_hbm, w_ref), (x_hbm, x_ref))
+        for a, b in (
+            (ret_hbm, ret_ref),
+            (h_hbm, h_ref),
+            (w_hbm.at[:, :, :, :, pl.ds(3 * width, width)], w_ref.at[:, :, :, :, pl.ds(3 * width, width)]),
+            (ct_hbm, ct_ref),
+            (c_hbm, c_ref),
+        )
     ]
-    second = [loads.start(qkv_hbm, qkv_ref), loads.start(yrow_hbm.at[me_e], yback.at[me_e])]
+    second = [
+        loads.start(a, b)
+        for a, b in (
+            (x_hbm, x_ref),
+            (qkv_hbm, qkv_ref),
+            (w_hbm.at[:, :, :, :, pl.ds(0, 3 * width)], w_ref.at[:, :, :, :, pl.ds(0, 3 * width)]),
+            (yrow_hbm.at[me_e], yback.at[me_e]),
+        )
+    ]
     greet(far + [core, xpeer])
 
     w_copies = [links.push(gw_hbm.at[xx * 2 + 1 - c], r1_hbm.at[xx], core) for xx in range(2)]
@@ -941,7 +972,7 @@
         gt_ref[rows, :] = dh
         dhb = dh.astype(BF16)
         dhb_scr[rows, :] = dhb
-        dc = dot_t(dhb, weight(w_ref, 6, 2)).astype(BF16)
+        dc = dot_t(dhb, weight(w_ref, 3 * width, 4 * width)).astype(BF16)
         dc_scr[rows, :] = dc
         d_scr[:, rows] = lax.dot_general(
             member,
@@ -963,7 +994,18 @@
 
     for copy in w_copies:
         copy.wait()
-    x_copies = []
+
+    def to_x(i):
+        rows = pl.ds(pl.multiple_of(i * (width // 4), width // 4), width // 4)
+        return pltpu.make_async_remote_copy(
+            src_ref=nsum.at[0, rows],
+            dst_ref=r2_hbm.at[rows],
+            send_sem=send_sems.at[16 + i],
+            recv_sem=recv_sems.at[16 + i],
+            device_id=xpeer,
+            device_id_type=MESH,
+        )
+
     for step in range(2):
         xx = 1 - x if step == 0 else x
         la = loads.start(gw_hbm.at[xx * 2 + c], na)
@@ -972,7 +1014,10 @@
         lb.wait()
         nsum[step] = (na[...].astype(F32) + nb[...].astype(F32)).astype(BF16)
         if step == 0:
-            x_copies.append(links.push(nsum.at[0], r2_hbm, xpeer))
+            to_x(0).start()
+
+    for copy in second:
+        copy.wait()
 
     @pl.loop(0, blocks)
     def _(i):
@@ -981,8 +1026,6 @@
         dhb_scr[rows, :] = (normed * gain_one).astype(BF16)
 
     actt_scr[...] = dhb_scr[...].T
-    for copy in second:
-        copy.wait()
     low = iota((BLOCK, 128), 1) < HEAD_DIM
     scale = HEAD_DIM**-0.5
 
@@ -1038,11 +1081,13 @@
         def _():
             reduce(t - 2).step(3)
 
+        to_x(t + 1).start()
+
     @pl.loop(0, blocks)
     def _(i):
         rows = pl.ds(pl.multiple_of(i * BLOCK, BLOCK), BLOCK)
         normed, factor = normalize(x_ref[rows, :].astype(F32))
-        dn = dot_t(dqkv_scr[rows, :], weight(w_ref, 0, 6))
+        dn = dot_t(dqkv_scr[rows, :], weight(w_ref, 0, 3 * width))
         ggs[0, 0:1, :] += jnp.sum(dn * normed, axis=0, keepdims=True)
         gt_ref[rows, :] += norm_back(dn * gain_one, normed, factor)
 
@@ -1079,19 +1124,34 @@
     gains_copy.wait()
     ggs[3] = ggs[2] + rg[2]
     gain_copies = [links.push(ggs.at[3], rg.at[2 + k], device(across(z, k), y, x, c)) for k in (1, 2, 3)]
-    for copy in x_copies:
-        copy.wait()
+    for i in range(4):
+        to_x(i).wait()
     lb = loads.start(r2_hbm, nb)
     lb.wait()
     gw_out[...] = nsum[1].astype(F32) + nb[...].astype(F32)
     reduce(3).step(4)
     for copy in gain_copies:
         copy.wait()
-    gg_ref[...] = ggs[3] + rg[3] + rg[4] + rg[5]
+    share = width // 32
+    mine = ((z * 2 + y) * 2 + x) * 2 + c
+    take = (iota((width, 128), 0) == mine * share + iota((width, 128), 1)).astype(F32)
+    gg_ref[...] = lax.dot_general(
+        ggs[3] + rg[3] + rg[4] + rg[5],
+        take,
+        (((1,), (0,)), ((), ())),
+        precision=lax.Precision.HIGHEST,
+        preferred_element_type=F32,
+    )[0:2, 0:share]
     for ph in range(4):
-        own_ref[ph, c] = fin[ph, pl.ds(pl.multiple_of(c * 24, 8), 24), :]
+        kept = fin[ph, pl.ds(pl.multiple_of(c * 24, 8), 24), :]
         reduce(ph).four().wait()
-        own_ref[ph, 1 - c] = q4[ph]
+        for owner, part in ((c, kept), (1 - c, q4[ph])):
+            if ph == 0:
+                owno_ref[:, pl.ds(pl.multiple_of(owner * half, 128), half)] = part
+            else:
+                for j in range(3):
+                    at = pl.multiple_of(j * width + (2 * (ph - 1) + owner) * 128, 128)
+                    ownq_ref[:, pl.ds(at, 128)] = part[:, j * 128 : (j + 1) * 128]
     for copy in stores:
         copy.wait()
 
@@ -1110,11 +1170,12 @@
             jax.ShapeDtypeStruct(gw.shape[1:], BF16),
             jax.ShapeDtypeStruct(gw.shape[1:], F32),
             jax.ShapeDtypeStruct((tokens, width), BF16),
-            jax.ShapeDtypeStruct((4, 2, 24, half), F32),
-            jax.ShapeDtypeStruct((8, width), F32),
+            jax.ShapeDtypeStruct((24, 3 * width), F32),
+            jax.ShapeDtypeStruct((24, width), F32),
+            jax.ShapeDtypeStruct((2, 24), F32),
         ),
         in_specs=[any_spec] * 9 + [vmem] * 4,
-        out_specs=(any_spec, any_spec, any_spec, vmem, any_spec, vmem, vmem),
+        out_specs=(any_spec, any_spec, any_spec, vmem, any_spec, vmem, vmem, vmem),
         scratch_shapes=[
             pltpu.VMEM((slots, width), BF16),
             pltpu.VMEM((tokens, width), BF16),
@@ -1392,11 +1453,6 @@
     everyone = ("expert", "narrow")
 
     if n_expert == 8 and n_narrow == 4:
-        share = w_qkv.shape[0]
-        halves = jnp.concatenate((w_qkv, w_out), axis=1).reshape(share, 4, 2, width // 2)
-        halves = halves.transpose(2, 0, 1, 3).reshape(2, share, 2 * width)
-        gain_cols = jnp.broadcast_to(jnp.pad(norm_gains.T, ((0, 0), (0, 126))), (2, share, 128))
-        shard = jnp.concatenate((halves, gain_cols), axis=2).astype(F32)
         listed = jnp.concatenate(
             (
                 routes.reshape(1, tok_count).astype(F32),
@@ -1406,10 +1462,10 @@
             )
         )
         qkv, context, hidden, act_slots, w_blocks, dy_rows, w_in_all, w_hid_all, stats, cols, gains = head(
-            tokens, cotangent, shard, w_in[0], w_hid[0], listed, n_expert, capacity
+            tokens, cotangent, w_in[0], w_hid[0], listed, w_qkv, w_out, norm_gains, n_expert, capacity
         )
         da_back, y_rows, gin_own, ghid = swap(act_slots, dy_rows, w_in_all, w_hid_all, w_in[0], w_hid[0])
-        grad_tokens, _r1, _r2, ghid_own, block_out, own, gg = tail(
+        grad_tokens, _r1, _r2, ghid_own, block_out, own_qkv, own_out, own_gains = tail(
             da_back.reshape(slot_rows, width),
             cols,
             listed,
@@ -1424,14 +1480,12 @@
             y_rows,
             ghid,
         )
-        me = lax.axis_index("expert") * n_narrow + lax.axis_index("narrow")
-        heads = own[1:].reshape(6, share, 3, 128).transpose(1, 2, 0, 3)
         return (
             block_out,
             grad_tokens,
-            heads.reshape(share, 3 * width),
-            own[0].transpose(1, 0, 2).reshape(share, width),
-            lax.dynamic_slice_in_dim(gg[:2], me * share, share, axis=1),
+            own_qkv,
+            own_out,
+            own_gains,
             gin_own[None],
             ghid_own[None],
         )

time: 387 us -> 351 us (0.907)
  Pallas kernels: 362 us -> 337 us
  local copies, waits for them, and re-layouts: 17.1 us -> 10.4 us
    pallas_call x1, Pallas kernels: 124 us -> 106 us  [tail(): pl.pallas_call(tail_kernel, out_shape=(jax.ShapeDtypeStruct((tokens, widt...]
    pallas_call x1, Pallas kernels: 107 us -> 96.3 us  [head(): pl.pallas_call(functools.partial(head_kernel, capacity, experts), out_sha...]
    unnamed x12 -> x19, local copies, waits for them, and re-layouts: 11 us -> 10.3 us
where the time goes in v5:
time: 351 us
  Pallas kernels  337 us (96%)
  local copies, waits for them, and re-layouts  10.4 us (3%)
    pallas_call x1, Pallas kernels, swap(): pl.pallas_call(swap_kernel, out_shape=(jax.ShapeDtypeStruct((count, cap,...  135 us
    pallas_call x1, Pallas kernels, tail(): pl.pallas_call(tail_kernel, out_shape=(jax.ShapeDtypeStruct((tokens, widt...  106 us
    pallas_call x1, Pallas kernels, head(): pl.pallas_call(functools.partial(head_kernel, capacity, experts), out_sha...  96.3 us
    unnamed x19, local copies, waits for them, and re-layouts  10.3 us

profile of v5, /device:TPU:0, one launch (start us, length us, event | category | flops | bytes accessed | tf_op | source)
XLA Modules:
  0.0 350.8 jit_solution(1235452706141605304)
XLA Ops:
  0.6 0.1 pad.3.clone
  0.7 0.7 convert_element_type.19
  1.4 0.7 convert_bitcast_fusion
  2.1 1.4 maximum_maximum_fusion.row_ref
  3.5 96.3 %shard_map.153 = (bf16[1024,2304]{1,0:T(8,128)(2,1)}, bf16[1024,768]{1,0:T(8,128)(2,1)}, f32[1024,768]{1,0:T(8,128)}, bf16[8,256,768]{2,1,0:T(8,128)(2,1)}, bf16...) custom-call(bf16[1024,768]{1,0:T(8,128)(2,1)} %x_hbm.3, ...), custom_call_target="tpu_custom_call" | custom-call | flops 64424509440 | bytes 41943040 | tf_op jit(solution)/shard_map/pallas_call | solution.py:705
  99.8 135.0 %shard_map.154 = (bf16[8,256,768]{2,1,0:T(8,128)(2,1)}, bf16[8,256,768]{2,1,0:T(8,128)(2,1)}, f32[768,768]{1,0:T(8,128)}, bf16[4,768,768]{2,1,0:T(8,128)(2,1)}) custom-call(bf16[8,256,768]{2,1,0:T(8,128)(2,1)} %get-tuple-element.28.act_hbm, bf16[8,256,768]{2,1,0:T(8,128)(2,1)} %get-tuple-element.29.dy_hbm, bf16[4,768,768]{2,1,0:T(8,128)(2,1)} %get-tuple-element.30.win_hbm, ...), custom_call_target="tpu_custom_call" | custom-call | flops 107374182400 | bytes 62914560 | tf_op jit(solution)/shard_map/pallas_call | solution.py:1415
  234.8 105.7 %shard_map.155 = (f32[1024,768]{1,0:T(8,128)}, bf16[2,768,768]{2,1,0:T(8,128)(2,1)}, bf16[768,768]{1,0:T(8,128)(2,1)}, f32[768,768]{1,0:T(8,128)}, bf16[1024,768...) custom-call(bf16[2048,768]{1,0:T(8,128)(2,1)} %bitcast.15, bf16[1024,768]{1,0:T(8,128)(2,1)} %x_hbm.3, ...), custom_call_target="tpu_custom_call" | custom-call | flops 85899345920 | bytes 41943040 | tf_op jit(solution)/shard_map/pallas_call | solution.py:1165
  340.5 0.0 copy-start
  340.5 2.8 copy.24
  343.3 0.0 copy-done
  343.3 0.0 copy-start.3
  343.3 0.0 copy-start.4
  343.3 0.0 copy-start.5
  343.3 0.0 copy-start.1
  343.4 1.7 copy.25
  345.0 0.0 copy-done.3
  345.0 0.7 copy.26
  345.7 0.0 copy-done.4
  345.7 0.6 copy.27
  346.4 0.0 copy-done.5
  346.4 0.6 copy.28
  346.9 0.0 copy-done.1
  346.9 0.0 copy-start.2
  346.9 1.4 copy.29
  348.3 1.1 copy-done.2
  349.4 1.4 copy.30
  (1 shorter events, 0.0 us)
Async XLA Ops:
  340.5 2.8 copy-start
  343.3 1.7 copy-start.3
  343.3 2.4 copy-start.4
  343.3 3.0 copy-start.5
  343.3 3.6 %copy-start.1 = (f32[768,768]{1,0:T(8,128)S(1)}, f32[768,768]{1,0:T(8,128)}, u32[]{:S(2)}) copy-start(f32[768,768]{1,0:T(8,128)} %get-tuple-element.47) | copy-start | bytes 7077892
  346.9 2.5 copy-start.2

commit v6 on v5

--- a/solution.py
+++ b/solution.py
@@ -494,7 +494,6 @@
     act_ref,
     dy_ref,
     bias_scr,
-    col_scr,
     send_sems,
     recv_sems,
     load_sems,
@@ -537,13 +536,6 @@
 
     parts = [(hand(win_hbm, win4_hbm, upper), win4_hbm, upper)]
 
-    wide = max(8, experts)
-    hot = (iota((wide, tokens), 0).astype(F32) == row_ref[0:1, :]).astype(F32)
-    before = (iota((tokens, tokens), 0) < iota((tokens, tokens), 1)).astype(BF16)
-    rank = dot(hot.astype(BF16), before)
-    base = (iota((wide, tokens), 0) * capacity).astype(F32)
-    srow = jnp.sum(hot * (rank + base), axis=0, keepdims=True)
-
     def cols(j):
         return pl.ds(pl.multiple_of((2 * j + c) * half, 128), half)
 
@@ -563,6 +555,13 @@
             if piece == 0:
                 group.append(links.push(wg.at[z, y, x], wg.at[z, y, x], to))
         ring_z.append(group)
+
+    wide = max(8, experts)
+    hot = (iota((wide, tokens), 0).astype(F32) == row_ref[0:1, :]).astype(F32)
+    before = (iota((tokens, tokens), 0) < iota((tokens, tokens), 1)).astype(BF16)
+    rank = dot(hot.astype(BF16), before)
+    base = (iota((wide, tokens), 0) * capacity).astype(F32)
+    srow = jnp.sum(hot * (rank + base), axis=0, keepdims=True)
 
     listed = row_ref[...].T
     hot_c = (iota((tokens, 128), 1).astype(F32) == listed[:, 0:1]).astype(F32)
@@ -644,39 +643,38 @@
         qkv_ref[rows, :] = dot(act, weight(wq, 0, 3 * width)).astype(BF16)
 
     storing.append(loads.start(qkv_ref, qkv_hbm))
-    col_scr[...] = jnp.zeros_like(col_scr)
     low = iota((BLOCK, 128), 1) < HEAD_DIM
-    for qb in range(blocks):
-        kb = max(0, qb - LOOKBACK)
-        span = (qb - kb + 1) * BLOCK
-        rows = pl.ds(qb * BLOCK, BLOCK)
-        keys = pl.ds(kb * BLOCK, span)
-        q_pos = iota((BLOCK, span), 0) + qb * BLOCK
-        k_pos = iota((BLOCK, span), 1) + kb * BLOCK
-        ok = (k_pos <= q_pos) & (col_ref[rows, 2:3] == row_ref[2:3, keys])
-        bias_scr[:, :span] = jnp.where(ok, 0.0, BIG_NEGATIVE)
-
-        @pl.loop(0, pairs)
-        def _(hp):
-            at = pl.multiple_of(hp * 128, 128)
+    tiles = [(qb, kb) for qb in range(blocks) for kb in range(max(0, qb - LOOKBACK), qb + 1)]
+    for n, (qb, kb) in enumerate(tiles):
+        ok = col_ref[pl.ds(kb * BLOCK, BLOCK), 2:3] == row_ref[2:3, pl.ds(qb * BLOCK, BLOCK)]
+        if kb == qb:
+            ok = ok & (iota((BLOCK, BLOCK), 0) <= iota((BLOCK, BLOCK), 1))
+        bias_scr[n] = jnp.where(ok, 0.0, BIG_NEGATIVE)
+
+    @pl.loop(0, pairs)
+    def _(hp):
+        at = pl.multiple_of(hp * 128, 128)
+        for qb in range(blocks):
+            mine = [(n, kb) for n, (qq, kb) in enumerate(tiles) if qq == qb]
+            rows = pl.ds(qb * BLOCK, BLOCK)
             q = qkv_ref[rows, pl.ds(at, 128)] * jnp.asarray(HEAD_DIM**-0.5, BF16)
-            k = qkv_ref[keys, pl.ds(width + at, 128)]
-            v = qkv_ref[keys, pl.ds(2 * width + at, 128)]
+            v = qkv_ref[pl.ds(mine[0][1] * BLOCK, len(mine) * BLOCK), pl.ds(2 * width + at, 128)]
             outs = []
-            col = col_scr[rows, :]
             for side in range(2):
-                mine = low if side == 0 else ~low
-                s = dot_t(jnp.where(mine, q, 0), k) + bias_scr[:, :span]
-                top = jnp.max(s, axis=1, keepdims=True)
-                raised = jnp.exp(s - top)
-                total = jnp.sum(raised, axis=1, keepdims=True)
-                outs.append(dot((raised * (1.0 / total)).astype(BF16), v))
-                col = jnp.where(iota((BLOCK, 128), 1) == 2 * hp + side, top + jnp.log(total), col)
-            col_scr[rows, :] = col
+                q_half = jnp.where(low, q, 0) if side == 0 else jnp.where(low, 0, q)
+                scores = [
+                    dot_t(qkv_ref[pl.ds(kb * BLOCK, BLOCK), pl.ds(width + at, 128)], q_half) + bias_scr[n] for n, kb in mine
+                ]
+                top = functools.reduce(jnp.maximum, [jnp.max(s, axis=0, keepdims=True) for s in scores])
+                raised = [jnp.exp(s - top) for s in scores]
+                total = functools.reduce(jnp.add, [jnp.sum(r, axis=0, keepdims=True) for r in raised])
+                share = 1.0 / total
+                weights = jnp.concatenate([(r * share).astype(BF16) for r in raised], axis=0)
+                outs.append(t_dot(weights, v))
+                stat_ref[pl.ds(2 * hp + side, 1), rows] = top + jnp.log(total)
             c_ref[rows, pl.ds(at, 128)] = jnp.where(low, outs[0], outs[1]).astype(BF16)
 
     storing.append(loads.start(c_ref, c_hbm))
-    stat_ref[...] = col_scr[...].T
 
     @pl.loop(0, blocks)
     def _(i):
@@ -713,7 +711,7 @@
             jax.ShapeDtypeStruct(slots, BF16),
             jax.ShapeDtypeStruct((4,) + w_in.shape, BF16),
             jax.ShapeDtypeStruct((4,) + w_hid.shape, BF16),
-            jax.ShapeDtypeStruct((128, tokens), F32),
+            jax.ShapeDtypeStruct((16, tokens), F32),
             jax.ShapeDtypeStruct((tokens, 8), F32),
             jax.ShapeDtypeStruct((8, width), F32),
         ),
@@ -733,8 +731,7 @@
             pltpu.VMEM((tokens, width), BF16),
             pltpu.VMEM(slots, BF16),
             pltpu.VMEM(slots, BF16),
-            pltpu.VMEM((BLOCK, (LOOKBACK + 1) * BLOCK), F32),
-            pltpu.VMEM((tokens, 128), F32),
+            pltpu.VMEM((tokens // BLOCK * (LOOKBACK + 1), BLOCK, BLOCK), F32),
             pltpu.SemaphoreType.DMA((48,)),
             pltpu.SemaphoreType.DMA((48,)),
             pltpu.SemaphoreType.DMA((16,)),
@@ -872,8 +869,6 @@
     stat_ref,
     gain_ref,
     gt_hbm,
-    r1_hbm,
-    r2_hbm,
     gw_out,
     out_hbm,
     ownq_ref,
@@ -903,8 +898,8 @@
     q4,
     ggs,
     rg,
-    na,
-    nb,
+    near,
+    next_x,
     nsum,
     yback,
     send_sems,
@@ -941,6 +936,8 @@
     second = [
         loads.start(a, b)
         for a, b in (
+            (gw_hbm.at[(1 - x) * 2 + c], nsum.at[0]),
+            (gw_hbm.at[x * 2 + c], nsum.at[1]),
             (x_hbm, x_ref),
             (qkv_hbm, qkv_ref),
             (w_hbm.at[:, :, :, :, pl.ds(0, 3 * width)], w_ref.at[:, :, :, :, pl.ds(0, 3 * width)]),
@@ -949,12 +946,14 @@
     ]
     greet(far + [core, xpeer])
 
-    w_copies = [links.push(gw_hbm.at[xx * 2 + 1 - c], r1_hbm.at[xx], core) for xx in range(2)]
-    y_copies = [links.push(yrow_hbm.at[to[0]], yback.at[me_e], to) for to in far]
+    w_copies = [links.push(gw_hbm.at[xx * 2 + 1 - c], near.at[xx], core) for xx in range(2)]
+    y_near, y_far = [], []
+    for k, to in zip(FLIPS, far):
+        (y_far if k >= 4 else y_near).append(links.push(yrow_hbm.at[to[0]], yback.at[me_e], to))
 
     gain_one = gain_ref[0:1, :]
     gain_two = gain_ref[1:2, :]
-    member = (iota((16, width), 1) // HEAD_DIM == iota((16, width), 0)).astype(F32)
+    member = (iota((16, 2 * width), 1) % width // HEAD_DIM == iota((16, 2 * width), 0)).astype(BF16)
     for copy in first:
         copy.wait()
     ggs[...] = jnp.zeros_like(ggs)
@@ -974,13 +973,10 @@
         dhb_scr[rows, :] = dhb
         dc = dot_t(dhb, weight(w_ref, 3 * width, 4 * width)).astype(BF16)
         dc_scr[rows, :] = dc
-        d_scr[:, rows] = lax.dot_general(
-            member,
-            dc.astype(F32) * c_ref[rows, :].astype(F32),
-            (((1,), (1,)), ((), ())),
-            precision=lax.Precision.HIGHEST,
-            preferred_element_type=F32,
-        )
+        product = dc.astype(F32) * c_ref[rows, :].astype(F32)
+        high = product.astype(BF16)
+        rest = (product - high.astype(F32)).astype(BF16)
+        d_scr[:, rows] = dot_t(member, jnp.concatenate((high, rest), axis=1))
 
     def put(ph, value):
         for owner in range(2):
@@ -999,25 +995,17 @@
         rows = pl.ds(pl.multiple_of(i * (width // 4), width // 4), width // 4)
         return pltpu.make_async_remote_copy(
             src_ref=nsum.at[0, rows],
-            dst_ref=r2_hbm.at[rows],
+            dst_ref=next_x.at[rows],
             send_sem=send_sems.at[16 + i],
             recv_sem=recv_sems.at[16 + i],
             device_id=xpeer,
             device_id_type=MESH,
         )
 
-    for step in range(2):
-        xx = 1 - x if step == 0 else x
-        la = loads.start(gw_hbm.at[xx * 2 + c], na)
-        lb = loads.start(r1_hbm.at[xx], nb)
-        la.wait()
-        lb.wait()
-        nsum[step] = (na[...].astype(F32) + nb[...].astype(F32)).astype(BF16)
-        if step == 0:
-            to_x(0).start()
-
     for copy in second:
         copy.wait()
+    nsum[0] = (nsum[0].astype(F32) + near[1 - x].astype(F32)).astype(BF16)
+    to_x(0).start()
 
     @pl.loop(0, blocks)
     def _(i):
@@ -1101,34 +1089,38 @@
     ggs[1] = ggs[0] + rg[0]
     gains_copy = links.push(ggs.at[1], rg.at[1], xpeer)
 
-    def finish(lo, hi):
-        @pl.loop(lo, hi)
+    def finish(side, last):
+        group = slots // 2
+        places = yback.shape[0] // 2
+
+        @pl.loop(0, blocks)
         def _(i):
             rows = pl.ds(pl.multiple_of(i * BLOCK, BLOCK), BLOCK)
-            got = dot(picks(rows), yback[...].reshape(slots, width))
-            ct_ref[rows, :] = (h_ref[rows, :] + jax.nn.sigmoid(col_ref[rows, 1:2]) * got).astype(BF16)
-
-    for copy in y_copies:
-        copy.wait()
-    finish(0, 2)
+            pick = ((iota((BLOCK, group), 1) + side * group).astype(F32) == col_ref[rows, 0:1]).astype(BF16)
+            got = dot(pick, yback[pl.ds(side * places, places)].reshape(group, width))
+            value = h_ref[rows, :] + jax.nn.sigmoid(col_ref[rows, 1:2]) * got
+            if last:
+                ct_ref[rows, :] = value.astype(BF16)
+            else:
+                h_ref[rows, :] = value
+
     reduce(3).step(2)
     reduce(2).step(3)
     reduce(1).step(4)
     gains_copy.wait()
     ggs[2] = ggs[1] + rg[1]
     gains_copy = links.push(ggs.at[2], rg.at[2], ypeer)
-    finish(2, blocks)
-    stores.append(loads.start(ct_ref, out_hbm))
     reduce(3).step(3)
     reduce(2).step(4)
     gains_copy.wait()
     ggs[3] = ggs[2] + rg[2]
     gain_copies = [links.push(ggs.at[3], rg.at[2 + k], device(across(z, k), y, x, c)) for k in (1, 2, 3)]
+    for copy in y_near:
+        copy.wait()
+    finish(z // 2, False)
     for i in range(4):
         to_x(i).wait()
-    lb = loads.start(r2_hbm, nb)
-    lb.wait()
-    gw_out[...] = nsum[1].astype(F32) + nb[...].astype(F32)
+    gw_out[...] = nsum[1].astype(F32) + near[x].astype(F32) + next_x[...].astype(F32)
     reduce(3).step(4)
     for copy in gain_copies:
         copy.wait()
@@ -1152,6 +1144,10 @@
                 for j in range(3):
                     at = pl.multiple_of(j * width + (2 * (ph - 1) + owner) * 128, 128)
                     ownq_ref[:, pl.ds(at, 128)] = part[:, j * 128 : (j + 1) * 128]
+    for copy in y_far:
+        copy.wait()
+    finish(1 - z // 2, True)
+    stores.append(loads.start(ct_ref, out_hbm))
     for copy in stores:
         copy.wait()
 
@@ -1166,8 +1162,6 @@
         tail_kernel,
         out_shape=(
             jax.ShapeDtypeStruct((tokens, width), F32),
-            jax.ShapeDtypeStruct((2,) + gw.shape[1:], BF16),
-            jax.ShapeDtypeStruct(gw.shape[1:], BF16),
             jax.ShapeDtypeStruct(gw.shape[1:], F32),
             jax.ShapeDtypeStruct((tokens, width), BF16),
             jax.ShapeDtypeStruct((24, 3 * width), F32),
@@ -1175,7 +1169,7 @@
             jax.ShapeDtypeStruct((2, 24), F32),
         ),
         in_specs=[any_spec] * 9 + [vmem] * 4,
-        out_specs=(any_spec, any_spec, any_spec, vmem, any_spec, vmem, vmem, vmem),
+        out_specs=(any_spec, vmem, any_spec, vmem, vmem, vmem),
         scratch_shapes=[
             pltpu.VMEM((slots, width), BF16),
             pltpu.VMEM((tokens, width), BF16),
@@ -1201,7 +1195,7 @@
             pltpu.VMEM((4, 24, half), F32),
             pltpu.VMEM((4, 8, width), F32),
             pltpu.VMEM((6, 8, width), F32),
-            pltpu.VMEM(gw.shape[1:], BF16),
+            pltpu.VMEM((2,) + gw.shape[1:], BF16),
             pltpu.VMEM(gw.shape[1:], BF16),
             pltpu.VMEM((2,) + gw.shape[1:], BF16),
             pltpu.VMEM(y_rows.shape, BF16),
@@ -1465,7 +1459,7 @@
             tokens, cotangent, w_in[0], w_hid[0], listed, w_qkv, w_out, norm_gains, n_expert, capacity
         )
         da_back, y_rows, gin_own, ghid = swap(act_slots, dy_rows, w_in_all, w_hid_all, w_in[0], w_hid[0])
-        grad_tokens, _r1, _r2, ghid_own, block_out, own_qkv, own_out, own_gains = tail(
+        grad_tokens, ghid_own, block_out, own_qkv, own_out, own_gains = tail(
             da_back.reshape(slot_rows, width),
             cols,
             listed,

time: 351 us -> 347 us (0.989)
    pallas_call x1, Pallas kernels: 96.3 us -> 92.3 us  [head(): pl.pallas_call(functools.partial(head_kernel, capacity, experts), out_sha...]
where the time goes in v6:
time: 347 us; the launch traced here: 346 us
  Pallas kernels  334 us (96%)
  local copies, waits for them, and re-layouts  9.26 us (3%)
    pallas_call x1, Pallas kernels, swap(): pl.pallas_call(swap_kernel, out_shape=(jax.ShapeDtypeStruct((count, cap,...  135 us
    pallas_call x1, Pallas kernels, tail(): pl.pallas_call(tail_kernel, out_shape=(jax.ShapeDtypeStruct((tokens, widt...  106 us
    pallas_call x1, Pallas kernels, head(): pl.pallas_call(functools.partial(head_kernel, capacity, experts), out_sha...  92.3 us
    unnamed x19, local copies, waits for them, and re-layouts  9.18 us

profile of v6, /device:TPU:0, one launch (start us, length us, event | category | flops | bytes accessed | tf_op | source)
XLA Modules:
  0.0 346.5 jit_solution(14241168870405964194)
XLA Ops:
  0.6 0.1 pad.3.clone
  0.7 0.7 convert_element_type.19
  1.4 0.7 convert_bitcast_fusion
  2.1 1.4 maximum_maximum_fusion.row_ref
  3.5 92.3 %shard_map.153 = (bf16[1024,2304]{1,0:T(8,128)(2,1)}, bf16[1024,768]{1,0:T(8,128)(2,1)}, f32[1024,768]{1,0:T(8,128)}, bf16[8,256,768]{2,1,0:T(8,128)(2,1)}, bf16...) custom-call(bf16[1024,768]{1,0:T(8,128)(2,1)} %x_hbm.3, ...), custom_call_target="tpu_custom_call" | custom-call | flops 64424509440 | bytes 41943040 | tf_op jit(solution)/shard_map/pallas_call | solution.py:703
  95.8 135.0 %shard_map.154 = (bf16[8,256,768]{2,1,0:T(8,128)(2,1)}, bf16[8,256,768]{2,1,0:T(8,128)(2,1)}, f32[768,768]{1,0:T(8,128)}, bf16[4,768,768]{2,1,0:T(8,128)(2,1)}) custom-call(bf16[8,256,768]{2,1,0:T(8,128)(2,1)} %get-tuple-element.28.act_hbm, bf16[8,256,768]{2,1,0:T(8,128)(2,1)} %get-tuple-element.29.dy_hbm, bf16[4,768,768]{2,1,0:T(8,128)(2,1)} %get-tuple-element.30.win_hbm, ...), custom_call_target="tpu_custom_call" | custom-call | flops 107374182400 | bytes 62914560 | tf_op jit(solution)/shard_map/pallas_call | solution.py:1409
  230.8 106.4 %shard_map.155 = (f32[1024,768]{1,0:T(8,128)}, f32[768,768]{1,0:T(8,128)}, bf16[1024,768]{1,0:T(8,128)(2,1)}, f32[24,2304]{1,0:T(8,128)}, f32[24,768]{1,0:T(8,128)}, /*index=5*/f32[2,24]{1,0:T(2,128)}) custom-call(bf16[2048,768]{1,0:T(8,128)(2,1)} %bitcast.15, bf16[1024,768]{1,0:T(8,128)(2,1)} %x_hbm.3, bf16[1024,768]{1,0:T(8,128)(2,1)} %ct_hbm.3, ...), custom_call_target="tpu_custom_call" | custom-call | flops 85899345920 | bytes 41943040 | tf_op jit(solution)/shard_map/pallas_call | solution.py:1161
  337.3 0.0 copy-start
  337.3 2.8 copy.24
  340.1 0.0 copy-done
  340.1 0.0 copy-start.3
  340.1 0.0 copy-start.4
  340.1 0.0 copy-start.5
  340.1 0.0 copy-start.1
  340.1 1.7 copy.25
  341.8 0.0 copy-done.3
  341.8 0.0 copy-start.2
  341.8 0.7 copy.26
  342.5 0.0 copy-done.4
  342.5 0.6 copy.27
  343.1 0.0 copy-done.5
  343.1 0.6 copy.28
  343.7 0.0 copy-done.1
  343.7 1.4 copy.29
  345.1 0.0 copy-done.2
  345.1 1.4 copy.30
  (1 shorter events, 0.0 us)
Async XLA Ops:
  337.3 2.8 copy-start
  340.1 1.7 copy-start.3
  340.1 2.4 copy-start.4
  340.1 3.0 copy-start.5
  340.1 3.6 %copy-start.1 = (f32[768,768]{1,0:T(8,128)S(1)}, f32[768,768]{1,0:T(8,128)}, u32[]{:S(2)}) copy-start(f32[768,768]{1,0:T(8,128)} %get-tuple-element.47) | copy-start | bytes 7077892
  341.8 3.3 copy-start.2

commit v7 on v6

--- a/solution.py
+++ b/solution.py
@@ -571,11 +571,16 @@
     scol = jnp.sum(hot_c * (rank_c + base_c), axis=1, keepdims=True)
     col_ref[...] = jnp.where(iota(listed.shape, 1) == 0, scol, listed)
 
-    def fill(values, out):
+    def storing_act(i):
+        return pltpu.make_async_copy(act_ref.at[i], act_hbm.at[i], load_sems.at[16 + i])
+
+    def fill(values, out, then=None):
         @pl.loop(0, out.shape[0])
         def _(i):
             ids = (iota((capacity, tokens), 0) + i * capacity).astype(F32)
             out[i] = dot((ids == srow).astype(BF16), values).astype(BF16)
+            if then is not None:
+                then(i).start()
 
     loading_ct.wait()
     fill((jax.nn.sigmoid(listed[:, 1:2]) * ct_ref[...].astype(F32)).astype(BF16), dy_ref)
@@ -685,8 +690,8 @@
         a_scr[rows, :] = (normed * gain_two).astype(BF16)
 
     storing.append(loads.start(h_ref, h_hbm))
-    fill(a_scr[...], act_ref)
-    storing.append(loads.start(act_ref, act_hbm))
+    fill(a_scr[...], act_ref, storing_act)
+    storing += [storing_act(i) for i in range(experts)]
     for i in range(1, 4):
         pass_on(i)
     for copy in storing + [own_dy] + core_slices + dy_copies:
@@ -734,7 +739,7 @@
             pltpu.VMEM((tokens // BLOCK * (LOOKBACK + 1), BLOCK, BLOCK), F32),
             pltpu.SemaphoreType.DMA((48,)),
             pltpu.SemaphoreType.DMA((48,)),
-            pltpu.SemaphoreType.DMA((16,)),
+            pltpu.SemaphoreType.DMA((16 + experts,)),
         ],
         compiler_params=pltpu.CompilerParams(vmem_limit_bytes=62 << 20, collective_id=0, has_side_effects=True),
         cost_estimate=pl.CostEstimate(flops=60 << 30, bytes_accessed=40 << 20, transcendentals=0),
@@ -902,6 +907,7 @@
     next_x,
     nsum,
     yback,
+    gw_scr,
     send_sems,
     recv_sems,
     red_send,
@@ -1120,7 +1126,8 @@
     finish(z // 2, False)
     for i in range(4):
         to_x(i).wait()
-    gw_out[...] = nsum[1].astype(F32) + near[x].astype(F32) + next_x[...].astype(F32)
+    gw_scr[...] = nsum[1].astype(F32) + near[x].astype(F32) + next_x[...].astype(F32)
+    stores.append(loads.start(gw_scr, gw_out))
     reduce(3).step(4)
     for copy in gain_copies:
         copy.wait()
@@ -1169,7 +1176,7 @@
             jax.ShapeDtypeStruct((2, 24), F32),
         ),
         in_specs=[any_spec] * 9 + [vmem] * 4,
-        out_specs=(any_spec, vmem, any_spec, vmem, vmem, vmem),
+        out_specs=(any_spec, any_spec, any_spec, vmem, vmem, vmem),
         scratch_shapes=[
             pltpu.VMEM((slots, width), BF16),
             pltpu.VMEM((tokens, width), BF16),
@@ -1199,6 +1206,7 @@
             pltpu.VMEM(gw.shape[1:], BF16),
             pltpu.VMEM((2,) + gw.shape[1:], BF16),
             pltpu.VMEM(y_rows.shape, BF16),
+            pltpu.VMEM(gw.shape[1:], F32),
             pltpu.SemaphoreType.DMA((20,)),
             pltpu.SemaphoreType.DMA((20,)),
             pltpu.SemaphoreType.DMA((28,)),

time: 347 us -> 347 us (level)
  no operation moved by 1% of the time
where the time goes in v7:
time: 347 us
  Pallas kernels  334 us (96%)
  local copies, waits for them, and re-layouts  9.26 us (3%)
    pallas_call x1, Pallas kernels, swap(): pl.pallas_call(swap_kernel, out_shape=(jax.ShapeDtypeStruct((count, cap,...  135 us
    pallas_call x1, Pallas kernels, tail(): pl.pallas_call(tail_kernel, out_shape=(jax.ShapeDtypeStruct((tokens, widt...  107 us
    pallas_call x1, Pallas kernels, head(): pl.pallas_call(functools.partial(head_kernel, capacity, experts), out_sha...  92.6 us
    unnamed x19, local copies, waits for them, and re-layouts  9.18 us

profile of v7, /device:TPU:0, one launch (start us, length us, event | category | flops | bytes accessed | tf_op | source)
XLA Modules:
  0.0 346.9 jit_solution(516262280456767829)
XLA Ops:
  0.6 0.1 pad.3.clone
  0.7 0.7 convert_element_type.19
  1.4 0.7 convert_bitcast_fusion
  2.1 1.4 maximum_maximum_fusion.row_ref
  3.5 92.6 %shard_map.153 = (bf16[1024,2304]{1,0:T(8,128)(2,1)}, bf16[1024,768]{1,0:T(8,128)(2,1)}, f32[1024,768]{1,0:T(8,128)}, bf16[8,256,768]{2,1,0:T(8,128)(2,1)}, bf16...) custom-call(bf16[1024,768]{1,0:T(8,128)(2,1)} %x_hbm.3, ...), custom_call_target="tpu_custom_call" | custom-call | flops 64424509440 | bytes 41943040 | tf_op jit(solution)/shard_map/pallas_call | solution.py:708
  96.1 134.8 %shard_map.154 = (bf16[8,256,768]{2,1,0:T(8,128)(2,1)}, bf16[8,256,768]{2,1,0:T(8,128)(2,1)}, f32[768,768]{1,0:T(8,128)}, bf16[4,768,768]{2,1,0:T(8,128)(2,1)}) custom-call(bf16[8,256,768]{2,1,0:T(8,128)(2,1)} %get-tuple-element.28.act_hbm, bf16[8,256,768]{2,1,0:T(8,128)(2,1)} %get-tuple-element.29.dy_hbm, bf16[4,768,768]{2,1,0:T(8,128)(2,1)} %get-tuple-element.30.win_hbm, ...), custom_call_target="tpu_custom_call" | custom-call | flops 107374182400 | bytes 62914560 | tf_op jit(solution)/shard_map/pallas_call | solution.py:1417
  230.9 106.8 %shard_map.155 = (f32[1024,768]{1,0:T(8,128)}, f32[768,768]{1,0:T(8,128)}, bf16[1024,768]{1,0:T(8,128)(2,1)}, f32[24,2304]{1,0:T(8,128)}, f32[24,768]{1,0:T(8,128)}, /*index=5*/f32[2,24]{1,0:T(2,128)}) custom-call(bf16[2048,768]{1,0:T(8,128)(2,1)} %bitcast.15, bf16[1024,768]{1,0:T(8,128)(2,1)} %x_hbm.3, bf16[1024,768]{1,0:T(8,128)(2,1)} %ct_hbm.3, ...), custom_call_target="tpu_custom_call" | custom-call | flops 85899345920 | bytes 41943040 | tf_op jit(solution)/shard_map/pallas_call | solution.py:1168
  337.7 0.0 copy-start
  337.7 2.8 copy.24
  340.5 0.0 copy-done
  340.5 0.0 copy-start.3
  340.5 0.0 copy-start.4
  340.5 0.0 copy-start.5
  340.5 0.0 copy-start.1
  340.5 1.7 copy.25
  342.2 0.0 copy-done.3
  342.2 0.0 copy-start.2
  342.2 0.7 copy.26
  342.9 0.0 copy-done.4
  342.9 0.6 copy.27
  343.5 0.0 copy-done.5
  343.5 0.6 copy.28
  344.1 0.0 copy-done.1
  344.1 1.4 copy.29
  345.5 0.0 copy-done.2
  345.5 1.4 copy.30
  (1 shorter events, 0.0 us)
Async XLA Ops:
  337.7 2.8 copy-start
  340.5 1.7 copy-start.3
  340.5 2.4 copy-start.4
  340.5 3.0 copy-start.5
  340.5 3.6 %copy-start.1 = (f32[768,768]{1,0:T(8,128)S(1)}, f32[768,768]{1,0:T(8,128)}, u32[]{:S(2)}) copy-start(f32[768,768]{1,0:T(8,128)} %get-tuple-element.47) | copy-start | bytes 7077892
  342.2 3.3 copy-start.2

commit v8 on v6

--- a/solution.py
+++ b/solution.py
@@ -1297,7 +1297,9 @@
         copy.wait()
 
     @pl.loop(0, count)
-    def _(k):
+    def _(turn):
+        k = lax.rem(turn, 2) * 4 + lax.rem(turn // 2, 2) * 2 + turn // 4
+
         @pl.when(k > 0)
         def _():
             outward(k).wait_recv()

time: 347 us -> 363 us (1.046)
  Pallas kernels: 334 us -> 350 us
    pallas_call x1, Pallas kernels: 135 us -> 143 us  [swap(): pl.pallas_call(swap_kernel, out_shape=(jax.ShapeDtypeStruct((count, cap,...]
    pallas_call x1, Pallas kernels: 106 us -> 114 us  [tail(): pl.pallas_call(tail_kernel, out_shape=(jax.ShapeDtypeStruct((tokens, widt...]
where the time goes in v8:
time: 363 us
  Pallas kernels  350 us (96%)
  local copies, waits for them, and re-layouts  9.26 us (3%)
    pallas_call x1, Pallas kernels, swap(): pl.pallas_call(swap_kernel, out_shape=(jax.ShapeDtypeStruct((count, cap,...  143 us
    pallas_call x1, Pallas kernels, tail(): pl.pallas_call(tail_kernel, out_shape=(jax.ShapeDtypeStruct((tokens, widt...  114 us
    pallas_call x1, Pallas kernels, head(): pl.pallas_call(functools.partial(head_kernel, capacity, experts), out_sha...  92.3 us
    unnamed x19, local copies, waits for them, and re-layouts  9.18 us

profile of v8, /device:TPU:0, one launch (start us, length us, event | category | flops | bytes accessed | tf_op | source)
XLA Modules:
  0.0 362.6 jit_solution(3007565863507266402)
XLA Ops:
  0.6 0.1 pad.3.clone
  0.7 0.7 convert_element_type.19
  1.4 0.7 convert_bitcast_fusion
  2.1 1.4 maximum_maximum_fusion.row_ref
  3.5 92.3 %shard_map.153 = (bf16[1024,2304]{1,0:T(8,128)(2,1)}, bf16[1024,768]{1,0:T(8,128)(2,1)}, f32[1024,768]{1,0:T(8,128)}, bf16[8,256,768]{2,1,0:T(8,128)(2,1)}, bf16...) custom-call(bf16[1024,768]{1,0:T(8,128)(2,1)} %x_hbm.3, ...), custom_call_target="tpu_custom_call" | custom-call | flops 64424509440 | bytes 41943040 | tf_op jit(solution)/shard_map/pallas_call | solution.py:703
  95.8 143.4 %shard_map.154 = (bf16[8,256,768]{2,1,0:T(8,128)(2,1)}, bf16[8,256,768]{2,1,0:T(8,128)(2,1)}, f32[768,768]{1,0:T(8,128)}, bf16[4,768,768]{2,1,0:T(8,128)(2,1)}) custom-call(bf16[8,256,768]{2,1,0:T(8,128)(2,1)} %get-tuple-element.28.act_hbm, bf16[8,256,768]{2,1,0:T(8,128)(2,1)} %get-tuple-element.29.dy_hbm, bf16[4,768,768]{2,1,0:T(8,128)(2,1)} %get-tuple-element.30.win_hbm, ...), custom_call_target="tpu_custom_call" | custom-call | flops 107374182400 | bytes 62914560 | tf_op jit(solution)/shard_map/pallas_call | solution.py:1411
  239.2 114.2 %shard_map.155 = (f32[1024,768]{1,0:T(8,128)}, f32[768,768]{1,0:T(8,128)}, bf16[1024,768]{1,0:T(8,128)(2,1)}, f32[24,2304]{1,0:T(8,128)}, f32[24,768]{1,0:T(8,128)}, /*index=5*/f32[2,24]{1,0:T(2,128)}) custom-call(bf16[2048,768]{1,0:T(8,128)(2,1)} %bitcast.15, bf16[1024,768]{1,0:T(8,128)(2,1)} %x_hbm.3, bf16[1024,768]{1,0:T(8,128)(2,1)} %ct_hbm.3, ...), custom_call_target="tpu_custom_call" | custom-call | flops 85899345920 | bytes 41943040 | tf_op jit(solution)/shard_map/pallas_call | solution.py:1161
  353.4 0.0 copy-start
  353.4 2.8 copy.24
  356.2 0.0 copy-done
  356.2 0.0 copy-start.3
  356.2 0.0 copy-start.4
  356.2 0.0 copy-start.5
  356.3 0.0 copy-start.1
  356.3 1.7 copy.25
  357.9 0.0 copy-done.3
  357.9 0.0 copy-start.2
  357.9 0.7 copy.26
  358.6 0.0 copy-done.4
  358.6 0.6 copy.27
  359.3 0.0 copy-done.5
  359.3 0.6 copy.28
  359.8 0.0 copy-done.1
  359.8 1.4 copy.29
  361.2 0.0 copy-done.2
  361.2 1.4 copy.30
  (1 shorter events, 0.0 us)
Async XLA Ops:
  353.4 2.8 copy-start
  356.2 1.7 copy-start.3
  356.2 2.4 copy-start.4
  356.2 3.0 copy-start.5
  356.3 3.6 copy-start.1
  357.9 3.3 copy-start.2
